TPU v7x, 32 devices: a whole 2x2x4 slice. The times are simulated.
32 devices in a mesh: groups: 2 (over x), chan: 16 (over z, y, core).
Axes of the slice: x: 2, y: 2, z: 4, core: 2. Of those that a mesh axis runs over, the one named last changes fastest.
Arguments:
- data: bfloat16 [28672, 4096], P(('groups', 'chan')), parts along dimension 0, as said below
- alive: int32 [8192], P(('groups', 'chan')), parts along dimension 0, may hold values 0 or 1
- sources: int32 [2, 16], replicated, may hold values from 0 to 4095, as said below
Outputs:
- correlations: bfloat16 [4, 16, 256, 4096], P('groups', None, None, 'chan'), parts along dimension 0
There are 2 independent parts, one for each index of `groups`. A program takes and returns all parts, laid end to end along the dimension named above; an argument that names none is the same for every part. Nothing has to cross between parts.
Inputs may be any that keep to these rules, and one draw needn't show every extreme that they name: `sources`: no channel number appears twice in the array, and channel 4096 - 1 is always one of them. `data`: samples have channel and time-block scales of their own.
All inputs are finite; a program needn't handle non-finite values. No bound on the sum of `alive` on one device may be relied on, other than what follows from the above.
Results may differ from a plain program's by a relative error of at most 0.0076.
Values may be sent and summed in bfloat16 or wider, within the bound.
No kernel may reach another device: no remote copies, remote signals or barrier semaphores. Data moves between devices by JAX's collectives and lax.ppermute only.
A program may use at most 128 MiB of HBM per device.

v0:
```python
import math

import jax
import jax.numpy as jnp
from jax import lax
from jax.sharding import PartitionSpec as P

SEGMENT_LENGTH = 512
NF = 128
LAGS = 256
SRC = 16
ROUNDS = 2
SEGMENT_TALLY = 28


def forward_table():
    times = jnp.arange(SEGMENT_LENGTH, dtype=jnp.int32)[:, None]
    bins = jnp.arange(NF, dtype=jnp.int32)[None, :] + 1
    angle = 2.0 * math.pi / SEGMENT_LENGTH * (bins * times % SEGMENT_LENGTH).astype(jnp.float32)
    table = jnp.concatenate([jnp.cos(angle), -jnp.sin(angle)], axis=1) / math.sqrt(SEGMENT_LENGTH)
    return table.astype(jnp.bfloat16)


def inverse_table():
    shifts = jnp.arange(LAGS, dtype=jnp.int32)[:, None] - LAGS // 2
    bins = jnp.arange(NF, dtype=jnp.int32)[None, :] + 1
    angle = 2.0 * math.pi / SEGMENT_LENGTH * (bins * shifts % SEGMENT_LENGTH).astype(jnp.float32)
    return jnp.concatenate([jnp.cos(angle), -jnp.sin(angle)], axis=1).astype(jnp.bfloat16)


def body(data, alive, sources):
    count = lax.axis_size("chan")
    width = data.shape[1] // count
    table = forward_table()
    split = data.reshape(data.shape[0], count, width)
    moved = lax.all_to_all(split, "chan", split_axis=1, concat_axis=0, tiled=True)
    blocks = moved.reshape(SEGMENT_TALLY, SEGMENT_LENGTH, moved.shape[2])
    spectra = jnp.einsum("tk,wtc->wkc", table, blocks, preferred_element_type=jnp.float32)
    level = jnp.mean(spectra[:, :NF] ** 2 + spectra[:, NF:] ** 2, axis=0)
    factor = alive.astype(jnp.float32)[None, :] / jnp.sqrt(level + 0.01)
    factor = jnp.concatenate([factor, factor], axis=0)
    whitened = (spectra * factor[None]).astype(jnp.bfloat16)
    ids = sources.reshape(-1)
    owner = ids // width
    local = ids % width
    mine = owner == lax.axis_index("chan")
    picked = jnp.transpose(jnp.take(whitened, local, axis=2), (2, 0, 1)).astype(jnp.float32)
    picked = jnp.where(mine[:, None, None], picked, 0.0)
    src = lax.psum(picked, "chan").astype(jnp.bfloat16)
    src_re, src_im = (src[:, :, :NF], src[:, :, NF:])
    own_re, own_im = (whitened[:, :NF], whitened[:, NF:])
    form = "qwf,wfc->qfc"
    correlogram_realpart = jnp.einsum(
        form, src_re, own_re, preferred_element_type=jnp.float32
    ) + jnp.einsum(form, src_im, own_im, preferred_element_type=jnp.float32)
    cross_imaginary = jnp.einsum(
        form, src_re, own_im, preferred_element_type=jnp.float32
    ) - jnp.einsum(form, src_im, own_re, preferred_element_type=jnp.float32)
    cross = jnp.concatenate([correlogram_realpart, cross_imaginary], axis=1).astype(jnp.bfloat16)
    lagged = jnp.einsum("lk,qkc->qlc", inverse_table(), cross, preferred_element_type=jnp.float32)
    lagged = lagged / math.sqrt(NF * SEGMENT_TALLY)
    return lagged.reshape(ROUNDS, SRC, LAGS, width).astype(jnp.bfloat16)


def solution(mesh):
    return jax.shard_map(
        body,
        mesh=mesh,
        in_specs=(P(("groups", "chan"), None), P(("groups", "chan")), P()),
        out_specs=P("groups", None, None, "chan"),
        check_vma=False,
    )
```

profile of v0, /device:TPU:0, one launch (start us, length us, event | category | flops | bytes accessed | tf_op | source)
XLA Modules:
  0.0 326.9 jit_solution(7985542122648060904)
XLA Ops:
  0.0 6.9 %copy.27 = bf16[112,16,8,256]{3,2,0,1:T(8,128)(2,1)} copy(bf16[112,16,8,256]{3,2,1,0:T(8,128)(2,1)} %bitcast.32) | data formatting | bytes 14680064 | tf_op jit(solution)/shard_map/reshape | solution.py:35
  6.9 7.6 %all-to-all-start = ((bf16[896,16,256]{2,0,1:T(8,128)(2,1)}), bf16[896,16,256]{2,0,1:T(8,128)(2,1)}, u32[]{:S(2)}, u32[]{:S(2)}) async-start(bf16[896,16,256]{2,0,1:T(8,128)(2,1)} %bitcast.31), calls=%async_computation | async-start | bytes 14680064 | tf_op jit(solution)/shard_map/all_to_all | solution.py:36
  14.4 0.1 reshape.125
  14.5 0.1 reshape.124
  14.7 0.6 cosine_convert_fusion
  15.3 1.1 fusion.33
  16.4 130.5 %all-to-all-done = bf16[896,16,256]{2,0,1:T(8,128)(2,1)} async-done(((bf16[896,16,256]{2,0,1:T(8,128)(2,1)}), bf16[896,16,256]{2,0,1:T(8,128)(2,1)}, u32[]{:S(2)}, u32[]{:S(2)}) %all-to-all-start) | async-done | bytes 7340064 | tf_op jit(solution)/shard_map/all_to_all | solution.py:36
  146.9 5.2 %convolution_bitcast_fusion = f32[28,256,256]{2,1,0:T(8,128)S(1)} fusion(bf16[28,512,256]{2,1,0:T(8,128)(2,1)} %bitcast.3, f32[512,128]{0,1:T(8,128)S(1)} %get-tuple-element.14, f32[512,128]{0,1:T(8,128)S(1)} %get-tuple-element.13), kind=kOutput, calls=%fused_computation.14 | convolution fusion | flops 1879441408 | bytes 15204352 | tf_op jit(solution)/shard_map/tk,wtc->wkc/dot_general | solution.py:38
  152.0 0.5 fusion.5
  152.6 2.6 multiply_convert_fusion.1
  155.2 7.7 %copy.7 = bf16[28,256,256]{1,0,2:T(8,128)(2,1)} copy(bf16[28,256,256]{2,1,0:T(8,128)(2,1)} %multiply_convert_fusion.1) | data formatting | bytes 7340032 | tf_op jit(solution)/shard_map/convert_element_type | solution.py:42
  162.9 3.6 %fusion.40 = (bf16[28,128,256]{2,1,0:T(8,128)(2,1)S(1)}, bf16[28,128,256]{2,1,0:T(8,128)(2,1)}) fusion(bf16[28,256,256]{2,1,0:T(8,128)(2,1)} %multiply_convert_fusion.1), kind=kLoop, calls=%fused_computation.76 | loop fusion | bytes 7340032 | tf_op jit(solution)/shard_map/slice | solution.py:51
  166.6 2.8 gather_fusion
  169.3 0.2 convert_select_fusion
  169.6 100.6 %all-reduce.1 = bf16[32,28,256]{2,1,0:T(8,128)(2,1)S(1)} all-reduce(f32[32,28,256]{2,1,0:T(8,128)S(1)} %convert_select_fusion), channel_id=1, replica_groups=mesh['groups'=2,'chan'=16] {'chan'}, use_global_device_ids=true, to_apply=%region_1.2 | all-reduce | flops 229376 | bytes 1376256 | tf_op jit(solution)/shard_map/psum | solution.py:49
  270.2 0.1 fusion.41
  270.3 2.6 copy.13
  272.8 1.6 copy.10
  274.5 0.0 copy-start
  274.5 0.0 copy-start.1
  274.5 4.6 %fusion.14 = f32[128,256,32]{1,2,0:T(8,128)} fusion(bf16[32,28,128]{0,1,2:T(8,128)(2,1)} %copy.13, bf16[28,128,256]{2,1,0:T(8,128)(2,1)S(1)} %get-tuple-element.5), kind=kOutput, calls=%fused_computation.21 | convolution fusion | flops 58720256 | bytes 6258688 | tf_op jit(solution)/shard_map/qwf,wfc->qfc/dot_general | solution.py:58
  279.1 0.0 copy-done.1
  279.1 3.2 fusion.12
  282.4 3.3 fusion.10
  285.6 3.3 %fusion.16 = f32[128,256,32]{1,2,0:T(8,128)} fusion(bf16[32,28,128]{0,1,2:T(8,128)(2,1)S(1)} %copy.10, bf16[28,128,256]{2,1,0:T(8,128)(2,1)S(1)} %get-tuple-element.5), kind=kOutput, calls=%fused_computation.23 | convolution fusion | flops 58720256 | bytes 6258688 | tf_op jit(solution)/shard_map/qwf,wfc->qfc/dot_general | solution.py:53
  288.9 5.3 %copy.16 = f32[128,256,32]{0,1,2:T(8,128)} copy(f32[128,256,32]{1,2,0:T(8,128)} %fusion.14) | data formatting | bytes 8388608 | tf_op jit(solution)/shard_map/qwf,wfc->qfc/dot_general | solution.py:58
  294.2 5.3 %copy.15 = f32[128,256,32]{0,1,2:T(8,128)} copy(f32[128,256,32]{1,2,0:T(8,128)} %fusion.10) | data formatting | bytes 8388608 | tf_op jit(solution)/shard_map/qwf,wfc->qfc/dot_general | solution.py:56
  299.6 5.3 %copy.14 = f32[128,256,32]{0,1,2:T(8,128)} copy(f32[128,256,32]{1,2,0:T(8,128)} %fusion.12) | data formatting | bytes 8388608 | tf_op jit(solution)/shard_map/qwf,wfc->qfc/dot_general | solution.py:55
  304.9 5.3 %copy.11 = f32[128,256,32]{0,1,2:T(8,128)} copy(f32[128,256,32]{1,2,0:T(8,128)} %fusion.16) | data formatting | bytes 8388608 | tf_op jit(solution)/shard_map/qwf,wfc->qfc/dot_general | solution.py:53
  310.2 7.6 %fusion.8 = (bf16[32,128,256]{1,2,0:T(8,128)(2,1)S(1)}, bf16[32,128,256]{1,2,0:T(8,128)(2,1)S(1)}) fusion(f32[128,256,32]{0,1,2:T(8,128)} %copy.11, f32[128,256,32]{0,1,2:T(8,128)} %copy.14, f32[128,256,32]{0,1,2:T(8,128)} %copy.15, f32[128,256,32]{0,1,2:T(8,128)} %copy.16), kind=kLoop, calls=%fused_computation.15 | loop fusion | flops 4194304 | bytes 20971520 | tf_op jit(solution)/shard_map/add | solution.py:53
  317.8 2.9 multiply_convert_fusion
  320.7 6.2 %copy.8 = bf16[2,16,256,256]{3,2,1,0:T(8,128)(2,1)} copy(bf16[2,16,256,256]{2,3,1,0:T(8,128)(2,1)} %bitcast.33) | data formatting | bytes 8388608 | tf_op jit(solution)/shard_map/convert_element_type | solution.py:62
  (13 shorter events, 0.1 us)
Async XLA Ops:
  6.9 7.6 %copy-start.3 = (s32[2,16]{1,0:T(2,128)S(1)}, s32[2,16]{1,0:T(2,128)}, u32[]{:S(2)}) copy-start(s32[2,16]{1,0:T(2,128)} %param.5) | copy-start | bytes 388
  6.9 7.8 %copy-start.2 = (s32[256]{0:T(256)S(1)}, s32[256]{0:T(256)}, u32[]{:S(2)}) copy-start(s32[256]{0:T(256)} %param.4) | copy-start | bytes 3076
  6.9 140.0 %all-to-all-start = ((bf16[896,16,256]{2,0,1:T(8,128)(2,1)}), bf16[896,16,256]{2,0,1:T(8,128)(2,1)}, u32[]{:S(2)}, u32[]{:S(2)}) async-start(bf16[896,16,256]{2,0,1:T(8,128)(2,1)} %bitcast.31), calls=%async_computation | async-start | bytes 14680064 | tf_op jit(solution)/shard_map/all_to_all | solution.py:36
  274.5 4.7 %copy-start = (bf16[28,128,256]{2,1,0:T(8,128)(2,1)S(1)}, bf16[28,128,256]{2,1,0:T(8,128)(2,1)}, u32[]{:S(2)}) copy-start(bf16[28,128,256]{2,1,0:T(8,128)(2,1)} %get-tuple-element.6) | copy-start | bytes 5505028
  274.5 4.7 %copy-start.1 = (bf16[32,28,128]{0,1,2:T(8,128)(2,1)S(1)}, bf16[32,28,128]{0,1,2:T(8,128)(2,1)}, u32[]{:S(2)}) copy-start(bf16[32,28,128]{0,1,2:T(8,128)(2,1)} %copy.13) | copy-start | bytes 688132
where the time goes:
time: 328 us; the launch traced here: 327 us
  waiting for transfers between devices  130 us (40%)
  blocking collectives  101 us (31%)
  local copies, waits for them, and re-layouts  52.9 us (16%)
  matrix products  22.5 us (7%)
  other arithmetic  12.8 us (4%)
  starting transfers between devices  7.56 us (2%)
    all_to_all x1, waiting for transfers between devices, body(): lax.all_to_all(split, 'chan', split_axis=1, concat_axis=0, tiled=True)  130 us
    psum x1, blocking collectives, body(): src = lax.psum(picked, 'chan').astype(jnp.bfloat16)  101 us
    convert_element_type x1, local copies, waits for them, and re-layouts, body(): whitened = (spectra * factor[None]).astype(jnp.bfloat16)  7.7 us
    add x1, other arithmetic, body(): jnp.einsum(form, src_re, own_re, preferred_element_type=jnp.float32)  7.63 us
    all_to_all x1, starting transfers between devices, body(): lax.all_to_all(split, 'chan', split_axis=1, concat_axis=0, tiled=True)  7.56 us
    reshape x1, local copies, waits for them, and re-layouts, body(): split = data.reshape(data.shape[0], count, width)  6.85 us
  transfers between devices with their start and end apart: 1, of which 1 were waited for; matrix products, arithmetic and copies ran while one was open for 1% of the time, Pallas kernels for 0%

commit v1 on v0

v1 whole, which is shorter than its diff:
```python
import math

import jax
import jax.numpy as jnp
from jax import lax
from jax.experimental import pallas as pl
from jax.experimental.pallas import tpu as pltpu
from jax.sharding import PartitionSpec as P

SEGMENT_LENGTH = 512
NF = 128
LAGS = 256
SRC = 16
ROUNDS = 2
SEGMENT_TALLY = 28

SOURCES = SRC * ROUNDS
BINS = 2 * NF
SUB = 8
TILES = NF // SUB
TEAM = 4
TEAM_WINDOWS = 7
STEP = 128
HELD = TEAM_WINDOWS * SEGMENT_LENGTH // TEAM
STRADDLE = HELD - SEGMENT_LENGTH
WHOLE = 16
SPLIT = 12
PACKED = 1024


def tile_order(table):
    table = table.reshape(2, TILES, SUB, table.shape[1])
    return jnp.transpose(table, (1, 0, 2, 3)).reshape(BINS, table.shape[3])


def forward_table():
    times = jnp.arange(SEGMENT_LENGTH, dtype=jnp.int32)[None, :]
    bins = jnp.arange(NF, dtype=jnp.int32)[:, None] + 1
    angle = 2.0 * math.pi / SEGMENT_LENGTH * (bins * times % SEGMENT_LENGTH).astype(jnp.float32)
    table = jnp.concatenate([jnp.cos(angle), -jnp.sin(angle)], axis=0) / math.sqrt(SEGMENT_LENGTH)
    return tile_order(table).astype(jnp.bfloat16)


def inverse_table():
    shifts = jnp.arange(LAGS, dtype=jnp.int32)[None, :] - LAGS // 2
    bins = jnp.arange(NF, dtype=jnp.int32)[:, None] + 1
    angle = 2.0 * math.pi / SEGMENT_LENGTH * (bins * shifts % SEGMENT_LENGTH).astype(jnp.float32)
    table = jnp.concatenate([jnp.cos(angle), -jnp.sin(angle)], axis=0)
    return tile_order(table).T.astype(jnp.bfloat16)


def prepare_kernel(place_ref, data_ref, table_ref, ids_ref, flags_ref, whole_ref, rows_ref, picked_ref, acc_ref):
    step = pl.program_id(0)
    place = place_ref[0]
    columns = data_ref.shape[1]
    width = columns // TEAM
    start = pl.multiple_of(place * STEP, STEP)
    block = data_ref[pl.ds(start, SEGMENT_LENGTH), :]
    spectra = jnp.dot(table_ref[...], block, preferred_element_type=jnp.float32).astype(jnp.bfloat16)
    for k in range(TEAM):
        whole_ref[k] = spectra[:, k * width : (k + 1) * width]
    for j in range(STRADDLE // STEP):
        source = pl.multiple_of(jnp.where(j < place, j, j + SEGMENT_LENGTH // STEP) * STEP, STEP)
        piece = data_ref[pl.ds(source, STEP), :]
        for k in range(TEAM):
            rows_ref[k, 0, j * STEP : (j + 1) * STEP, :] = piece[:, k * width : (k + 1) * width]
    channel = lax.broadcasted_iota(jnp.int32, (columns, 128), 0) + step * columns
    chosen = jnp.where(channel == ids_ref[...], 1.0, 0.0).astype(jnp.bfloat16)
    part = jnp.dot(data_ref[...], chosen, preferred_element_type=jnp.float32)

    @pl.when(step == 0)
    def _():
        acc_ref[...] = part

    @pl.when(step > 0)
    def _():
        acc_ref[...] += part

    @pl.when(step == pl.num_programs(0) - 1)
    def _():
        picked_ref[:, :HELD] = acc_ref[...].T[:SOURCES, :].astype(jnp.bfloat16)
        picked_ref[:, HELD:] = flags_ref[...]


def prepare(place, data, table, ids, flags, count):
    columns = data.shape[1] // count * TEAM
    steps = count // TEAM
    width = columns // TEAM
    return pl.pallas_call(
        prepare_kernel,
        grid_spec=pltpu.PrefetchScalarGridSpec(
            num_scalar_prefetch=1,
            grid=(steps,),
            in_specs=[
                pl.BlockSpec((HELD, columns), lambda i, p: (0, i)),
                pl.BlockSpec((BINS, SEGMENT_LENGTH), lambda i, p: (0, 0)),
                pl.BlockSpec((1, 128), lambda i, p: (0, 0)),
                pl.BlockSpec((SOURCES, PACKED - HELD), lambda i, p: (0, 0)),
            ],
            out_specs=[
                pl.BlockSpec((TEAM, BINS, width), lambda i, p: (i, 0, 0)),
                pl.BlockSpec((TEAM, 1, STRADDLE, width), lambda i, p: (0, i, 0, 0)),
                pl.BlockSpec((SOURCES, PACKED), lambda i, p: (0, 0)),
            ],
            scratch_shapes=[pltpu.VMEM((HELD, 128), jnp.float32)],
        ),
        out_shape=[
            jax.ShapeDtypeStruct((count, BINS, width), jnp.bfloat16),
            jax.ShapeDtypeStruct((TEAM, steps, STRADDLE, width), jnp.bfloat16),
            jax.ShapeDtypeStruct((SOURCES, PACKED), jnp.bfloat16),
        ],
        compiler_params=pltpu.CompilerParams(vmem_limit_bytes=24 << 20),
    )(place, data, table, ids, flags)


def straddle_kernel(rows_ref, table_ref, out_ref):
    width = rows_ref.shape[3]
    rows = rows_ref[...].reshape(TEAM * STRADDLE, width)
    for k in range(TEAM * STRADDLE // SEGMENT_LENGTH):
        block = rows[k * SEGMENT_LENGTH : (k + 1) * SEGMENT_LENGTH]
        spectra = jnp.dot(table_ref[...], block, preferred_element_type=jnp.float32)
        out_ref[0, k * BINS : (k + 1) * BINS, :] = spectra.astype(jnp.bfloat16)


def straddle(rows, table):
    _, steps, _, width = rows.shape
    depth = TEAM * STRADDLE // SEGMENT_LENGTH * BINS
    return pl.pallas_call(
        straddle_kernel,
        grid=(steps,),
        in_specs=[
            pl.BlockSpec((TEAM, 1, STRADDLE, width), lambda i: (0, i, 0, 0)),
            pl.BlockSpec((BINS, SEGMENT_LENGTH), lambda i: (0, 0)),
        ],
        out_specs=pl.BlockSpec((1, depth, width), lambda i: (i, 0, 0)),
        out_shape=jax.ShapeDtypeStruct((steps, depth, width), jnp.bfloat16),
        compiler_params=pltpu.CompilerParams(vmem_limit_bytes=16 << 20),
    )(rows, table)


PHASES = 4
BATCH = TILES // PHASES
QUERIES = SOURCES // PHASES


def correlate_kernel(left_ref, whole_ref, split_ref, alive_ref, inverse_ref, out_ref, cross_ref):
    step = pl.program_id(0)
    width = whole_ref.shape[2]
    rows = 2 * SUB
    cut = WHOLE * rows

    @pl.when(step < PHASES)
    def _():
        alive = alive_ref[...]
        for k in range(BATCH):
            whole = whole_ref[:, k * rows : (k + 1) * rows, :]
            split = split_ref[:, k * rows : (k + 1) * rows, :]
            power = jnp.sum(jnp.square(whole.astype(jnp.float32)), axis=0)
            power += jnp.sum(jnp.square(split.astype(jnp.float32)), axis=0)
            level = (power[:SUB] + power[SUB:]) / SEGMENT_TALLY
            factor = alive / jnp.sqrt(level + 0.01)
            factor = jnp.concatenate([factor, factor], axis=0)[None]
            cross = jnp.dot(
                left_ref[k, :, :cut], whole.reshape(WHOLE * rows, width), preferred_element_type=jnp.float32
            )
            cross += jnp.dot(
                left_ref[k, :, cut:], split.reshape(SPLIT * rows, width), preferred_element_type=jnp.float32
            )
            cross = cross.reshape(SOURCES, rows, width)
            cross = jnp.where(factor > 0.0, cross * factor, 0.0).astype(jnp.bfloat16)
            start = pl.multiple_of((step * BATCH + k) * rows, rows)
            cross_ref[:, pl.ds(start, rows), :] = cross

    @pl.when(step >= PHASES)
    def _():
        first = (step - PHASES) * QUERIES
        for k in range(QUERIES):
            lagged = jnp.dot(inverse_ref[...], cross_ref[first + k], preferred_element_type=jnp.float32)
            out_ref[k] = (lagged / math.sqrt(NF * SEGMENT_TALLY)).astype(jnp.bfloat16)


def correlate(left, whole, split, alive, inverse):
    width = whole.shape[2]
    depth = left.shape[2]
    return pl.pallas_call(
        correlate_kernel,
        grid=(2 * PHASES,),
        in_specs=[
            pl.BlockSpec((BATCH, SOURCES * 2 * SUB, depth), lambda i: (jnp.minimum(i, PHASES - 1), 0, 0)),
            pl.BlockSpec((WHOLE, BATCH * 2 * SUB, width), lambda i: (0, jnp.minimum(i, PHASES - 1), 0)),
            pl.BlockSpec((SPLIT, BATCH * 2 * SUB, width), lambda i: (0, jnp.minimum(i, PHASES - 1), 0)),
            pl.BlockSpec((1, width), lambda i: (0, 0)),
            pl.BlockSpec((LAGS, BINS), lambda i: (0, 0)),
        ],
        out_specs=pl.BlockSpec((QUERIES, LAGS, width), lambda i: (jnp.maximum(i - PHASES, 0), 0, 0)),
        out_shape=jax.ShapeDtypeStruct((SOURCES, LAGS, width), jnp.bfloat16),
        scratch_shapes=[pltpu.VMEM((SOURCES, BINS, width), jnp.bfloat16)],
        compiler_params=pltpu.CompilerParams(vmem_limit_bytes=32 << 20),
    )(left, whole, split, alive, inverse)


def source_matrix(samples, alive, table):
    samples = samples.reshape(SOURCES, TEAM, TEAM_WINDOWS, SEGMENT_LENGTH)
    whole = samples[:, :, 0::2].reshape(SOURCES, WHOLE, SEGMENT_LENGTH)
    split = samples[:, :, 1::2].reshape(SOURCES, SPLIT, SEGMENT_LENGTH)
    samples = jnp.concatenate([whole, split], axis=1)
    spectra = jnp.einsum("qwt,kt->qwk", samples, table, preferred_element_type=jnp.float32)
    spectra = spectra.reshape(SOURCES, SEGMENT_TALLY, TILES, 2, SUB)
    level = jnp.mean(spectra[:, :, :, 0] ** 2 + spectra[:, :, :, 1] ** 2, axis=1)
    factor = alive[:, None, None] / jnp.sqrt(level + 0.01)
    src = (spectra * factor[:, None, :, None, :]).astype(jnp.bfloat16)
    src = jnp.transpose(src, (2, 0, 1, 3, 4))
    turned = jnp.stack([-src[:, :, :, 1], src[:, :, :, 0]], axis=3)
    depth = SEGMENT_TALLY * 2 * SUB
    both = jnp.stack([src, turned], axis=2).reshape(TILES, SOURCES, 2, 1, depth)
    row = jnp.arange(SUB, dtype=jnp.int32)[:, None]
    column = jnp.arange(depth, dtype=jnp.int32)[None, :]
    left = jnp.where(column % SUB == row, both, jnp.bfloat16(0.0))
    return left.reshape(TILES, SOURCES * 2 * SUB, depth)


def body(data, alive, sources):
    count = lax.axis_size("chan")
    me = lax.axis_index("chan")
    width = data.shape[1] // count
    table = forward_table()
    ids = sources.reshape(-1)
    near = ids[:, None] == me * width + jnp.arange(width, dtype=jnp.int32)[None, :]
    flags = jnp.sum(jnp.where(near, alive[None, :], 0), axis=1).astype(jnp.bfloat16)
    if data.shape[0] == HELD and count == TEAM * TEAM:
        lanes = jnp.concatenate([ids, jnp.full((128 - SOURCES,), -1, jnp.int32)])[None, :]
        flags = jnp.broadcast_to(flags[:, None], (SOURCES, PACKED - HELD))
        place = (me % TEAM).astype(jnp.int32)[None]
        whole, rows, picked = prepare(place, data, table, lanes, flags, count)
        planes = range(count // TEAM)
        teams = [[z * TEAM + p for p in range(TEAM)] for z in planes]
        across = [[z * TEAM + p for z in planes] for p in range(TEAM)]
        picked = lax.all_gather(picked, "chan", axis=0)
        rows = lax.all_to_all(rows, "chan", 0, 0, tiled=True, axis_index_groups=teams)
        whole = lax.all_to_all(whole, "chan", 0, 0, tiled=True)
        split = straddle(rows, table)
        split = lax.all_to_all(split, "chan", 0, 0, tiled=True, axis_index_groups=across)
        split = split.reshape(SPLIT, BINS, width)
        alive_sources = jnp.sum(picked[:, :, HELD].astype(jnp.float32), axis=0)
        samples = jnp.transpose(picked[:, :, :HELD], (1, 0, 2))
    else:
        chosen = jnp.where(jnp.arange(data.shape[1], dtype=jnp.int32)[:, None] == ids[None, :], 1.0, 0.0)
        picked = jnp.dot(data, chosen.astype(jnp.bfloat16), preferred_element_type=jnp.float32)
        picked = lax.all_gather(picked.astype(jnp.bfloat16), "chan", axis=0)
        samples = jnp.transpose(picked, (2, 0, 1))
        alive_sources = lax.psum(flags.astype(jnp.float32), "chan")
        blocks = data.reshape(data.shape[0], count, width)
        blocks = lax.all_to_all(blocks, "chan", split_axis=1, concat_axis=0, tiled=True)
        blocks = blocks.reshape(SEGMENT_TALLY, SEGMENT_LENGTH, width)
        spectra = jnp.einsum("kt,wtc->wkc", table, blocks, preferred_element_type=jnp.float32)
        spectra = spectra.astype(jnp.bfloat16).reshape(TEAM, TEAM_WINDOWS, BINS, width)
        whole = spectra[:, 0::2].reshape(WHOLE, BINS, width)
        split = spectra[:, 1::2].reshape(SPLIT, BINS, width)
    left = source_matrix(samples, alive_sources, table)
    out = correlate(left, whole, split, alive.astype(jnp.float32)[None, :], inverse_table())
    return out.reshape(ROUNDS, SRC, LAGS, width)


def solution(mesh):
    return jax.shard_map(
        body,
        mesh=mesh,
        in_specs=(P(("groups", "chan"), None), P(("groups", "chan")), P()),
        out_specs=P("groups", None, None, "chan"),
        check_vma=False,
    )
```

time: 328 us -> 177 us (0.54)
  waiting for transfers between devices: 130 us -> 43 us
  blocking collectives: 101 us -> 41 us
  matrix products: 22.5 us -> 1.13 us
  local copies, waits for them, and re-layouts: 52.9 us -> 32.3 us
  Pallas kernels: 0 us -> 15.1 us
  between operations: 0.16 us -> 13.6 us
  starting transfers between devices: 7.56 us -> 19.1 us
    psum x1 -> x0, blocking collectives: 101 us -> none  [body(): src = lax.psum(picked, 'chan').astype(jnp.bfloat16)]
    all_to_all x1 -> x2, waiting for transfers between devices: 130 us -> 42.1 us  [the longest x1 39.6 us: body(): whole = lax.all_to_all(whole, 'chan', 0, 0, tiled=True)]
    all_to_all x0 -> x1, blocking collectives: none -> 41 us  [body(): lax.all_to_all(rows, 'chan', 0, 0, tiled=True, axis_index_groups=teams)]
    dot_general x6 -> x1, matrix products: 22.5 us -> 1.13 us  [source_matrix(): jnp.einsum('qwt,kt->qwk', samples, table, preferred_element_type=jnp.floa...]
    dot_general x4 -> x0, local copies, waits for them, and re-layouts: 21.3 us -> none  [the longest x1 5.34 us: body(): jnp.einsum(form, src_re, own_im, preferred_element_type=jnp.float32)]
    pallas_call x0 -> x3, Pallas kernels: none -> 15.1 us  [the longest x1 7.89 us: correlate(): pl.pallas_call(correlate_kernel, grid=(2 * PHASES,), in_specs=[pl.BlockSp...]
    convert_element_type x2 -> x3, local copies, waits for them, and re-layouts: 13.9 us -> 0.13 us  [the longest x2 0.11 us: inverse_table(): return tile_order(table).T.astype(jnp.bfloat16)]
    all_to_all x1 -> x2, starting transfers between devices: 7.56 us -> 19.1 us  [the longest x1 14.1 us: body(): lax.all_to_all(split, 'chan', 0, 0, tiled=True, axis_index_groups=across)]
  transfers between devices with their start and end apart: 1 -> 3, of which waited for: 1 -> 3; matrix products, arithmetic and copies ran while one was open for 1% -> 19% of each run, Pallas kernels for 0% -> 1%
where the time goes in v1:
time: 177 us
  waiting for transfers between devices  43 us (24%)
  blocking collectives  41 us (23%)
  local copies, waits for them, and re-layouts  32.3 us (18%)
  starting transfers between devices  19.1 us (11%)
  Pallas kernels  15.1 us (9%)
  between operations  13.6 us (8%)
  other arithmetic  11.3 us (6%)
    all_to_all x1, blocking collectives, body(): lax.all_to_all(rows, 'chan', 0, 0, tiled=True, axis_index_groups=teams)  41 us
    all_to_all x1, waiting for transfers between devices, body(): whole = lax.all_to_all(whole, 'chan', 0, 0, tiled=True)  39.6 us
    all_to_all x1, starting transfers between devices, body(): lax.all_to_all(split, 'chan', 0, 0, tiled=True, axis_index_groups=across)  14.1 us
    slice x2, local copies, waits for them, and re-layouts, source_matrix(): whole = samples[:, :, 0::2].reshape(SOURCES, WHOLE, SEGMENT_LENGTH)  11.4 us
    unnamed x15, local copies, waits for them, and re-layouts  9.56 us
    pallas_call x1, Pallas kernels, correlate(): pl.pallas_call(correlate_kernel, grid=(2 * PHASES,), in_specs=[pl.BlockSp...  7.89 us
    pallas_call x1, Pallas kernels, prepare(): pl.pallas_call(prepare_kernel, grid_spec=pltpu.PrefetchScalarGridSpec(num...  5.47 us
    all_to_all x1, starting transfers between devices, body(): whole = lax.all_to_all(whole, 'chan', 0, 0, tiled=True)  5.03 us
  transfers between devices with their start and end apart: 3, of which 3 were waited for; matrix products, arithmetic and copies ran while one was open for 19% of the time, Pallas kernels for 1%

profile of v1, /device:TPU:0, one launch (start us, length us, event | category | flops | bytes accessed | tf_op | source)
XLA Modules:
  0.0 176.6 jit_solution(601202426417977959)
XLA Ops:
  6.5 0.8 reshape.86
  7.3 0.9 select_reduce_fusion
  8.2 1.1 fusion.18
  9.3 0.7 copy-done.4
  10.2 3.1 %copy-done.1 = bf16[896,4096]{1,0:T(8,128)(2,1)S(1)} copy-done((bf16[896,4096]{1,0:T(8,128)(2,1)S(1)}, bf16[896,4096]{1,0:T(8,128)(2,1)}, u32[]{:S(2)}) %copy-start.1) | copy-done | bytes 7340056
  13.3 5.5 %shard_map.37 = (bf16[16,256,256]{2,1,0:T(8,128)(2,1)S(1)}, bf16[4,4,384,256]{3,2,1,0:T(8,128)(2,1)S(1)}, bf16[32,1024]{1,0:T(8,128)(2,1)}) custom-call(s32[1]{0:T(128)} %bitcast.1.place_ref, bf16[896,4096]{1,0:T(8,128)(2,1)S(1)} %copy-done.1, bf16[256,512]{1,0:T(8,128)(2,1)S(1)} %bitcast.45, s32[1,128]{1,0:T(1,128)S(1)} %pad_bitcast_fusion.ids_ref, ...), custom_call_target="tpu_custom_call" | custom-call | tf_op jit(solution)/shard_map/pallas_call | solution.py:89
  18.7 41.0 %all_to_all.15.rows_ref = bf16[4,4,384,256]{3,2,1,0:T(8,128)(2,1)S(1)} all-to-all(bf16[4,4,384,256]{3,2,1,0:T(8,128)(2,1)S(1)} %get-tuple-element.10), channel_id=1, replica_groups={{0,1,2,3},{4,5,6,7},{8,9,10,11},{12,13,14,15},{16,17,18,19},{20,21,22,2..., dimensions={0} | all-to-all | bytes 6291456 | tf_op jit(solution)/shard_map/all_to_all | solution.py:239
  59.7 5.0 %all-to-all-start = ((bf16[16,256,256]{2,1,0:T(8,128)(2,1)}), bf16[16,256,256]{2,1,0:T(8,128)(2,1)}, u32[]{:S(2)}, u32[]{:S(2)}) async-start(bf16[16,256,256]{2,1,0:T(8,128)(2,1)} %copy-done.3), calls=%async_computation | async-start | bytes 4194304 | tf_op jit(solution)/shard_map/all_to_all | solution.py:240
  64.8 0.7 all-gather.3.cloned.1.call-update
  65.5 1.8 %shard_map.38 = bf16[4,768,256]{2,1,0:T(8,128)(2,1)S(1)} custom-call(bf16[4,4,384,256]{3,2,1,0:T(8,128)(2,1)S(1)} %all_to_all.15.rows_ref, bf16[256,512]{1,0:T(8,128)(2,1)S(1)} %bitcast.46), custom_call_target="tpu_custom_call" | custom-call | tf_op jit(solution)/shard_map/pallas_call | solution.py:128
  67.3 1.1 copy-done.2
  68.4 39.6 %all-to-all-done.whole_ref = bf16[16,256,256]{2,1,0:T(8,128)(2,1)} async-done(((bf16[16,256,256]{2,1,0:T(8,128)(2,1)}), bf16[16,256,256]{2,1,0:T(8,128)(2,1)}, u32[]{:S(2)}, u32[]{:S(2)}) %all-to-all-start) | async-done | bytes 2097184 | tf_op jit(solution)/shard_map/all_to_all | solution.py:240
  108.0 14.1 %all-to-all-start.2 = ((bf16[4,768,256]{2,1,0:T(8,128)(2,1)}), bf16[4,768,256]{2,1,0:T(8,128)(2,1)S(1)}, u32[]{:S(2)}, u32[]{:S(2)}) async-start(bf16[4,768,256]{2,1,0:T(8,128)(2,1)} %copy-done.2), calls=%async_computation.2 | async-start | bytes 3145728 | tf_op jit(solution)/shard_map/all_to_all | solution.py:242
  122.1 0.6 cosine_convert_fusion
  123.1 1.3 slice.32
  124.4 1.2 copy.42
  125.6 2.1 %reshape.87 = bf16[32,4,7,512]{3,2,1,0:T(8,128)(2,1)S(1)} reshape(bf16[32,16,896]{2,1,0:T(8,128)(2,1)} %bitcast.51) | data formatting | bytes 1835008 | tf_op jit(solution)/shard_map/reshape | solution.py:203
  127.7 1.2 slice.26
  128.9 10.1 %slice.25 = bf16[32,4,4,512]{3,2,1,0:T(4,128)(2,1)} slice(bf16[32,4,7,512]{3,2,1,0:T(8,128)(2,1)S(1)} %reshape.87), slice={[0:32:1], [0:4:1], [0:7:2], [0:512:1]} | slice | bytes 1048576 | tf_op jit(solution)/shard_map/slice | solution.py:204
  139.3 1.3 copy.27
  140.6 1.0 convert_reduce_fusion
  141.7 1.1 fusion.3
  143.2 0.5 fusion
  143.6 2.2 %copy.29 = bf16[16,32,1,1,448]{4,1,3,2,0:T(8,128)(2,1)} copy(bf16[16,32,1,1,448]{1,0,4,3,2:T(8,128)(2,1)S(1)} %bitcast.49) | data formatting | bytes 917504 | tf_op jit(solution)/shard_map/stack | solution.py:215
  146.0 0.4 pad_maximum_fusion
  146.4 2.2 %copy.30 = bf16[16,32,1,1,448]{4,1,3,2,0:T(8,128)(2,1)} copy(bf16[16,32,1,1,448]{1,0,4,3,2:T(8,128)(2,1)S(1)} %bitcast.50) | data formatting | bytes 917504 | tf_op jit(solution)/shard_map/stack | solution.py:215
  148.5 1.3 maximum_bitcast_fusion
  149.8 1.1 copy.31
  151.0 5.0 %bitcast_select_fusion.left_ref = bf16[16,512,448]{2,1,0:T(8,128)(2,1)} fusion(pred[512,448]{1,0:T(8,128)(4,1)S(1)} %bitcast.56, bf16[16,32,2,448]{3,2,1,0:T(2,128)(2,1)S(1)} %copy.31), kind=kLoop, calls=%fused_computation | loop fusion | flops 3670016 | bytes 8486912 | tf_op jit(solution)/shard_map/jit(_where)/select_n | solution.py:218
  156.0 2.5 %all-to-all-done.2 = bf16[4,768,256]{2,1,0:T(8,128)(2,1)S(1)} async-done(((bf16[4,768,256]{2,1,0:T(8,128)(2,1)}), bf16[4,768,256]{2,1,0:T(8,128)(2,1)S(1)}, u32[]{:S(2)}, u32[]{:S(2)}) %all-to-all-start.2) | async-done | bytes 1572896 | tf_op jit(solution)/shard_map/all_to_all | solution.py:242
  158.5 3.4 %copy-done = bf16[16,512,448]{2,1,0:T(8,128)(2,1)S(1)} copy-done((bf16[16,512,448]{2,1,0:T(8,128)(2,1)S(1)}, bf16[16,512,448]{2,1,0:T(8,128)(2,1)}, u32[]{:S(2)}) %copy-start) | copy-done | bytes 7340056
  161.9 7.9 %shard_map.39 = bf16[32,256,256]{2,1,0:T(8,128)(2,1)} custom-call(bf16[16,512,448]{2,1,0:T(8,128)(2,1)S(1)} %copy-done, bf16[16,256,256]{2,1,0:T(8,128)(2,1)} %all-to-all-done.whole_ref, bf16[12,256,256]{2,1,0:T(8,128)(2,1)S(1)} %bitcast.44, f32[1,256]{1,0:T(1,128)S(1)} %bitcast.48, bf16[256,256]{1,0:T(8,128)(2,1)S(1)} %bitcast.47), custom_call_target="tpu_custom_call" | custom-call | tf_op jit(solution)/shard_map/pallas_call | solution.py:185
  (31 shorter events, 1.5 us)
Async XLA Ops:
  9.3 0.7 copy-start.4
  10.2 3.1 %copy-start.1 = (bf16[896,4096]{1,0:T(8,128)(2,1)S(1)}, bf16[896,4096]{1,0:T(8,128)(2,1)}, u32[]{:S(2)}) copy-start(bf16[896,4096]{1,0:T(8,128)(2,1)} %data_ref.1) | copy-start | bytes 22020100
  18.7 41.0 %copy-start.3 = (bf16[16,256,256]{2,1,0:T(8,128)(2,1)}, bf16[16,256,256]{2,1,0:T(8,128)(2,1)S(1)}, u32[]{:S(2)}) copy-start(bf16[16,256,256]{2,1,0:T(8,128)(2,1)S(1)} %get-tuple-element.9) | copy-start | bytes 6291460
  59.7 48.3 %all-to-all-start = ((bf16[16,256,256]{2,1,0:T(8,128)(2,1)}), bf16[16,256,256]{2,1,0:T(8,128)(2,1)}, u32[]{:S(2)}, u32[]{:S(2)}) async-start(bf16[16,256,256]{2,1,0:T(8,128)(2,1)} %copy-done.3), calls=%async_computation | async-start | bytes 4194304 | tf_op jit(solution)/shard_map/all_to_all | solution.py:240
  64.7 58.4 %all-gather.3.cloned.1.call-start = ((), (), s32[]{:S(2)}) async-start(), calls=%async_computation.3 | async-start | bytes 1114112 | tf_op jit(solution)/shard_map/all_gather | solution.py:238
  67.3 1.2 copy-start.2
  68.4 54.3 %copy-start.6 = (s32[256]{0:T(256)S(1)}, s32[256]{0:T(256)}, u32[]{:S(2)}) copy-start(s32[256]{0:T(256)} %param.4) | copy-start | bytes 3076
  108.0 50.5 %all-to-all-start.2 = ((bf16[4,768,256]{2,1,0:T(8,128)(2,1)}), bf16[4,768,256]{2,1,0:T(8,128)(2,1)S(1)}, u32[]{:S(2)}, u32[]{:S(2)}) async-start(bf16[4,768,256]{2,1,0:T(8,128)(2,1)} %copy-done.2), calls=%async_computation.2 | async-start | bytes 3145728 | tf_op jit(solution)/shard_map/all_to_all | solution.py:242
  127.7 14.0 %copy-start.5 = (bf16[256,512]{1,0:T(8,128)(2,1)S(1)}, bf16[256,512]{1,0:T(8,128)(2,1)}, u32[]{:S(2)}) copy-start(bf16[256,512]{1,0:T(8,128)(2,1)} %copy-done.4) | copy-start | bytes 786436
  158.5 3.4 %copy-start = (bf16[16,512,448]{2,1,0:T(8,128)(2,1)S(1)}, bf16[16,512,448]{2,1,0:T(8,128)(2,1)}, u32[]{:S(2)}) copy-start(bf16[16,512,448]{2,1,0:T(8,128)(2,1)} %bitcast_select_fusion.left_ref) | copy-start | bytes 22020100
Sparse Core Ops, SparseCore 0:
  67.7 55.3 all-gather.2

commit v2 on v0

v2 whole, which is shorter than its diff:
```python
import functools
import math

import jax
import jax.numpy as jnp
import ml_dtypes
import numpy as np
from jax import lax
from jax.experimental import pallas as pl
from jax.experimental.pallas import tpu as pltpu
from jax.sharding import PartitionSpec as P

SEGMENT_LENGTH = 512
NF = 128
LAGS = 256
SRC = 16
ROUNDS = 2
SEGMENT_TALLY = 28

SOURCES = SRC * ROUNDS
BINS = 2 * NF
SUB = 8
TILES = NF // SUB
TEAM = 4
TEAM_WINDOWS = 7
STEP = 128
HELD = TEAM_WINDOWS * SEGMENT_LENGTH // TEAM
STRADDLE = HELD - SEGMENT_LENGTH
HALF = SEGMENT_LENGTH // 2
WHOLE = 16
SPLIT = 12
PACKED = 1024
SHARE = SOURCES // TEAM
DEPTH = 512
LARGE = 56 << 20


def angles(times):
    bins = np.arange(NF)[:, None] + 1
    turn = bins * times[None, :] % SEGMENT_LENGTH * (2.0 * np.pi / SEGMENT_LENGTH)
    table = np.stack([np.cos(turn), -np.sin(turn)])
    table = table.reshape(2, TILES, SUB, times.size).transpose(1, 0, 2, 3)
    return table.reshape(BINS, times.size)


def forward_table():
    table = angles(np.arange(SEGMENT_LENGTH)) / math.sqrt(SEGMENT_LENGTH)
    return jnp.asarray(table.astype(ml_dtypes.bfloat16))


def inverse_table():
    table = angles(np.arange(LAGS) - LAGS // 2)
    return jnp.asarray(np.ascontiguousarray(table.T).astype(ml_dtypes.bfloat16))


def position():
    me = lax.axis_index("chan")
    return me // TEAM, me % TEAM


def straddling(data_ref, j, place, column, width):
    row = pl.multiple_of(jnp.where(j < place, j, j + SEGMENT_LENGTH // STEP) * STEP, STEP)
    return data_ref[pl.ds(row, STEP), pl.ds(pl.multiple_of(column * width, width), width)]


def transform(table_ref, block):
    return jnp.dot(table_ref[...], block, preferred_element_type=jnp.float32).astype(jnp.bfloat16)


def prepare_kernel(sources_ref, alive_ref, data_ref, table_ref, whole_ref, acc_ref):
    step = pl.program_id(0)
    _, place = position()
    columns = data_ref.shape[1]
    width = columns // TEAM
    start = pl.multiple_of(place * STEP, STEP)
    for k in range(TEAM):
        lanes = slice(k * width, (k + 1) * width)
        whole_ref[step * TEAM + k, :BINS, :] = transform(table_ref, data_ref[pl.ds(start, SEGMENT_LENGTH), lanes])
    lane = lax.broadcasted_iota(jnp.int32, (1, 128), 1)
    ids = jnp.full((1, 128), -1, jnp.int32)
    for q in range(SOURCES):
        ids = jnp.where(lane == q, sources_ref[q // SRC, q % SRC], ids)
    channel = lax.broadcasted_iota(jnp.int32, (columns, 128), 0)
    chosen = jnp.where(channel == ids - step * columns, 1.0, 0.0).astype(jnp.bfloat16)
    part = jnp.dot(data_ref[...], chosen, preferred_element_type=jnp.float32)

    @pl.when(step == 0)
    def _():
        acc_ref[...] = part

    @pl.when(step > 0)
    def _():
        acc_ref[...] += part

    @pl.when(step == pl.num_programs(0) - 1)
    def _():
        row = lax.broadcasted_iota(jnp.int32, (SOURCES, PACKED - HELD), 0)
        flags = jnp.zeros((SOURCES, PACKED - HELD), jnp.float32)
        for q in range(SOURCES):
            local = sources_ref[q // SRC, q % SRC] - lax.axis_index("chan") * width
            inside = (local >= 0) & (local < width)
            flag = jnp.where(inside, alive_ref[jnp.clip(local, 0, width - 1)], 0)
            flags = jnp.where(row == q, flag.astype(jnp.float32), flags)
        picked = jnp.concatenate([acc_ref[...].T[:SOURCES, :], flags], axis=1)
        for k in range(TEAM):
            quarter = picked[k * SHARE : (k + 1) * SHARE]
            rows = [quarter[:, c * width : (c + 1) * width] for c in range(PACKED // width)]
            rows = jnp.concatenate(rows, axis=0).astype(jnp.bfloat16)
            for plane in range(whole_ref.shape[0] // TEAM):
                whole_ref[plane * TEAM + k, BINS:, :] = rows


def prepare(sources, alive, data, table, count):
    columns = data.shape[1] // count * TEAM
    width = columns // TEAM
    depth = BINS + SHARE * PACKED // width
    return pl.pallas_call(
        prepare_kernel,
        grid=(count // TEAM,),
        in_specs=[
            pl.BlockSpec(memory_space=pltpu.SMEM),
            pl.BlockSpec(memory_space=pltpu.SMEM),
            pl.BlockSpec((HELD, columns), lambda i: (0, i)),
            pl.BlockSpec((BINS, SEGMENT_LENGTH), lambda i: (0, 0)),
        ],
        out_specs=pl.BlockSpec((count, depth, width), lambda i: (0, 0, 0)),
        scratch_shapes=[pltpu.VMEM((HELD, 128), jnp.float32)],
        out_shape=jax.ShapeDtypeStruct((count, depth, width), jnp.bfloat16),
        compiler_params=pltpu.CompilerParams(vmem_limit_bytes=LARGE),
        name="prepare",
    )(sources, alive, data, table)


def lend_kernel(data_ref, out_ref):
    _, place = position()
    width = out_ref.shape[2]
    for side in range(2):
        for j in range(STRADDLE // STEP):
            piece = straddling(data_ref, j, place, side * 2 + 1 - place % 2, width)
            out_ref[side, j * STEP : (j + 1) * STEP, :] = piece


def lend(data, count):
    width = data.shape[1] // count
    return pl.pallas_call(
        lend_kernel,
        grid=(count // TEAM,),
        in_specs=[pl.BlockSpec((HELD, TEAM * width), lambda i: (0, i))],
        out_specs=pl.BlockSpec((2, STRADDLE, width), lambda i: (i, 0, 0)),
        out_shape=jax.ShapeDtypeStruct((count // 2, STRADDLE, width), jnp.bfloat16),
        compiler_params=pltpu.CompilerParams(vmem_limit_bytes=LARGE),
        cost_estimate=pl.CostEstimate(flops=0, bytes_accessed=1 << 20, transcendentals=0),
        name="lend",
    )(data)


def halves_kernel(data_ref, lent_ref, table_ref, keep_ref, give_ref, scratch_ref):
    _, place = position()
    side, core = place // 2, place % 2
    width = keep_ref.shape[2]
    for slot, (out_ref, target) in enumerate(((keep_ref, side), (give_ref, 1 - side))):
        chip_ref = scratch_ref.at[slot]
        for j in range(STRADDLE // STEP):
            start = pl.multiple_of(core * STRADDLE + j * STEP, STEP)
            chip_ref[pl.ds(start, STEP), :] = straddling(data_ref, j, place, target * 2 + core, width)
        chip_ref[pl.ds(pl.multiple_of((1 - core) * STRADDLE, STEP), STRADDLE), :] = lent_ref[target]
        start = pl.multiple_of(side * HALF, HALF)
        out_ref[0, :BINS, :] = transform(table_ref, chip_ref[pl.ds(start, SEGMENT_LENGTH), :])
        start = pl.multiple_of((1 - side) * SEGMENT_LENGTH, HALF)
        out_ref[0, BINS:, :] = chip_ref[pl.ds(start, HALF), :]


def halves(data, lent, table, count):
    width = data.shape[1] // count
    planes = count // TEAM
    shape = jax.ShapeDtypeStruct((planes, BINS + HALF, width), jnp.bfloat16)
    return pl.pallas_call(
        halves_kernel,
        grid=(planes,),
        in_specs=[
            pl.BlockSpec((HELD, TEAM * width), lambda i: (0, i)),
            pl.BlockSpec((2, STRADDLE, width), lambda i: (i, 0, 0)),
            pl.BlockSpec((BINS, SEGMENT_LENGTH), lambda i: (0, 0)),
        ],
        out_specs=[pl.BlockSpec((1, BINS + HALF, width), lambda i: (i, 0, 0))] * 2,
        scratch_shapes=[pltpu.VMEM((2, 2 * STRADDLE, width), jnp.bfloat16)],
        out_shape=[shape, shape],
        compiler_params=pltpu.CompilerParams(vmem_limit_bytes=LARGE),
        cost_estimate=pl.CostEstimate(flops=0, bytes_accessed=1 << 20, transcendentals=0),
        name="halves",
    )(data, lent, table)


def straddle_kernel(keep_ref, got_ref, table_ref, *refs):
    out_refs, scratch_ref = refs[:-1], refs[-1]
    mine, place = position()
    side = place // 2
    for k, out_ref in enumerate(out_refs):
        plane = mine ^ k
        out_ref[2 * side] = keep_ref[plane, :BINS, :]
        out_ref[2 - 2 * side] = got_ref[plane, :BINS, :]
        scratch_ref[k, pl.ds(pl.multiple_of(side * HALF, HALF), HALF), :] = keep_ref[plane, BINS:, :]
        scratch_ref[k, pl.ds(pl.multiple_of((1 - side) * HALF, HALF), HALF), :] = got_ref[plane, BINS:, :]
        out_ref[1] = transform(table_ref, scratch_ref[k])


def straddle(keep, got, table):
    planes, _, width = keep.shape
    shape = jax.ShapeDtypeStruct((SPLIT // TEAM, BINS, width), jnp.bfloat16)
    return pl.pallas_call(
        straddle_kernel,
        out_shape=[shape] * planes,
        scratch_shapes=[pltpu.VMEM((planes, SEGMENT_LENGTH, width), jnp.bfloat16)],
        compiler_params=pltpu.CompilerParams(vmem_limit_bytes=16 << 20),
        cost_estimate=pl.CostEstimate(flops=0, bytes_accessed=1 << 20, transcendentals=0),
        name="straddle",
    )(keep, got, table)


def whiten_kernel(picked_ref, table_ref, out_ref, samples_ref):
    width = picked_ref.shape[2]
    flags = jnp.zeros((SHARE, PACKED - HELD), jnp.float32)
    for j in range(picked_ref.shape[0]):
        rows = picked_ref[j].astype(jnp.float32)
        for block in range(PACKED // 128):
            lane = block * 128 % width
            piece = rows[block * 128 // width * SHARE :][:SHARE, lane : lane + 128]
            if block * 128 < HELD:
                window, lane = divmod(j * HELD + block * 128, SEGMENT_LENGTH)
                samples_ref[window * SHARE : (window + 1) * SHARE, lane : lane + 128] = piece
            else:
                flags += piece
    spectra = lax.dot_general(
        samples_ref[...].astype(jnp.bfloat16),
        table_ref[...],
        (((1,), (1,)), ((), ())),
        preferred_element_type=jnp.float32,
    ).reshape(SEGMENT_TALLY, SHARE, BINS)
    power = jnp.sum(jnp.square(spectra), axis=0)
    lane = lax.broadcasted_iota(jnp.int32, (SHARE, BINS), 1)
    other = jnp.where(lane % (2 * SUB) < SUB, pltpu.roll(power, BINS - SUB, 1), pltpu.roll(power, SUB, 1))
    level = (power + other) / SEGMENT_TALLY
    factor = jnp.concatenate([flags] * (BINS // 128), axis=1) / jnp.sqrt(level + 0.01)
    src = (spectra * factor[None]).astype(jnp.bfloat16).astype(jnp.float32)
    lane = lax.broadcasted_iota(jnp.int32, (SHARE, 128), 1) // (2 * SUB)
    each = 128 // (2 * SUB)
    for tile in range(TILES):
        half, at = divmod(tile, each)
        for group in range(DEPTH // 128):
            out = jnp.zeros((SHARE, 128), jnp.float32)
            for k in range(each):
                window = group * each + k
                if window < SEGMENT_TALLY:
                    piece = src[window, :, half * 128 : (half + 1) * 128]
                    shift = (k - at) * 2 * SUB % 128
                    piece = pltpu.roll(piece, shift, 1) if shift else piece
                    out = jnp.where(lane == k, piece, out)
            out_ref[tile, :, group * 128 : (group + 1) * 128] = out.astype(jnp.bfloat16)


def whiten(whole, table):
    count, depth, width = whole.shape
    rows = depth - BINS
    return pl.pallas_call(
        whiten_kernel,
        grid=(1,),
        in_specs=[
            pl.BlockSpec((count, rows, width), lambda i: (0, BINS // rows, 0)),
            pl.BlockSpec((BINS, SEGMENT_LENGTH), lambda i: (0, 0)),
        ],
        out_specs=pl.BlockSpec((TILES, SHARE, DEPTH), lambda i: (0, 0, 0)),
        scratch_shapes=[pltpu.VMEM((SEGMENT_TALLY * SHARE, SEGMENT_LENGTH), jnp.float32)],
        out_shape=jax.ShapeDtypeStruct((TILES, SHARE, DEPTH), jnp.bfloat16),
        compiler_params=pltpu.CompilerParams(vmem_limit_bytes=16 << 20),
        cost_estimate=pl.CostEstimate(flops=0, bytes_accessed=1 << 18, transcendentals=0),
        name="whiten",
    )(whole, table)


def left_kernel(*refs):
    src_refs, left_ref = refs[:-1], refs[-1]
    src = jnp.concatenate([ref[0].astype(jnp.float32) for ref in src_refs], axis=0)
    lane = lax.broadcasted_iota(jnp.int32, (SOURCES, DEPTH), 1)
    turned = jnp.where(lane % (2 * SUB) < SUB, -pltpu.roll(src, DEPTH - SUB, 1), pltpu.roll(src, SUB, 1))
    row = lax.broadcasted_iota(jnp.int32, (1, 2 * SUB, DEPTH), 1)
    lane = lax.broadcasted_iota(jnp.int32, (1, 2 * SUB, DEPTH), 2)
    both = jnp.where(row < SUB, src[:, None, :], turned[:, None, :])
    both = jnp.where(lane % SUB == row % SUB, both, 0.0)
    left_ref[0] = both.reshape(SOURCES * 2 * SUB, DEPTH).astype(jnp.bfloat16)


def left_factor(src):
    return pl.pallas_call(
        left_kernel,
        grid=(TILES,),
        in_specs=[pl.BlockSpec((1, SHARE, DEPTH), lambda i: (i, 0, 0))] * TEAM,
        out_specs=pl.BlockSpec((1, SOURCES * 2 * SUB, DEPTH), lambda i: (i, 0, 0)),
        out_shape=jax.ShapeDtypeStruct((TILES, SOURCES * 2 * SUB, DEPTH), jnp.bfloat16),
        compiler_params=pltpu.CompilerParams(vmem_limit_bytes=16 << 20),
        cost_estimate=pl.CostEstimate(flops=0, bytes_accessed=1 << 20, transcendentals=0),
        name="left",
    )(*src)


def whiten_all(samples, alive, table):
    samples = samples.reshape(SOURCES, SEGMENT_TALLY, SEGMENT_LENGTH)
    spectra = jnp.einsum("qwt,kt->qwk", samples, table, preferred_element_type=jnp.float32)
    power = jnp.mean(spectra**2, axis=1).reshape(SOURCES, TILES, 2, SUB)
    level = power[:, :, :1] + power[:, :, 1:]
    factor = alive[:, None, None, None] / jnp.sqrt(level + 0.01)
    factor = jnp.broadcast_to(factor, (SOURCES, TILES, 2, SUB)).reshape(SOURCES, BINS)
    src = (spectra * factor[:, None, :]).astype(jnp.bfloat16)
    src = jnp.transpose(src.reshape(SOURCES, SEGMENT_TALLY, TILES, 2 * SUB), (2, 0, 1, 3))
    src = src.reshape(TILES, SOURCES, SEGMENT_TALLY * 2 * SUB)
    src = jnp.pad(src, ((0, 0), (0, 0), (0, DEPTH - SEGMENT_TALLY * 2 * SUB)))
    return [src[:, k * SHARE : (k + 1) * SHARE] for k in range(TEAM)]


PHASES = 4
BATCH = TILES // PHASES


def correlate_kernel(relative, left_ref, whole_ref, *refs):
    split_refs, (alive_ref, inverse_ref, out_ref, right_ref, cross_ref) = refs[:TEAM], refs[TEAM:]
    step = pl.program_id(0)
    mine, place = position() if relative else (0, 0)
    width = whole_ref.shape[2]
    rows = 2 * SUB
    span = TEAM_WINDOWS * rows

    @pl.when(step == 0)
    def _():
        pad = DEPTH - SEGMENT_TALLY * rows
        right_ref[:, DEPTH - pad :, :] = jnp.zeros((BATCH, pad, width), jnp.bfloat16)

    @pl.when(step < PHASES)
    def _():
        alive = alive_ref[...].astype(jnp.float32)
        for k in range(BATCH):
            tile = slice(k * rows, (k + 1) * rows)
            for j in range(WHOLE):
                start = j // TEAM * span + j % TEAM * 2 * rows
                right_ref[k, start : start + rows, :] = whole_ref[j, tile, :]
            for plane in range(TEAM):
                for j in range(SPLIT // TEAM):
                    start = pl.multiple_of((plane ^ mine) * span + (2 * j + 1) * rows, rows)
                    right_ref[k, pl.ds(start, rows), :] = split_refs[plane][j, tile, :]
            right = right_ref[k]
            power = jnp.square(right.astype(jnp.float32)).reshape(DEPTH // rows, rows, width)
            power = jnp.sum(power, axis=0)
            level = (power[:SUB] + power[SUB:]) / SEGMENT_TALLY
            factor = alive / jnp.sqrt(level + 0.01)
            factor = jnp.concatenate([factor, factor], axis=0)[None]
            cross = jnp.dot(left_ref[k], right, preferred_element_type=jnp.float32)
            cross = cross.reshape(SOURCES, rows, width)
            cross = jnp.where(factor > 0.0, cross * factor, 0.0).astype(jnp.bfloat16)
            start = pl.multiple_of((step * BATCH + k) * rows, rows)
            cross_ref[:, pl.ds(start, rows), :] = cross

    @pl.when(step >= PHASES)
    def _():
        first = ((step - PHASES) ^ place) * SHARE
        for k in range(SHARE):
            lagged = jnp.dot(inverse_ref[...], cross_ref[first + k], preferred_element_type=jnp.float32)
            out_ref[k] = (lagged / math.sqrt(NF * SEGMENT_TALLY)).astype(jnp.bfloat16)


def correlate(relative, left, whole, split, alive, inverse):
    width = whole.shape[2]
    early = lambda i: jnp.minimum(i, PHASES - 1)
    return pl.pallas_call(
        functools.partial(correlate_kernel, relative),
        grid=(2 * PHASES,),
        in_specs=[
            pl.BlockSpec((BATCH, SOURCES * 2 * SUB, DEPTH), lambda i: (early(i), 0, 0)),
            pl.BlockSpec((WHOLE, BATCH * 2 * SUB, width), lambda i: (0, early(i), 0)),
        ]
        + [pl.BlockSpec((SPLIT // TEAM, BATCH * 2 * SUB, width), lambda i: (0, early(i), 0))] * TEAM
        + [
            pl.BlockSpec((1, width), lambda i: (0, 0)),
            pl.BlockSpec((LAGS, BINS), lambda i: (0, 0)),
        ],
        out_specs=pl.BlockSpec((SHARE, LAGS, width), lambda i: (jnp.maximum(i - PHASES, 0), 0, 0)),
        scratch_shapes=[
            pltpu.VMEM((BATCH, DEPTH, width), jnp.bfloat16),
            pltpu.VMEM((SOURCES, BINS, width), jnp.bfloat16),
        ],
        out_shape=jax.ShapeDtypeStruct((SOURCES, LAGS, width), jnp.bfloat16),
        compiler_params=pltpu.CompilerParams(vmem_limit_bytes=24 << 20),
        name="correlate",
    )(left, whole, *split, alive, inverse)


def body(data, alive, sources):
    count = lax.axis_size("chan")
    width = data.shape[1] // count
    table = forward_table()
    relative = data.shape[0] == HELD and count == TEAM * TEAM
    if relative:
        swap = lambda x, k: lax.ppermute(x, "chan", [(i, i ^ k) for i in range(count)])
        whole = prepare(sources, alive, data, table, count)
        data, whole = lax.optimization_barrier((data, whole))
        lent = swap(lend(data, count), 1)
        whole = lax.all_to_all(whole, "chan", 0, 0, tiled=True)
        keep, give = halves(data, lent, table, count)
        split = straddle(keep, swap(give, 2), table)
        whole, _ = lax.optimization_barrier((whole, split[1]))
        split = [split[0]] + [swap(split[k], k * TEAM) for k in range(1, TEAM)]
        src = whiten(whole, table)
        src = [src] + [swap(src, k) for k in range(1, TEAM)]
    else:
        me = lax.axis_index("chan")
        ids = sources.reshape(-1)
        near = ids[:, None] == me * width + jnp.arange(width, dtype=jnp.int32)[None, :]
        flags = jnp.sum(jnp.where(near, alive[None, :], 0), axis=1).astype(jnp.float32)
        chosen = jnp.where(jnp.arange(data.shape[1], dtype=jnp.int32)[:, None] == ids[None, :], 1.0, 0.0)
        picked = jnp.dot(data, chosen.astype(jnp.bfloat16), preferred_element_type=jnp.float32)
        picked = lax.all_gather(picked.astype(jnp.bfloat16), "chan", axis=0)
        alive_sources = lax.psum(flags, "chan")
        blocks = data.reshape(data.shape[0], count, width)
        blocks = lax.all_to_all(blocks, "chan", split_axis=1, concat_axis=0, tiled=True)
        blocks = blocks.reshape(SEGMENT_TALLY, SEGMENT_LENGTH, width)
        spectra = jnp.einsum("kt,wtc->wkc", table, blocks, preferred_element_type=jnp.float32)
        spectra = spectra.astype(jnp.bfloat16).reshape(TEAM, TEAM_WINDOWS, BINS, width)
        whole = spectra[:, 0::2].reshape(WHOLE, BINS, width)
        split = [spectra[z, 1::2] for z in range(TEAM)]
        src = whiten_all(jnp.transpose(picked, (2, 0, 1)), alive_sources, table)
    left = left_factor(src)
    out = correlate(relative, left, whole, split, alive[None, :], inverse_table())
    return out.reshape(ROUNDS, SRC, LAGS, width)


def solution(mesh):
    return jax.shard_map(
        body,
        mesh=mesh,
        in_specs=(P(("groups", "chan"), None), P(("groups", "chan")), P()),
        out_specs=P("groups", None, None, "chan"),
        check_vma=False,
    )
```

time: 328 us -> 115 us (0.35)
  the two profiles are of different devices: /device:TPU:0 before, /device:TPU:20 now
where the time goes in v2:
time: 115 us
  waiting for transfers between devices  69 us (60%)
  Pallas kernels  31.1 us (27%)
  starting transfers between devices  12.4 us (11%)
  local copies, waits for them, and re-layouts  2.42 us (2%)
    ppermute x8, waiting for transfers between devices, body(): lax.ppermute(x, 'chan', [(i, i ^ k) for i in range(count)])  69 us
    pallas_call x1, Pallas kernels, correlate(): pl.pallas_call(functools.partial(correlate_kernel, relative), grid=(2 * P...  8.04 us
    pallas_call x1, Pallas kernels, prepare(): pl.pallas_call(prepare_kernel, grid=(count // TEAM,), in_specs=[pl.BlockS...  7.61 us
    ppermute x8, starting transfers between devices, body(): lax.ppermute(x, 'chan', [(i, i ^ k) for i in range(count)])  6.3 us
    all_to_all x1, starting transfers between devices, body(): whole = lax.all_to_all(whole, 'chan', 0, 0, tiled=True)  6.13 us
    pallas_call x1, Pallas kernels, halves(): pl.pallas_call(halves_kernel, grid=(planes,), in_specs=[pl.BlockSpec((HEL...  5.93 us
    pallas_call x1, Pallas kernels, lend(): pl.pallas_call(lend_kernel, grid=(count // TEAM,), in_specs=[pl.BlockSpec...  4.8 us
    pallas_call x1, Pallas kernels, left_factor(): pl.pallas_call(left_kernel, grid=(TILES,), in_specs=[pl.BlockSpec((1, SHA...  2.65 us
  transfers between devices with their start and end apart: 9, of which 6 were waited for; matrix products, arithmetic and copies ran while one was open for 0% of the time, Pallas kernels for 13%

profile of v2, /device:TPU:20, one launch (start us, length us, event | category | flops | bytes accessed | tf_op | source)
XLA Modules:
  0.0 114.9 jit_solution(8024648834339834909)
XLA Ops:
  0.0 7.6 %prepare.1 = bf16[16,288,256]{2,1,0:T(8,128)(2,1)} custom-call(s32[2,16]{1,0:T(2,128)} %sources_ref.1, s32[256]{0:T(256)} %alive_ref.1, bf16[896,4096]{1,0:T(8,128)(2,1)} %data_ref.3, bf16[256,512]{1,0:T(8,128)(2,1)} %constant.4.clone.table_ref), custom_call_target="tpu_custom_call" | custom-call | tf_op jit(solution)/shard_map/prepare/pallas_call | solution.py:117
  7.6 6.1 %all-to-all-start = ((bf16[16,288,256]{2,1,0:T(8,128)(2,1)}), bf16[16,288,256]{2,1,0:T(8,128)(2,1)S(1)}, u32[]{:S(2)}, u32[]{:S(2)}) async-start(bf16[16,288,256]{2,1,0:T(8,128)(2,1)} %prepare.1), calls=%async_computation | async-start | bytes 4718592 | tf_op jit(solution)/shard_map/all_to_all | solution.py:404
  13.7 4.8 %lend.1 = bf16[8,384,256]{2,1,0:T(8,128)(2,1)} custom-call(bf16[896,4096]{1,0:T(8,128)(2,1)} %data_ref.3), custom_call_target="tpu_custom_call" | custom-call | bytes 1048576 | tf_op jit(solution)/shard_map/lend/pallas_call | solution.py:145
  18.5 0.1 collective-permute-start
  18.7 3.5 %collective-permute-done.lent_ref = bf16[8,384,256]{2,1,0:T(8,128)(2,1)S(1)} collective-permute-done((bf16[8,384,256]{2,1,0:T(8,128)(2,1)}, bf16[8,384,256]{2,1,0:T(8,128)(2,1)S(1)}, u32[]{:S(2)}, u32[]{:S(2)}) %collective-permute-start) | collective-permute-done | bytes 1572896 | tf_op jit(solution)/shard_map/ppermute | solution.py:400
  22.2 1.2 %copy-done.4 = bf16[8,384,256]{2,1,0:T(8,128)(2,1)} copy-done((bf16[8,384,256]{2,1,0:T(8,128)(2,1)}, bf16[8,384,256]{2,1,0:T(8,128)(2,1)S(1)}, u32[]{:S(2)}) %copy-start.4) | copy-done | bytes 1572888
  23.3 5.9 %halves.1 = (bf16[4,512,256]{2,1,0:T(8,128)(2,1)}, bf16[4,512,256]{2,1,0:T(8,128)(2,1)}) custom-call(bf16[896,4096]{1,0:T(8,128)(2,1)} %data_ref.3, bf16[8,384,256]{2,1,0:T(8,128)(2,1)} %copy-done.4, bf16[256,512]{1,0:T(8,128)(2,1)} %constant.4.clone.table_ref), custom_call_target="tpu_custom_call" | custom-call | bytes 1048576 | tf_op jit(solution)/shard_map/halves/pallas_call | solution.py:177
  29.3 0.6 collective-permute-start.1
  29.8 37.6 %collective-permute-done.1.got_ref = bf16[4,512,256]{2,1,0:T(8,128)(2,1)S(1)} collective-permute-done((bf16[4,512,256]{2,1,0:T(8,128)(2,1)}, bf16[4,512,256]{2,1,0:T(8,128)(2,1)S(1)}, u32[]{:S(2)}, u32[]{:S(2)}) %collective-permute-start.1) | collective-permute-done | bytes 1048608 | tf_op jit(solution)/shard_map/ppermute | solution.py:400
  67.4 0.0 copy-done
  67.4 1.2 %copy-done.1 = bf16[4,512,256]{2,1,0:T(8,128)(2,1)S(1)} copy-done((bf16[4,512,256]{2,1,0:T(8,128)(2,1)S(1)}, bf16[4,512,256]{2,1,0:T(8,128)(2,1)}, u32[]{:S(2)}) %copy-start.1) | copy-done | bytes 1048600
  68.7 1.4 %straddle.1 = (bf16[3,256,256]{2,1,0:T(8,128)(2,1)S(1)}, bf16[3,256,256]{2,1,0:T(8,128)(2,1)}, bf16[3,256,256]{2,1,0:T(8,128)(2,1)}, bf16[3,256,256]{2,1,0:T(8,128)(2,1)}) custom-call(bf16[4,512,256]{2,1,0:T(8,128)(2,1)S(1)} %copy-done.1, bf16[4,512,256]{2,1,0:T(8,128)(2,1)S(1)} %collective-permute-done.1.got_ref, bf16[256,512]{1,0:T(8,128)(2,1)S(1)} %copy-done), custom_call_target="tpu_custom_call" | custom-call | bytes 1048576 | tf_op jit(solution)/shard_map/straddle/pallas_call | solution.py:210
  70.1 0.5 collective-permute-start.6
  70.5 1.7 %collective-permute-start.7 = (bf16[3,256,256]{2,1,0:T(8,128)(2,1)}, bf16[3,256,256]{2,1,0:T(8,128)(2,1)}, u32[]{:S(2)}, u32[]{:S(2)}) collective-permute-start(bf16[3,256,256]{2,1,0:T(8,128)(2,1)} %get-tuple-element.22), channel_id=1, source_target_pairs={{0,12},{1,13},{2,14},{3,15},{4,8},{5,9},{6,10},{7,11},{8,4},{9,5},... | collective-permute-start | bytes 1179656 | tf_op jit(solution)/shard_map/ppermute | solution.py:400
  72.2 2.2 %collective-permute-start.5 = (bf16[3,256,256]{2,1,0:T(8,128)(2,1)}, bf16[3,256,256]{2,1,0:T(8,128)(2,1)}, u32[]{:S(2)}, u32[]{:S(2)}) collective-permute-start(bf16[3,256,256]{2,1,0:T(8,128)(2,1)} %get-tuple-element.18), channel_id=1, source_target_pairs={{0,4},{1,5},{2,6},{3,7},{4,0},{5,1},{6,2},{7,3},{8,12},{9,13},{10,... | collective-permute-start | bytes 1179656 | tf_op jit(solution)/shard_map/ppermute | solution.py:400
  74.4 0.0 all-to-all-done.picked_ref.whole_ref
  74.5 0.6 whiten.1.refs_0_
  75.1 0.0 copy-start.2
  75.1 0.0 copy-start.3
  75.1 0.1 collective-permute-start.4
  75.2 1.1 collective-permute-start.3
  76.3 4.5 %collective-permute-done.4.refs_3_ = bf16[16,8,512]{2,1,0:T(8,128)(2,1)S(1)} collective-permute-done((bf16[16,8,512]{2,1,0:T(8,128)(2,1)S(1)}, bf16[16,8,512]{2,1,0:T(8,128)(2,1)S(1)}, u32[]{:S(2)}, u32[]{:S(2)}) %collective-permute-start.4) | collective-permute-done | bytes 131104 | tf_op jit(solution)/shard_map/ppermute | solution.py:400
  80.9 0.0 collective-permute-start.2
  80.9 2.3 %collective-permute-done.3.refs_2_ = bf16[16,8,512]{2,1,0:T(8,128)(2,1)S(1)} collective-permute-done((bf16[16,8,512]{2,1,0:T(8,128)(2,1)S(1)}, bf16[16,8,512]{2,1,0:T(8,128)(2,1)S(1)}, u32[]{:S(2)}, u32[]{:S(2)}) %collective-permute-start.3) | collective-permute-done | bytes 131104 | tf_op jit(solution)/shard_map/ppermute | solution.py:400
  83.1 0.0 collective-permute-done.2.refs_1_
  83.1 2.6 %left.1.left_ref = bf16[16,512,512]{2,1,0:T(8,128)(2,1)S(1)} custom-call(bf16[16,8,512]{2,1,0:T(8,128)(2,1)S(1)} %whiten.1.refs_0_, bf16[16,8,512]{2,1,0:T(8,128)(2,1)S(1)} %collective-permute-done.2.refs_1_, bf16[16,8,512]{2,1,0:T(8,128)(2,1)S(1)} %collective-permute-done.3.refs_2_, bf16[16,8,512]{2,1,0:T(8,128)(2,1)S(1)} %collective-permute-done.4.refs_3_), custom_call_target="tpu_custom_call" | custom-call | bytes 1048576 | tf_op jit(solution)/shard_map/left/pallas_call | solution.py:293
  85.8 11.5 %collective-permute-done.6.refs_2_ = bf16[3,256,256]{2,1,0:T(8,128)(2,1)S(1)} collective-permute-done((bf16[3,256,256]{2,1,0:T(8,128)(2,1)}, bf16[3,256,256]{2,1,0:T(8,128)(2,1)S(1)}, u32[]{:S(2)}, u32[]{:S(2)}) %collective-permute-start.6) | collective-permute-done | bytes 393248 | tf_op jit(solution)/shard_map/ppermute | solution.py:400
  97.3 9.6 %collective-permute-done.7.refs_3_ = bf16[3,256,256]{2,1,0:T(8,128)(2,1)} collective-permute-done((bf16[3,256,256]{2,1,0:T(8,128)(2,1)}, bf16[3,256,256]{2,1,0:T(8,128)(2,1)}, u32[]{:S(2)}, u32[]{:S(2)}) %collective-permute-start.7) | collective-permute-done | bytes 393248 | tf_op jit(solution)/shard_map/ppermute | solution.py:400
  106.9 0.0 collective-permute-done.5.refs_1_
  106.9 0.0 copy-done.2
  106.9 0.0 copy-done.3
  106.9 8.0 %correlate.1 = bf16[32,256,256]{2,1,0:T(8,128)(2,1)} custom-call(bf16[16,512,512]{2,1,0:T(8,128)(2,1)S(1)} %left.1.left_ref, bf16[16,288,256]{2,1,0:T(8,128)(2,1)S(1)} %all-to-all-done.picked_ref.whole_ref, bf16[3,256,256]{2,1,0:T(8,128)(2,1)S(1)} %get-tuple-element.20.refs_0_, bf16[3,256,256]{2,1,0:T(8,128)(2,1)} %collective-permute-done.5.refs_1_, ...), custom_call_target="tpu_custom_call" | custom-call | tf_op jit(solution)/shard_map/correlate/pallas_call | solution.py:371
  (3 shorter events, 0.0 us)
Async XLA Ops:
  7.6 66.8 %all-to-all-start = ((bf16[16,288,256]{2,1,0:T(8,128)(2,1)}), bf16[16,288,256]{2,1,0:T(8,128)(2,1)S(1)}, u32[]{:S(2)}, u32[]{:S(2)}) async-start(bf16[16,288,256]{2,1,0:T(8,128)(2,1)} %prepare.1), calls=%async_computation | async-start | bytes 4718592 | tf_op jit(solution)/shard_map/all_to_all | solution.py:404
  18.5 48.9 %copy-start = (bf16[256,512]{1,0:T(8,128)(2,1)S(1)}, bf16[256,512]{1,0:T(8,128)(2,1)}, u32[]{:S(2)}) copy-start(bf16[256,512]{1,0:T(8,128)(2,1)} %constant.4.clone.table_ref) | copy-start | bytes 786436
  18.5 3.6 %collective-permute-start = (bf16[8,384,256]{2,1,0:T(8,128)(2,1)}, bf16[8,384,256]{2,1,0:T(8,128)(2,1)S(1)}, u32[]{:S(2)}, u32[]{:S(2)}) collective-permute-start(bf16[8,384,256]{2,1,0:T(8,128)(2,1)} %lend.1), channel_id=1, source_target_pairs={{0,1},{1,0},{2,3},{3,2},{4,5},{5,4},{6,7},{7,6},{8,9},{9,8},{10,11... | collective-permute-start | bytes 4718600 | tf_op jit(solution)/shard_map/ppermute | solution.py:400
  22.2 1.2 %copy-start.4 = (bf16[8,384,256]{2,1,0:T(8,128)(2,1)}, bf16[8,384,256]{2,1,0:T(8,128)(2,1)S(1)}, u32[]{:S(2)}) copy-start(bf16[8,384,256]{2,1,0:T(8,128)(2,1)S(1)} %collective-permute-done.lent_ref) | copy-start | bytes 4718596
  29.3 38.1 %collective-permute-start.1 = (bf16[4,512,256]{2,1,0:T(8,128)(2,1)}, bf16[4,512,256]{2,1,0:T(8,128)(2,1)S(1)}, u32[]{:S(2)}, u32[]{:S(2)}) collective-permute-start(bf16[4,512,256]{2,1,0:T(8,128)(2,1)} %get-tuple-element.17), channel_id=1, source_target_pairs={{0,2},{1,3},{2,0},{3,1},{4,6},{5,7},{6,4},{7,5},{8,10},{9,11},{10,... | collective-permute-start | bytes 3145736 | tf_op jit(solution)/shard_map/ppermute | solution.py:400
  67.4 1.2 %copy-start.1 = (bf16[4,512,256]{2,1,0:T(8,128)(2,1)S(1)}, bf16[4,512,256]{2,1,0:T(8,128)(2,1)}, u32[]{:S(2)}) copy-start(bf16[4,512,256]{2,1,0:T(8,128)(2,1)} %get-tuple-element.16.keep_ref) | copy-start | bytes 3145732
  70.1 27.3 %collective-permute-start.6 = (bf16[3,256,256]{2,1,0:T(8,128)(2,1)}, bf16[3,256,256]{2,1,0:T(8,128)(2,1)S(1)}, u32[]{:S(2)}, u32[]{:S(2)}) collective-permute-start(bf16[3,256,256]{2,1,0:T(8,128)(2,1)} %get-tuple-element.21), channel_id=1, source_target_pairs={{0,8},{1,9},{2,10},{3,11},{4,12},{5,13},{6,14},{7,15},{8,0},{9,1},... | collective-permute-start | bytes 1179656 | tf_op jit(solution)/shard_map/ppermute | solution.py:400
  70.5 36.3 %collective-permute-start.7 = (bf16[3,256,256]{2,1,0:T(8,128)(2,1)}, bf16[3,256,256]{2,1,0:T(8,128)(2,1)}, u32[]{:S(2)}, u32[]{:S(2)}) collective-permute-start(bf16[3,256,256]{2,1,0:T(8,128)(2,1)} %get-tuple-element.22), channel_id=1, source_target_pairs={{0,12},{1,13},{2,14},{3,15},{4,8},{5,9},{6,10},{7,11},{8,4},{9,5},... | collective-permute-start | bytes 1179656 | tf_op jit(solution)/shard_map/ppermute | solution.py:400
  72.2 34.7 %collective-permute-start.5 = (bf16[3,256,256]{2,1,0:T(8,128)(2,1)}, bf16[3,256,256]{2,1,0:T(8,128)(2,1)}, u32[]{:S(2)}, u32[]{:S(2)}) collective-permute-start(bf16[3,256,256]{2,1,0:T(8,128)(2,1)} %get-tuple-element.18), channel_id=1, source_target_pairs={{0,4},{1,5},{2,6},{3,7},{4,0},{5,1},{6,2},{7,3},{8,12},{9,13},{10,... | collective-permute-start | bytes 1179656 | tf_op jit(solution)/shard_map/ppermute | solution.py:400
  75.1 31.8 %copy-start.2 = (bf16[256,256]{1,0:T(8,128)(2,1)S(1)}, bf16[256,256]{1,0:T(8,128)(2,1)}, u32[]{:S(2)}) copy-start(bf16[256,256]{1,0:T(8,128)(2,1)} %constant.5.clone.refs_5_) | copy-start | bytes 393220
  75.1 31.8 %copy-start.3 = (s32[256]{0:T(256)S(1)}, s32[256]{0:T(256)}, u32[]{:S(2)}) copy-start(s32[256]{0:T(256)} %alive_ref.1) | copy-start | bytes 3076
  75.1 5.8 %collective-permute-start.4 = (bf16[16,8,512]{2,1,0:T(8,128)(2,1)S(1)}, bf16[16,8,512]{2,1,0:T(8,128)(2,1)S(1)}, u32[]{:S(2)}, u32[]{:S(2)}) collective-permute-start(bf16[16,8,512]{2,1,0:T(8,128)(2,1)S(1)} %whiten.1.refs_0_), channel_id=1, source_target_pairs={{0,3},{1,2},{2,1},{3,0},{4,7},{5,6},{6,5},{7,4},{8,11},{9,10},{10,... | collective-permute-start | bytes 393224 | tf_op jit(solution)/shard_map/ppermute | solution.py:400
  75.2 7.9 %collective-permute-start.3 = (bf16[16,8,512]{2,1,0:T(8,128)(2,1)S(1)}, bf16[16,8,512]{2,1,0:T(8,128)(2,1)S(1)}, u32[]{:S(2)}, u32[]{:S(2)}) collective-permute-start(bf16[16,8,512]{2,1,0:T(8,128)(2,1)S(1)} %whiten.1.refs_0_), channel_id=1, source_target_pairs={{0,2},{1,3},{2,0},{3,1},{4,6},{5,7},{6,4},{7,5},{8,10},{9,11},{10,... | collective-permute-start | bytes 393224 | tf_op jit(solution)/shard_map/ppermute | solution.py:400
  80.9 2.3 %collective-permute-start.2 = (bf16[16,8,512]{2,1,0:T(8,128)(2,1)S(1)}, bf16[16,8,512]{2,1,0:T(8,128)(2,1)S(1)}, u32[]{:S(2)}, u32[]{:S(2)}) collective-permute-start(bf16[16,8,512]{2,1,0:T(8,128)(2,1)S(1)} %whiten.1.refs_0_), channel_id=1, source_target_pairs={{0,1},{1,0},{2,3},{3,2},{4,5},{5,4},{6,7},{7,6},{8,9},{9,8},{10,11... | collective-permute-start | bytes 393224 | tf_op jit(solution)/shard_map/ppermute | solution.py:400

commit v3 on v2

v3 whole, which is shorter than its diff:
```python
import functools
import math

import jax
import jax.numpy as jnp
import ml_dtypes
import numpy as np
from jax import lax
from jax.experimental import pallas as pl
from jax.experimental.pallas import tpu as pltpu
from jax.sharding import PartitionSpec as P

SEGMENT_LENGTH = 512
NF = 128
LAGS = 256
SRC = 16
ROUNDS = 2
SEGMENT_TALLY = 28

SOURCES = SRC * ROUNDS
BINS = 2 * NF
SUB = 8
TILES = NF // SUB
TEAM = 4
TEAM_WINDOWS = 7
STEP = 128
HELD = TEAM_WINDOWS * SEGMENT_LENGTH // TEAM
STRADDLE = HELD - SEGMENT_LENGTH
HALF = SEGMENT_LENGTH // 2
WHOLE = 16
SPLIT = 12
PACKED = 1024
SHARE = SOURCES // TEAM
DEPTH = 512
LARGE = 56 << 20


def angles(times):
    bins = np.arange(NF)[:, None] + 1
    turn = bins * times[None, :] % SEGMENT_LENGTH * (2.0 * np.pi / SEGMENT_LENGTH)
    table = np.stack([np.cos(turn), -np.sin(turn)])
    table = table.reshape(2, TILES, SUB, times.size).transpose(1, 0, 2, 3)
    return table.reshape(BINS, times.size)


def forward_table():
    table = angles(np.arange(SEGMENT_LENGTH)) / math.sqrt(SEGMENT_LENGTH)
    return jnp.asarray(table.astype(ml_dtypes.bfloat16))


def inverse_table():
    table = angles(np.arange(LAGS) - LAGS // 2)
    return jnp.asarray(np.ascontiguousarray(table.T).astype(ml_dtypes.bfloat16))


def position():
    me = lax.axis_index("chan")
    return me // TEAM, me % TEAM


def transform(table_ref, block):
    return jnp.dot(table_ref[...], block, preferred_element_type=jnp.float32).astype(jnp.bfloat16)


def free(size):
    return pl.CostEstimate(flops=0, bytes_accessed=0, transcendentals=0)


def window(data_ref, row, column, depth, width):
    row = pl.ds(pl.multiple_of(row, STEP), depth)
    return data_ref.at[row, pl.ds(pl.multiple_of(column, 128), width)]


def straddling(data_ref, j, place, column, width):
    row = jnp.where(j < place, j, j + SEGMENT_LENGTH // STEP) * STEP
    return window(data_ref, row, column * width, STEP, width)


def prepare_kernel(data_ref, table_ref, out_ref, block_ref, sems):
    _, place = position()
    planes, _, _, width = out_ref.shape
    copies = []
    for plane in range(planes):
        source = window(data_ref, place * STEP, plane * TEAM * width, SEGMENT_LENGTH, TEAM * width)
        copies.append(pltpu.make_async_copy(source, block_ref.at[plane], sems.at[plane]))
        copies[plane].start()
    for plane in range(planes):
        copies[plane].wait()
        for member in range(TEAM):
            column = pl.ds(pl.multiple_of((place ^ member) * width, width), width)
            out_ref[plane, member] = transform(table_ref, block_ref[plane, :, column])


def prepare(data, table, count):
    width = data.shape[1] // count
    planes = count // TEAM
    return pl.pallas_call(
        prepare_kernel,
        in_specs=[pl.BlockSpec(memory_space=pl.ANY), pl.BlockSpec(memory_space=pltpu.VMEM)],
        scratch_shapes=[
            pltpu.VMEM((planes, SEGMENT_LENGTH, TEAM * width), jnp.bfloat16),
            pltpu.SemaphoreType.DMA((planes,)),
        ],
        out_shape=jax.ShapeDtypeStruct((planes, TEAM, BINS, width), jnp.bfloat16),
        compiler_params=pltpu.CompilerParams(vmem_limit_bytes=LARGE),
        name="prepare",
    )(data, table)


def regroup_kernel(whole_ref, *out_refs):
    for member, out_ref in enumerate(out_refs, 1):
        out_ref[...] = whole_ref[:, member]


def regroup(whole):
    planes, _, rows, width = whole.shape
    return pl.pallas_call(
        regroup_kernel,
        out_shape=[jax.ShapeDtypeStruct((planes, rows, width), jnp.bfloat16)] * (TEAM - 1),
        compiler_params=pltpu.CompilerParams(vmem_limit_bytes=16 << 20),
        cost_estimate=free(1 << 20),
        name="regroup",
    )(whole)


def lend_kernel(data_ref, out_ref, sems):
    _, place = position()
    width = out_ref.shape[2]
    copies = []
    for target in range(out_ref.shape[0]):
        column = target // 2 * TEAM + target % 2 * 2 + 1 - place % 2
        for j in range(STRADDLE // STEP):
            source = straddling(data_ref, j, place, column, width)
            copy = pltpu.make_async_copy(source, out_ref.at[target, pl.ds(j * STEP, STEP)], sems.at[target, j])
            copy.start()
            copies.append(copy)
    for copy in copies:
        copy.wait()


def lend(data, count):
    width = data.shape[1] // count
    return pl.pallas_call(
        lend_kernel,
        in_specs=[pl.BlockSpec(memory_space=pl.ANY)],
        scratch_shapes=[pltpu.SemaphoreType.DMA((count // 2, STRADDLE // STEP))],
        out_shape=jax.ShapeDtypeStruct((count // 2, STRADDLE, width), jnp.bfloat16),
        compiler_params=pltpu.CompilerParams(vmem_limit_bytes=LARGE),
        cost_estimate=free(1 << 20),
        name="lend",
    )(data)


def halves_kernel(planes, data_ref, lent_ref, table_ref, keep_ref, give_ref, chip_ref, sems):
    mine, place = position()
    side, core = place // 2, place % 2
    width = keep_ref.shape[2]
    copies = []
    for i, k in enumerate(planes):
        plane = mine ^ k
        for t, target in enumerate((side, 1 - side)):
            for j in range(STRADDLE // STEP):
                source = straddling(data_ref, j, place, plane * TEAM + target * 2 + core, width)
                start = pl.multiple_of(core * STRADDLE + j * STEP, STEP)
                copies.append(pltpu.make_async_copy(source, chip_ref.at[i, t, pl.ds(start, STEP)], sems.at[i, t, j]))
            start = pl.multiple_of((1 - core) * STRADDLE, STEP)
            part = chip_ref.at[i, t, pl.ds(start, STRADDLE)]
            copies.append(pltpu.make_async_copy(lent_ref.at[plane * 2 + target], part, sems.at[i, t, STRADDLE // STEP]))
    for copy in copies:
        copy.start()
    for copy in copies:
        copy.wait()
    for i in range(len(planes)):
        for t, out_ref in enumerate((keep_ref, give_ref)):
            start = pl.multiple_of(side * HALF, HALF)
            out_ref[i, :BINS, :] = transform(table_ref, chip_ref[i, t, pl.ds(start, SEGMENT_LENGTH), :])
            start = pl.multiple_of((1 - side) * SEGMENT_LENGTH, HALF)
            out_ref[i, BINS:, :] = chip_ref[i, t, pl.ds(start, HALF), :]


def halves(planes, data, lent, table, count):
    width = data.shape[1] // count
    shape = jax.ShapeDtypeStruct((len(planes), BINS + HALF, width), jnp.bfloat16)
    return pl.pallas_call(
        functools.partial(halves_kernel, planes),
        in_specs=[
            pl.BlockSpec(memory_space=pl.ANY),
            pl.BlockSpec(memory_space=pl.ANY),
            pl.BlockSpec(memory_space=pltpu.VMEM),
        ],
        scratch_shapes=[
            pltpu.VMEM((len(planes), 2, 2 * STRADDLE, width), jnp.bfloat16),
            pltpu.SemaphoreType.DMA((len(planes), 2, STRADDLE // STEP + 1)),
        ],
        out_shape=[shape, shape],
        compiler_params=pltpu.CompilerParams(vmem_limit_bytes=LARGE),
        cost_estimate=free(1 << 20),
        name="halves",
    )(data, lent, table)


def straddle_kernel(keep_ref, got_ref, table_ref, *refs):
    out_refs, scratch_ref = refs[:-1], refs[-1]
    side = position()[1] // 2
    for k, out_ref in enumerate(out_refs):
        out_ref[2 * side] = keep_ref[k, :BINS, :]
        out_ref[2 - 2 * side] = got_ref[k, :BINS, :]
        scratch_ref[k, pl.ds(pl.multiple_of(side * HALF, HALF), HALF), :] = keep_ref[k, BINS:, :]
        scratch_ref[k, pl.ds(pl.multiple_of((1 - side) * HALF, HALF), HALF), :] = got_ref[k, BINS:, :]
        out_ref[1] = transform(table_ref, scratch_ref[k])


def straddle(keep, got, table):
    planes, _, width = keep.shape
    shape = jax.ShapeDtypeStruct((SPLIT // TEAM, BINS, width), jnp.bfloat16)
    return pl.pallas_call(
        straddle_kernel,
        out_shape=[shape] * planes,
        scratch_shapes=[pltpu.VMEM((planes, SEGMENT_LENGTH, width), jnp.bfloat16)],
        compiler_params=pltpu.CompilerParams(vmem_limit_bytes=16 << 20),
        cost_estimate=free(1 << 20),
        name="straddle",
    )(keep, got, table)


def pick_kernel(width, sources_ref, alive_ref, data_ref, *refs):
    out_refs, acc_ref, picked_ref = refs[:-2], refs[-2], refs[-1]
    step = pl.program_id(0)
    columns = data_ref.shape[1]
    lane = lax.broadcasted_iota(jnp.int32, (1, 128), 1)
    ids = jnp.full((1, 128), -1, jnp.int32)
    for q in range(SOURCES):
        ids = jnp.where(lane == q, sources_ref[q // SRC, q % SRC], ids)
    channel = lax.broadcasted_iota(jnp.int32, (columns, 128), 0)
    chosen = jnp.where(channel == ids - step * columns, 1.0, 0.0).astype(jnp.bfloat16)
    part = jnp.dot(data_ref[...], chosen, preferred_element_type=jnp.float32)

    @pl.when(step == 0)
    def _():
        acc_ref[...] = part

    @pl.when(step > 0)
    def _():
        acc_ref[...] += part

    @pl.when(step == pl.num_programs(0) - 1)
    def _():
        row = lax.broadcasted_iota(jnp.int32, (SOURCES, PACKED - HELD), 0)
        flags = jnp.zeros((SOURCES, PACKED - HELD), jnp.float32)
        for q in range(SOURCES):
            local = sources_ref[q // SRC, q % SRC] - lax.axis_index("chan") * width
            inside = (local >= 0) & (local < width)
            flag = jnp.where(inside, alive_ref[jnp.clip(local, 0, width - 1)], 0)
            flags = jnp.where(row == q, flag.astype(jnp.float32), flags)
        picked_ref[:, :HELD] = acc_ref[...].T[:SOURCES, :]
        picked_ref[:, HELD:] = flags
        for k, out_ref in enumerate(out_refs):
            start = pl.multiple_of((position()[1] ^ k) * SHARE, SHARE)
            out_ref[...] = picked_ref[pl.ds(start, SHARE), :].astype(jnp.bfloat16)


def pick(sources, alive, data, count):
    width = data.shape[1] // count
    columns = TEAM * width
    return pl.pallas_call(
        functools.partial(pick_kernel, width),
        grid=(count // TEAM,),
        in_specs=[
            pl.BlockSpec(memory_space=pltpu.SMEM),
            pl.BlockSpec(memory_space=pltpu.SMEM),
            pl.BlockSpec((HELD, columns), lambda i: (0, i)),
        ],
        out_specs=[pl.BlockSpec((SHARE, PACKED), lambda i: (0, 0))] * TEAM,
        scratch_shapes=[pltpu.VMEM((HELD, 128), jnp.float32), pltpu.VMEM((SOURCES, PACKED), jnp.float32)],
        out_shape=[jax.ShapeDtypeStruct((SHARE, PACKED), jnp.bfloat16)] * TEAM,
        compiler_params=pltpu.CompilerParams(vmem_limit_bytes=LARGE),
        cost_estimate=free(1 << 20),
        name="pick",
    )(sources, alive, data)


def sources_kernel(*refs):
    picked_refs, table_ref, out_ref, samples_ref = refs[:TEAM], refs[TEAM], refs[TEAM + 1], refs[TEAM + 2]
    place = position()[1]
    flags = jnp.zeros((SHARE, PACKED - HELD), jnp.float32)
    for k, picked_ref in enumerate(picked_refs):
        picked = picked_ref[...].astype(jnp.float32)
        flags += picked[:, HELD:]
        samples_ref[:, pl.ds(pl.multiple_of((place ^ k) * HELD, 128), HELD)] = picked[:, :HELD]
    samples = [samples_ref[:, w * SEGMENT_LENGTH : (w + 1) * SEGMENT_LENGTH] for w in range(TEAM_WINDOWS)]
    spectra = lax.dot_general(
        jnp.concatenate(samples, axis=0).astype(jnp.bfloat16),
        table_ref[...],
        (((1,), (1,)), ((), ())),
        preferred_element_type=jnp.float32,
    )
    flags = jnp.concatenate([flags] * (BINS // 128), axis=1)
    out_ref[...] = jnp.concatenate([spectra, flags], axis=0).astype(jnp.bfloat16)


def source_spectra(picked, table):
    return pl.pallas_call(
        sources_kernel,
        scratch_shapes=[pltpu.VMEM((SHARE, TEAM * HELD), jnp.float32)],
        out_shape=jax.ShapeDtypeStruct(((TEAM_WINDOWS + 1) * SHARE, BINS), jnp.bfloat16),
        cost_estimate=free(1 << 18),
        name="source_spectra",
    )(*picked, table)


def whiten_kernel(*refs):
    spectra_refs, out_ref, planes_ref = refs[:TEAM], refs[TEAM], refs[TEAM + 1]
    mine, _ = position()
    flags = jnp.zeros((SHARE, BINS), jnp.float32)
    for k, spectra_ref in enumerate(spectra_refs):
        spectra = spectra_ref[...].astype(jnp.float32)
        flags += spectra[TEAM_WINDOWS * SHARE :]
        planes_ref[mine ^ k] = spectra[: TEAM_WINDOWS * SHARE]
    spectra = planes_ref[...].reshape(SEGMENT_TALLY, SHARE, BINS)
    power = jnp.sum(jnp.square(spectra), axis=0)
    lane = lax.broadcasted_iota(jnp.int32, (SHARE, BINS), 1)
    other = jnp.where(lane % (2 * SUB) < SUB, pltpu.roll(power, BINS - SUB, 1), pltpu.roll(power, SUB, 1))
    level = (power + other) / SEGMENT_TALLY
    factor = flags / jnp.sqrt(level + 0.01)
    src = (spectra * factor[None]).astype(jnp.bfloat16).astype(jnp.float32)
    lane = lax.broadcasted_iota(jnp.int32, (SHARE, 128), 1) // (2 * SUB)
    each = 128 // (2 * SUB)
    for tile in range(TILES):
        half, at = divmod(tile, each)
        for group in range(DEPTH // 128):
            out = jnp.zeros((SHARE, 128), jnp.float32)
            for k in range(each):
                window = group * each + k
                if window < SEGMENT_TALLY:
                    piece = src[window, :, half * 128 : (half + 1) * 128]
                    shift = (k - at) * 2 * SUB % 128
                    piece = pltpu.roll(piece, shift, 1) if shift else piece
                    out = jnp.where(lane == k, piece, out)
            out_ref[tile, :, group * 128 : (group + 1) * 128] = out.astype(jnp.bfloat16)


def whiten(spectra):
    return pl.pallas_call(
        whiten_kernel,
        scratch_shapes=[pltpu.VMEM((TEAM, TEAM_WINDOWS * SHARE, BINS), jnp.float32)],
        out_shape=jax.ShapeDtypeStruct((TILES, SHARE, DEPTH), jnp.bfloat16),
        compiler_params=pltpu.CompilerParams(vmem_limit_bytes=16 << 20),
        cost_estimate=free(1 << 18),
        name="whiten",
    )(*spectra)


def left_kernel(*refs):
    src_refs, left_ref = refs[:-1], refs[-1]
    src = jnp.concatenate([ref[0].astype(jnp.float32) for ref in src_refs], axis=0)
    lane = lax.broadcasted_iota(jnp.int32, (SOURCES, DEPTH), 1)
    turned = jnp.where(lane % (2 * SUB) < SUB, -pltpu.roll(src, DEPTH - SUB, 1), pltpu.roll(src, SUB, 1))
    row = lax.broadcasted_iota(jnp.int32, (1, 2 * SUB, DEPTH), 1)
    lane = lax.broadcasted_iota(jnp.int32, (1, 2 * SUB, DEPTH), 2)
    both = jnp.where(row < SUB, src[:, None, :], turned[:, None, :])
    both = jnp.where(lane % SUB == row % SUB, both, 0.0)
    left_ref[0] = both.reshape(SOURCES * 2 * SUB, DEPTH).astype(jnp.bfloat16)


def left_factor(src):
    return pl.pallas_call(
        left_kernel,
        grid=(TILES,),
        in_specs=[pl.BlockSpec((1, SHARE, DEPTH), lambda i: (i, 0, 0))] * TEAM,
        out_specs=pl.BlockSpec((1, SOURCES * 2 * SUB, DEPTH), lambda i: (i, 0, 0)),
        out_shape=jax.ShapeDtypeStruct((TILES, SOURCES * 2 * SUB, DEPTH), jnp.bfloat16),
        compiler_params=pltpu.CompilerParams(vmem_limit_bytes=16 << 20),
        cost_estimate=pl.CostEstimate(flops=0, bytes_accessed=1 << 20, transcendentals=0),
        name="left",
    )(*src)


def whiten_all(samples, alive, table):
    samples = samples.reshape(SOURCES, SEGMENT_TALLY, SEGMENT_LENGTH)
    spectra = jnp.einsum("qwt,kt->qwk", samples, table, preferred_element_type=jnp.float32)
    power = jnp.mean(spectra**2, axis=1).reshape(SOURCES, TILES, 2, SUB)
    level = power[:, :, :1] + power[:, :, 1:]
    factor = alive[:, None, None, None] / jnp.sqrt(level + 0.01)
    factor = jnp.broadcast_to(factor, (SOURCES, TILES, 2, SUB)).reshape(SOURCES, BINS)
    src = (spectra * factor[:, None, :]).astype(jnp.bfloat16)
    src = jnp.transpose(src.reshape(SOURCES, SEGMENT_TALLY, TILES, 2 * SUB), (2, 0, 1, 3))
    src = src.reshape(TILES, SOURCES, SEGMENT_TALLY * 2 * SUB)
    src = jnp.pad(src, ((0, 0), (0, 0), (0, DEPTH - SEGMENT_TALLY * 2 * SUB)))
    return [src[:, k * SHARE : (k + 1) * SHARE] for k in range(TEAM)]


BATCH = 4


def correlate_kernel(relative, left_ref, whole_ref, *refs):
    other_refs, split_refs = refs[: TEAM - 1], refs[TEAM - 1 : 2 * TEAM - 1]
    alive_ref, inverse_ref, out_ref, right_ref, cross_ref, done_ref, sems = refs[2 * TEAM - 1 :]
    mine, place = position() if relative else (0, 0)
    width = right_ref.shape[2]
    rows = 2 * SUB
    span = TEAM_WINDOWS * rows
    pad = DEPTH - SEGMENT_TALLY * rows
    alive = alive_ref[...].astype(jnp.float32)

    @pl.loop(0, TILES // BATCH)
    def _(step):
        for k in range(BATCH):
            index = step * BATCH + k
            start = pl.multiple_of(index * rows, rows)
            tile = pl.ds(start, rows)
            right_ref[index, DEPTH - pad :, :] = jnp.zeros((pad, width), jnp.bfloat16)
            for plane in range(TEAM):
                for member in range(TEAM):
                    at = pl.multiple_of(plane * span + (member ^ place) * 2 * rows, rows)
                    piece = other_refs[member - 1][plane, tile, :] if member else whole_ref[plane, 0, tile, :]
                    right_ref[index, pl.ds(at, rows), :] = piece
                for j in range(SPLIT // TEAM):
                    at = pl.multiple_of((plane ^ mine) * span + (2 * j + 1) * rows, rows)
                    right_ref[index, pl.ds(at, rows), :] = split_refs[plane][j, tile, :]
            right = right_ref[index]
            power = jnp.square(right.astype(jnp.float32)).reshape(DEPTH // rows, rows, width)
            power = jnp.sum(power, axis=0)
            level = (power[:SUB] + power[SUB:]) / SEGMENT_TALLY
            factor = alive / jnp.sqrt(level + 0.01)
            factor = jnp.concatenate([factor, factor], axis=0)[None]
            cross = jnp.dot(left_ref[index], right, preferred_element_type=jnp.float32)
            cross = cross.reshape(SOURCES, rows, width)
            cross_ref[:, tile, :] = jnp.where(factor > 0.0, cross * factor, 0.0).astype(jnp.bfloat16)

    def copy(step):
        part = pl.ds(step * BATCH, BATCH)
        return pltpu.make_async_copy(done_ref.at[part], out_ref.at[part], sems.at[step])

    @pl.loop(0, SOURCES // BATCH)
    def _(step):
        for k in range(BATCH):
            index = step * BATCH + k
            held = (index // SHARE ^ place) * SHARE + index % SHARE
            lagged = jnp.dot(inverse_ref[...], cross_ref[held], preferred_element_type=jnp.float32)
            done_ref[index] = (lagged * (1.0 / math.sqrt(NF * SEGMENT_TALLY))).astype(jnp.bfloat16)
        copy(step).start()

    @pl.loop(0, SOURCES // BATCH)
    def _(step):
        copy(step).wait()


def correlate(relative, left, whole, others, split, alive, inverse):
    width = whole.shape[3]
    return pl.pallas_call(
        functools.partial(correlate_kernel, relative),
        out_specs=pl.BlockSpec(memory_space=pl.ANY),
        scratch_shapes=[
            pltpu.VMEM((TILES, DEPTH, width), jnp.bfloat16),
            pltpu.VMEM((SOURCES, BINS, width), jnp.bfloat16),
            pltpu.VMEM((SOURCES, LAGS, width), jnp.bfloat16),
            pltpu.SemaphoreType.DMA((SOURCES // BATCH,)),
        ],
        out_shape=jax.ShapeDtypeStruct((SOURCES, LAGS, width), jnp.bfloat16),
        compiler_params=pltpu.CompilerParams(vmem_limit_bytes=18 << 20),
        name="correlate",
    )(left, whole, *others, *split, alive, inverse)


def body(data, alive, sources):
    count = lax.axis_size("chan")
    width = data.shape[1] // count
    table = forward_table()
    relative = data.shape[0] == HELD and count == TEAM * TEAM
    if relative:
        swap = lambda x, k: lax.ppermute(x, "chan", [(i, i ^ k) for i in range(count)])
        team = range(1, TEAM)
        across = [[z * TEAM + p for z in range(count // TEAM)] for p in range(TEAM)]
        whole = prepare(data, table, count)
        data, whole = lax.optimization_barrier((data, whole))
        lent = lend(data, count)
        data, lent = lax.optimization_barrier((data, lent))
        lent = swap(lent, 1)
        whole = lax.all_to_all(whole, "chan", 0, 0, tiled=True, axis_index_groups=across)
        picked = pick(sources, alive, data, count)
        data, picked = lax.optimization_barrier((data, picked))
        picked = [picked[0]] + [swap(picked[k], k) for k in team]
        spectra = source_spectra(picked, table)
        keep_far, give_far = halves((2, 3), data, lent, table, count)
        give_far, spectra, data = lax.optimization_barrier((give_far, spectra, data))
        arrived = [swap(spectra, k * TEAM) for k in team]
        keep_near, give_near = halves((0, 1), data, lent, table, count)
        far = straddle(keep_far, swap(give_far, 2), table)
        arrived, whole, far = lax.optimization_barrier((arrived, whole, far))
        others = regroup(whole)
        src = whiten([spectra] + arrived)
        keep_near, src, others = lax.optimization_barrier((keep_near, src, others))
        others = [swap(others[k - 1], k) for k in team]
        near = straddle(keep_near, swap(give_near, 2), table)
        split = [near[0], swap(near[1], TEAM), swap(far[0], 2 * TEAM), swap(far[1], 3 * TEAM)]
        src = [src] + [swap(src, k) for k in team]
    else:
        me = lax.axis_index("chan")
        ids = sources.reshape(-1)
        near = ids[:, None] == me * width + jnp.arange(width, dtype=jnp.int32)[None, :]
        flags = jnp.sum(jnp.where(near, alive[None, :], 0), axis=1).astype(jnp.float32)
        chosen = jnp.where(jnp.arange(data.shape[1], dtype=jnp.int32)[:, None] == ids[None, :], 1.0, 0.0)
        picked = jnp.dot(data, chosen.astype(jnp.bfloat16), preferred_element_type=jnp.float32)
        picked = lax.all_gather(picked.astype(jnp.bfloat16), "chan", axis=0)
        alive_sources = lax.psum(flags, "chan")
        blocks = data.reshape(data.shape[0], count, width)
        blocks = lax.all_to_all(blocks, "chan", split_axis=1, concat_axis=0, tiled=True)
        blocks = blocks.reshape(SEGMENT_TALLY, SEGMENT_LENGTH, width)
        spectra = jnp.einsum("kt,wtc->wkc", table, blocks, preferred_element_type=jnp.float32)
        spectra = spectra.astype(jnp.bfloat16).reshape(TEAM, TEAM_WINDOWS, BINS, width)
        whole = spectra[:, 0:1]
        others = [spectra[:, 2 * k] for k in range(1, TEAM)]
        split = [spectra[z, 1::2] for z in range(TEAM)]
        src = whiten_all(jnp.transpose(picked, (2, 0, 1)), alive_sources, table)
    left = left_factor(src)
    out = correlate(relative, left, whole, others, split, alive[None, :], inverse_table())
    return out.reshape(ROUNDS, SRC, LAGS, width)


def solution(mesh):
    return jax.shard_map(
        body,
        mesh=mesh,
        in_specs=(P(("groups", "chan"), None), P(("groups", "chan")), P()),
        out_specs=P("groups", None, None, "chan"),
        check_vma=False,
    )
```

time: 115 us -> 108 us (0.939)
  the two profiles are of different devices: /device:TPU:20 before, /device:TPU:0 now
where the time goes in v3:
time: 108 us
  waiting for transfers between devices  49.1 us (45%)
  Pallas kernels  34.7 us (32%)
  starting transfers between devices  21.5 us (20%)
  local copies, waits for them, and re-layouts  2.12 us (2%)
    ppermute x18, waiting for transfers between devices, body(): lax.ppermute(x, 'chan', [(i, i ^ k) for i in range(count)])  49.1 us
    ppermute x18, starting transfers between devices, body(): lax.ppermute(x, 'chan', [(i, i ^ k) for i in range(count)])  15.2 us
    pallas_call x2, Pallas kernels, halves(): pl.pallas_call(functools.partial(halves_kernel, planes), in_specs=[pl.Blo...  7.95 us
    pallas_call x1, Pallas kernels, correlate(): pl.pallas_call(functools.partial(correlate_kernel, relative), out_specs=p...  6.74 us
    all_to_all x1, starting transfers between devices, body(): lax.all_to_all(whole, 'chan', 0, 0, tiled=True, axis_index_groups=across)  6.34 us
    pallas_call x1, Pallas kernels, pick(): pl.pallas_call(functools.partial(pick_kernel, width), grid=(count // TEAM...  6.12 us
    pallas_call x1, Pallas kernels, prepare(): pl.pallas_call(prepare_kernel, in_specs=[pl.BlockSpec(memory_space=pl.ANY...  5.32 us
    pallas_call x1, Pallas kernels, lend(): pl.pallas_call(lend_kernel, in_specs=[pl.BlockSpec(memory_space=pl.ANY)],...  2.78 us
  transfers between devices with their start and end apart: 19, of which 9 were waited for; matrix products, arithmetic and copies ran while one was open for 0% of the time, Pallas kernels for 21%

profile of v3, /device:TPU:0, one launch (start us, length us, event | category | flops | bytes accessed | tf_op | source)
XLA Modules:
  0.0 107.6 jit_solution(11898991547839872439)
XLA Ops:
  0.0 5.3 %prepare.1 = bf16[4,4,256,256]{3,2,1,0:T(8,128)(2,1)} custom-call(bf16[896,4096]{1,0:T(8,128)(2,1)} %data_ref.5, bf16[256,512]{1,0:T(8,128)(2,1)} %constant.4.clone.table_ref.refs_4_), custom_call_target="tpu_custom_call" | custom-call | tf_op jit(solution)/shard_map/prepare/pallas_call | solution.py:97
  5.3 6.3 %all-to-all-start = ((bf16[4,4,256,256]{3,2,1,0:T(8,128)(2,1)}), bf16[4,4,256,256]{3,2,1,0:T(8,128)(2,1)S(1)}, u32[]{:S(2)}, u32[]{:S(2)}) async-start(bf16[4,4,256,256]{3,2,1,0:T(8,128)(2,1)} %prepare.1), calls=%async_computation | async-start | bytes 4194304 | tf_op jit(solution)/shard_map/all_to_all | solution.py:479
  11.7 2.8 %lend.1 = bf16[8,384,256]{2,1,0:T(8,128)(2,1)} custom-call(bf16[896,4096]{1,0:T(8,128)(2,1)} %data_ref.5), custom_call_target="tpu_custom_call" | custom-call | tf_op jit(solution)/shard_map/lend/pallas_call | solution.py:143
  14.5 6.1 %pick.1 = (bf16[8,1024]{1,0:T(8,128)(2,1)}, bf16[8,1024]{1,0:T(8,128)(2,1)}, bf16[8,1024]{1,0:T(8,128)(2,1)}, bf16[8,1024]{1,0:T(8,128)(2,1)}) custom-call(s32[2,16]{1,0:T(2,128)} %sources_ref.1, s32[256]{0:T(256)} %alive_ref.1, bf16[896,4096]{1,0:T(8,128)(2,1)} %data_ref.5), custom_call_target="tpu_custom_call" | custom-call | tf_op jit(solution)/shard_map/pick/pallas_call | solution.py:265
  20.7 0.5 collective-permute-start.1
  21.2 1.5 %collective-permute-start.2 = (bf16[8,1024]{1,0:T(8,128)(2,1)}, bf16[8,1024]{1,0:T(8,128)(2,1)S(1)}, u32[]{:S(2)}, u32[]{:S(2)}) collective-permute-start(bf16[8,1024]{1,0:T(8,128)(2,1)} %get-tuple-element.54), channel_id=1, source_target_pairs={{0,2},{1,3},{2,0},{3,1},{4,6},{5,7},{6,4},{7,5},{8,10},{9,11},{10,... | collective-permute-start | bytes 49160 | tf_op jit(solution)/shard_map/ppermute | solution.py:471
  22.7 2.4 %collective-permute-done.2.refs_2_ = bf16[8,1024]{1,0:T(8,128)(2,1)S(1)} collective-permute-done((bf16[8,1024]{1,0:T(8,128)(2,1)}, bf16[8,1024]{1,0:T(8,128)(2,1)S(1)}, u32[]{:S(2)}, u32[]{:S(2)}) %collective-permute-start.2) | collective-permute-done | bytes 16416 | tf_op jit(solution)/shard_map/ppermute | solution.py:471
  25.1 1.1 %collective-permute-done.3.refs_3_ = bf16[8,1024]{1,0:T(8,128)(2,1)S(1)} collective-permute-done((bf16[8,1024]{1,0:T(8,128)(2,1)}, bf16[8,1024]{1,0:T(8,128)(2,1)S(1)}, u32[]{:S(2)}, u32[]{:S(2)}) %collective-permute-start.3) | collective-permute-done | bytes 16416 | tf_op jit(solution)/shard_map/ppermute | solution.py:471
  26.2 0.6 copy-done.11
  26.8 1.8 %source_spectra.1.refs_0_ = bf16[64,256]{1,0:T(8,128)(2,1)} custom-call(bf16[8,1024]{1,0:T(8,128)(2,1)} %get-tuple-element.52.refs_0_, bf16[8,1024]{1,0:T(8,128)(2,1)} %copy-done.9, bf16[8,1024]{1,0:T(8,128)(2,1)} %copy-done.10, bf16[8,1024]{1,0:T(8,128)(2,1)} %copy-done.11, bf16[256,512]{1,0:T(8,128)(2,1)} %constant.4.clone.table_ref.refs_4_), custom_call_target="tpu_custom_call" | custom-call | tf_op jit(solution)/shard_map/source_spectra/pallas_call | solution.py:302
  28.6 4.0 %halves.2 = (bf16[2,512,256]{2,1,0:T(8,128)(2,1)}, bf16[2,512,256]{2,1,0:T(8,128)(2,1)}) custom-call(bf16[896,4096]{1,0:T(8,128)(2,1)} %data_ref.5, bf16[8,384,256]{2,1,0:T(8,128)(2,1)} %collective-permute-done.lent_ref, bf16[256,512]{1,0:T(8,128)(2,1)} %constant.4.clone.table_ref.refs_4_), custom_call_target="tpu_custom_call" | custom-call | tf_op jit(solution)/shard_map/halves/pallas_call | solution.py:184
  32.6 1.2 %collective-permute-start.7 = (bf16[2,512,256]{2,1,0:T(8,128)(2,1)}, bf16[2,512,256]{2,1,0:T(8,128)(2,1)S(1)}, u32[]{:S(2)}, u32[]{:S(2)}) collective-permute-start(bf16[2,512,256]{2,1,0:T(8,128)(2,1)} %get-tuple-element.61), channel_id=1, source_target_pairs={{0,2},{1,3},{2,0},{3,1},{4,6},{5,7},{6,4},{7,5},{8,10},{9,11},{10,... | collective-permute-start | bytes 1572872 | tf_op jit(solution)/shard_map/ppermute | solution.py:471
  33.8 4.0 %halves.3 = (bf16[2,512,256]{2,1,0:T(8,128)(2,1)}, bf16[2,512,256]{2,1,0:T(8,128)(2,1)}) custom-call(bf16[896,4096]{1,0:T(8,128)(2,1)} %data_ref.5, bf16[8,384,256]{2,1,0:T(8,128)(2,1)} %collective-permute-done.lent_ref, bf16[256,512]{1,0:T(8,128)(2,1)} %constant.4.clone.table_ref.refs_4_), custom_call_target="tpu_custom_call" | custom-call | tf_op jit(solution)/shard_map/halves/pallas_call | solution.py:184
  37.8 1.0 collective-permute-start.14
  38.8 3.8 %collective-permute-start.6 = (bf16[64,256]{1,0:T(8,128)(2,1)S(1)}, bf16[64,256]{1,0:T(8,128)(2,1)S(1)}, u32[]{:S(2)}, u32[]{:S(2)}) collective-permute-start(bf16[64,256]{1,0:T(8,128)(2,1)S(1)} %copy-done.4), channel_id=1, source_target_pairs={{0,12},{1,13},{2,14},{3,15},{4,8},{5,9},{6,10},{7,11},{8,4},{9,5},... | collective-permute-start | bytes 98312 | tf_op jit(solution)/shard_map/ppermute | solution.py:471
  42.6 0.6 collective-permute-start.4
  43.2 4.5 %collective-permute-done.7.got_ref = bf16[2,512,256]{2,1,0:T(8,128)(2,1)S(1)} collective-permute-done((bf16[2,512,256]{2,1,0:T(8,128)(2,1)}, bf16[2,512,256]{2,1,0:T(8,128)(2,1)S(1)}, u32[]{:S(2)}, u32[]{:S(2)}) %collective-permute-start.7) | collective-permute-done | bytes 524320 | tf_op jit(solution)/shard_map/ppermute | solution.py:471
  47.7 0.4 straddle.2
  48.1 0.7 copy-done.6
  48.8 0.7 copy-done.8
  49.6 1.4 %collective-permute-done.6.refs_3_ = bf16[64,256]{1,0:T(8,128)(2,1)S(1)} collective-permute-done((bf16[64,256]{1,0:T(8,128)(2,1)S(1)}, bf16[64,256]{1,0:T(8,128)(2,1)S(1)}, u32[]{:S(2)}, u32[]{:S(2)}) %collective-permute-start.6) | collective-permute-done | bytes 32800 | tf_op jit(solution)/shard_map/ppermute | solution.py:471
  51.0 11.7 %collective-permute-done.5.refs_2_ = bf16[64,256]{1,0:T(8,128)(2,1)S(1)} collective-permute-done((bf16[64,256]{1,0:T(8,128)(2,1)S(1)}, bf16[64,256]{1,0:T(8,128)(2,1)S(1)}, u32[]{:S(2)}, u32[]{:S(2)}) %collective-permute-start.5) | collective-permute-done | bytes 32800 | tf_op jit(solution)/shard_map/ppermute | solution.py:471
  63.1 0.4 whiten.1.refs_0_
  63.6 1.6 %collective-permute-start.9 = (bf16[16,8,512]{2,1,0:T(8,128)(2,1)S(1)}, bf16[16,8,512]{2,1,0:T(8,128)(2,1)S(1)}, u32[]{:S(2)}, u32[]{:S(2)}) collective-permute-start(bf16[16,8,512]{2,1,0:T(8,128)(2,1)S(1)} %whiten.1.refs_0_), channel_id=1, source_target_pairs={{0,2},{1,3},{2,0},{3,1},{4,6},{5,7},{6,4},{7,5},{8,10},{9,11},{10,... | collective-permute-start | bytes 393224 | tf_op jit(solution)/shard_map/ppermute | solution.py:471
  65.7 3.6 %collective-permute-done.10.refs_3_ = bf16[16,8,512]{2,1,0:T(8,128)(2,1)S(1)} collective-permute-done((bf16[16,8,512]{2,1,0:T(8,128)(2,1)S(1)}, bf16[16,8,512]{2,1,0:T(8,128)(2,1)S(1)}, u32[]{:S(2)}, u32[]{:S(2)}) %collective-permute-start.10) | collective-permute-done | bytes 131104 | tf_op jit(solution)/shard_map/ppermute | solution.py:471
  69.3 1.6 %collective-permute-start.12 = (bf16[4,256,256]{2,1,0:T(8,128)(2,1)S(1)}, bf16[4,256,256]{2,1,0:T(8,128)(2,1)S(1)}, u32[]{:S(2)}, u32[]{:S(2)}) collective-permute-start(bf16[4,256,256]{2,1,0:T(8,128)(2,1)S(1)} %get-tuple-element.73), channel_id=1, source_target_pairs={{0,2},{1,3},{2,0},{3,1},{4,6},{5,7},{6,4},{7,5},{8,10},{9,11},{10,... | collective-permute-start | bytes 1572872 | tf_op jit(solution)/shard_map/ppermute | solution.py:471
  70.9 1.4 %collective-permute-done.9.refs_2_ = bf16[16,8,512]{2,1,0:T(8,128)(2,1)S(1)} collective-permute-done((bf16[16,8,512]{2,1,0:T(8,128)(2,1)S(1)}, bf16[16,8,512]{2,1,0:T(8,128)(2,1)S(1)}, u32[]{:S(2)}, u32[]{:S(2)}) %collective-permute-start.9) | collective-permute-done | bytes 131104 | tf_op jit(solution)/shard_map/ppermute | solution.py:471
  72.7 2.4 %collective-permute-start.17 = (bf16[3,256,256]{2,1,0:T(8,128)(2,1)S(1)}, bf16[3,256,256]{2,1,0:T(8,128)(2,1)S(1)}, u32[]{:S(2)}, u32[]{:S(2)}) collective-permute-start(bf16[3,256,256]{2,1,0:T(8,128)(2,1)S(1)} %copy-done.7), channel_id=1, source_target_pairs={{0,12},{1,13},{2,14},{3,15},{4,8},{5,9},{6,10},{7,11},{8,4},{9,5},... | collective-permute-start | bytes 1179656 | tf_op jit(solution)/shard_map/ppermute | solution.py:471
  75.1 14.8 %collective-permute-done.16.refs_5_ = bf16[3,256,256]{2,1,0:T(8,128)(2,1)S(1)} collective-permute-done((bf16[3,256,256]{2,1,0:T(8,128)(2,1)}, bf16[3,256,256]{2,1,0:T(8,128)(2,1)S(1)}, u32[]{:S(2)}, u32[]{:S(2)}) %collective-permute-start.16) | collective-permute-done | bytes 393248 | tf_op jit(solution)/shard_map/ppermute | solution.py:471
  89.9 2.7 %left.1.left_ref = bf16[16,512,512]{2,1,0:T(8,128)(2,1)S(1)} custom-call(bf16[16,8,512]{2,1,0:T(8,128)(2,1)S(1)} %whiten.1.refs_0_, bf16[16,8,512]{2,1,0:T(8,128)(2,1)S(1)} %collective-permute-done.8.refs_1_, bf16[16,8,512]{2,1,0:T(8,128)(2,1)S(1)} %collective-permute-done.9.refs_2_, bf16[16,8,512]{2,1,0:T(8,128)(2,1)S(1)} %collective-permute-done.10.refs_3_), custom_call_target="tpu_custom_call" | custom-call | bytes 1048576 | tf_op jit(solution)/shard_map/left/pallas_call | solution.py:366
  92.6 8.3 %collective-permute-done.15.refs_4_ = bf16[3,256,256]{2,1,0:T(8,128)(2,1)S(1)} collective-permute-done((bf16[3,256,256]{2,1,0:T(8,128)(2,1)S(1)}, bf16[3,256,256]{2,1,0:T(8,128)(2,1)S(1)}, u32[]{:S(2)}, u32[]{:S(2)}) %collective-permute-start.15) | collective-permute-done | bytes 393248 | tf_op jit(solution)/shard_map/ppermute | solution.py:471
  100.9 6.7 %correlate.1 = bf16[32,256,256]{2,1,0:T(8,128)(2,1)} custom-call(bf16[16,512,512]{2,1,0:T(8,128)(2,1)S(1)} %left.1.left_ref, bf16[4,4,256,256]{3,2,1,0:T(8,128)(2,1)S(1)} %all-to-all-done.whole_ref, bf16[4,256,256]{2,1,0:T(8,128)(2,1)S(1)} %collective-permute-done.11.refs_0_, bf16[4,256,256]{2,1,0:T(8,128)(2,1)S(1)} %collective-permute-done.12.refs_1_, ...), custom_call_target="tpu_custom_call" | custom-call | tf_op jit(solution)/shard_map/correlate/pallas_call | solution.py:450
  (42 shorter events, 1.5 us)
Async XLA Ops:
  5.3 57.3 %all-to-all-start = ((bf16[4,4,256,256]{3,2,1,0:T(8,128)(2,1)}), bf16[4,4,256,256]{3,2,1,0:T(8,128)(2,1)S(1)}, u32[]{:S(2)}, u32[]{:S(2)}) async-start(bf16[4,4,256,256]{3,2,1,0:T(8,128)(2,1)} %prepare.1), calls=%async_computation | async-start | bytes 4194304 | tf_op jit(solution)/shard_map/all_to_all | solution.py:479
  14.5 14.1 %collective-permute-start = (bf16[8,384,256]{2,1,0:T(8,128)(2,1)}, bf16[8,384,256]{2,1,0:T(8,128)(2,1)}, u32[]{:S(2)}, u32[]{:S(2)}) collective-permute-start(bf16[8,384,256]{2,1,0:T(8,128)(2,1)} %lend.1), channel_id=1, source_target_pairs={{0,1},{1,0},{2,3},{3,2},{4,5},{5,4},{6,7},{7,6},{8,9},{9,8},{10,11... | collective-permute-start | bytes 4718600 | tf_op jit(solution)/shard_map/ppermute | solution.py:471
  20.7 2.0 %collective-permute-start.1 = (bf16[8,1024]{1,0:T(8,128)(2,1)}, bf16[8,1024]{1,0:T(8,128)(2,1)S(1)}, u32[]{:S(2)}, u32[]{:S(2)}) collective-permute-start(bf16[8,1024]{1,0:T(8,128)(2,1)} %get-tuple-element.53), channel_id=1, source_target_pairs={{0,1},{1,0},{2,3},{3,2},{4,5},{5,4},{6,7},{7,6},{8,9},{9,8},{10,11... | collective-permute-start | bytes 49160 | tf_op jit(solution)/shard_map/ppermute | solution.py:471
  21.2 3.9 %collective-permute-start.2 = (bf16[8,1024]{1,0:T(8,128)(2,1)}, bf16[8,1024]{1,0:T(8,128)(2,1)S(1)}, u32[]{:S(2)}, u32[]{:S(2)}) collective-permute-start(bf16[8,1024]{1,0:T(8,128)(2,1)} %get-tuple-element.54), channel_id=1, source_target_pairs={{0,2},{1,3},{2,0},{3,1},{4,6},{5,7},{6,4},{7,5},{8,10},{9,11},{10,... | collective-permute-start | bytes 49160 | tf_op jit(solution)/shard_map/ppermute | solution.py:471
  22.7 3.5 %collective-permute-start.3 = (bf16[8,1024]{1,0:T(8,128)(2,1)}, bf16[8,1024]{1,0:T(8,128)(2,1)S(1)}, u32[]{:S(2)}, u32[]{:S(2)}) collective-permute-start(bf16[8,1024]{1,0:T(8,128)(2,1)} %get-tuple-element.55), channel_id=1, source_target_pairs={{0,3},{1,2},{2,1},{3,0},{4,7},{5,6},{6,5},{7,4},{8,11},{9,10},{10,... | collective-permute-start | bytes 49160 | tf_op jit(solution)/shard_map/ppermute | solution.py:471
  22.7 3.5 %copy-start.9 = (bf16[8,1024]{1,0:T(8,128)(2,1)}, bf16[8,1024]{1,0:T(8,128)(2,1)S(1)}, u32[]{:S(2)}) copy-start(bf16[8,1024]{1,0:T(8,128)(2,1)S(1)} %collective-permute-done.1.refs_1_) | copy-start | bytes 49156
  25.1 1.1 %copy-start.10 = (bf16[8,1024]{1,0:T(8,128)(2,1)}, bf16[8,1024]{1,0:T(8,128)(2,1)S(1)}, u32[]{:S(2)}) copy-start(bf16[8,1024]{1,0:T(8,128)(2,1)S(1)} %collective-permute-done.2.refs_2_) | copy-start | bytes 49156
  26.2 0.6 copy-start.11
  32.6 6.2 %copy-start.4 = (bf16[64,256]{1,0:T(8,128)(2,1)S(1)}, bf16[64,256]{1,0:T(8,128)(2,1)}, u32[]{:S(2)}) copy-start(bf16[64,256]{1,0:T(8,128)(2,1)} %source_spectra.1.refs_0_) | copy-start | bytes 98308
  32.6 15.1 %copy-start = (bf16[256,512]{1,0:T(8,128)(2,1)S(1)}, bf16[256,512]{1,0:T(8,128)(2,1)}, u32[]{:S(2)}) copy-start(bf16[256,512]{1,0:T(8,128)(2,1)} %constant.4.clone.table_ref.refs_4_) | copy-start | bytes 786436
  32.6 15.1 %copy-start.2 = (bf16[2,512,256]{2,1,0:T(8,128)(2,1)S(1)}, bf16[2,512,256]{2,1,0:T(8,128)(2,1)}, u32[]{:S(2)}) copy-start(bf16[2,512,256]{2,1,0:T(8,128)(2,1)} %get-tuple-element.60.keep_ref) | copy-start | bytes 1572868
  32.6 15.1 %collective-permute-start.7 = (bf16[2,512,256]{2,1,0:T(8,128)(2,1)}, bf16[2,512,256]{2,1,0:T(8,128)(2,1)S(1)}, u32[]{:S(2)}, u32[]{:S(2)}) collective-permute-start(bf16[2,512,256]{2,1,0:T(8,128)(2,1)} %get-tuple-element.61), channel_id=1, source_target_pairs={{0,2},{1,3},{2,0},{3,1},{4,6},{5,7},{6,4},{7,5},{8,10},{9,11},{10,... | collective-permute-start | bytes 1572872 | tf_op jit(solution)/shard_map/ppermute | solution.py:471
  37.8 34.5 %copy-start.1 = (bf16[2,512,256]{2,1,0:T(8,128)(2,1)S(1)}, bf16[2,512,256]{2,1,0:T(8,128)(2,1)}, u32[]{:S(2)}) copy-start(bf16[2,512,256]{2,1,0:T(8,128)(2,1)} %get-tuple-element.75.keep_ref) | copy-start | bytes 1572868
  37.8 27.6 %collective-permute-start.14 = (bf16[2,512,256]{2,1,0:T(8,128)(2,1)}, bf16[2,512,256]{2,1,0:T(8,128)(2,1)S(1)}, u32[]{:S(2)}, u32[]{:S(2)}) collective-permute-start(bf16[2,512,256]{2,1,0:T(8,128)(2,1)} %get-tuple-element.76), channel_id=1, source_target_pairs={{0,2},{1,3},{2,0},{3,1},{4,6},{5,7},{6,4},{7,5},{8,10},{9,11},{10,... | collective-permute-start | bytes 1572872 | tf_op jit(solution)/shard_map/ppermute | solution.py:471
  38.8 12.2 %collective-permute-start.6 = (bf16[64,256]{1,0:T(8,128)(2,1)S(1)}, bf16[64,256]{1,0:T(8,128)(2,1)S(1)}, u32[]{:S(2)}, u32[]{:S(2)}) collective-permute-start(bf16[64,256]{1,0:T(8,128)(2,1)S(1)} %copy-done.4), channel_id=1, source_target_pairs={{0,12},{1,13},{2,14},{3,15},{4,8},{5,9},{6,10},{7,11},{8,4},{9,5},... | collective-permute-start | bytes 98312 | tf_op jit(solution)/shard_map/ppermute | solution.py:471
  42.6 20.1 %collective-permute-start.5 = (bf16[64,256]{1,0:T(8,128)(2,1)S(1)}, bf16[64,256]{1,0:T(8,128)(2,1)S(1)}, u32[]{:S(2)}, u32[]{:S(2)}) collective-permute-start(bf16[64,256]{1,0:T(8,128)(2,1)S(1)} %copy-done.4), channel_id=1, source_target_pairs={{0,8},{1,9},{2,10},{3,11},{4,12},{5,13},{6,14},{7,15},{8,0},{9,1},... | collective-permute-start | bytes 98312 | tf_op jit(solution)/shard_map/ppermute | solution.py:471
  42.6 20.1 %collective-permute-start.4 = (bf16[64,256]{1,0:T(8,128)(2,1)S(1)}, bf16[64,256]{1,0:T(8,128)(2,1)S(1)}, u32[]{:S(2)}, u32[]{:S(2)}) collective-permute-start(bf16[64,256]{1,0:T(8,128)(2,1)S(1)} %copy-done.4), channel_id=1, source_target_pairs={{0,4},{1,5},{2,6},{3,7},{4,0},{5,1},{6,2},{7,3},{8,12},{9,13},{10,... | collective-permute-start | bytes 98312 | tf_op jit(solution)/shard_map/ppermute | solution.py:471
  48.1 0.7 copy-start.6
  48.8 0.7 copy-start.8
  62.7 10.0 %copy-start.7 = (bf16[3,256,256]{2,1,0:T(8,128)(2,1)S(1)}, bf16[3,256,256]{2,1,0:T(8,128)(2,1)}, u32[]{:S(2)}) copy-start(bf16[3,256,256]{2,1,0:T(8,128)(2,1)} %copy-done.6) | copy-start | bytes 1179652
  62.7 27.2 %collective-permute-start.16 = (bf16[3,256,256]{2,1,0:T(8,128)(2,1)}, bf16[3,256,256]{2,1,0:T(8,128)(2,1)S(1)}, u32[]{:S(2)}, u32[]{:S(2)}) collective-permute-start(bf16[3,256,256]{2,1,0:T(8,128)(2,1)} %copy-done.8), channel_id=1, source_target_pairs={{0,8},{1,9},{2,10},{3,11},{4,12},{5,13},{6,14},{7,15},{8,0},{9,1},... | collective-permute-start | bytes 1179656 | tf_op jit(solution)/shard_map/ppermute | solution.py:471
  63.5 5.8 %collective-permute-start.10 = (bf16[16,8,512]{2,1,0:T(8,128)(2,1)S(1)}, bf16[16,8,512]{2,1,0:T(8,128)(2,1)S(1)}, u32[]{:S(2)}, u32[]{:S(2)}) collective-permute-start(bf16[16,8,512]{2,1,0:T(8,128)(2,1)S(1)} %whiten.1.refs_0_), channel_id=1, source_target_pairs={{0,3},{1,2},{2,1},{3,0},{4,7},{5,6},{6,5},{7,4},{8,11},{9,10},{10,... | collective-permute-start | bytes 393224 | tf_op jit(solution)/shard_map/ppermute | solution.py:471
  63.6 8.7 %collective-permute-start.9 = (bf16[16,8,512]{2,1,0:T(8,128)(2,1)S(1)}, bf16[16,8,512]{2,1,0:T(8,128)(2,1)S(1)}, u32[]{:S(2)}, u32[]{:S(2)}) collective-permute-start(bf16[16,8,512]{2,1,0:T(8,128)(2,1)S(1)} %whiten.1.refs_0_), channel_id=1, source_target_pairs={{0,2},{1,3},{2,0},{3,1},{4,6},{5,7},{6,4},{7,5},{8,10},{9,11},{10,... | collective-permute-start | bytes 393224 | tf_op jit(solution)/shard_map/ppermute | solution.py:471
  65.2 7.5 %collective-permute-start.8 = (bf16[16,8,512]{2,1,0:T(8,128)(2,1)S(1)}, bf16[16,8,512]{2,1,0:T(8,128)(2,1)S(1)}, u32[]{:S(2)}, u32[]{:S(2)}) collective-permute-start(bf16[16,8,512]{2,1,0:T(8,128)(2,1)S(1)} %whiten.1.refs_0_), channel_id=1, source_target_pairs={{0,1},{1,0},{2,3},{3,2},{4,5},{5,4},{6,7},{7,6},{8,9},{9,8},{10,11... | collective-permute-start | bytes 393224 | tf_op jit(solution)/shard_map/ppermute | solution.py:471
  65.4 35.4 %collective-permute-start.11 = (bf16[4,256,256]{2,1,0:T(8,128)(2,1)S(1)}, bf16[4,256,256]{2,1,0:T(8,128)(2,1)S(1)}, u32[]{:S(2)}, u32[]{:S(2)}) collective-permute-start(bf16[4,256,256]{2,1,0:T(8,128)(2,1)S(1)} %get-tuple-element.72), channel_id=1, source_target_pairs={{0,1},{1,0},{2,3},{3,2},{4,5},{5,4},{6,7},{7,6},{8,9},{9,8},{10,11... | collective-permute-start | bytes 1572872 | tf_op jit(solution)/shard_map/ppermute | solution.py:471
  69.3 31.6 %collective-permute-start.12 = (bf16[4,256,256]{2,1,0:T(8,128)(2,1)S(1)}, bf16[4,256,256]{2,1,0:T(8,128)(2,1)S(1)}, u32[]{:S(2)}, u32[]{:S(2)}) collective-permute-start(bf16[4,256,256]{2,1,0:T(8,128)(2,1)S(1)} %get-tuple-element.73), channel_id=1, source_target_pairs={{0,2},{1,3},{2,0},{3,1},{4,6},{5,7},{6,4},{7,5},{8,10},{9,11},{10,... | collective-permute-start | bytes 1572872 | tf_op jit(solution)/shard_map/ppermute | solution.py:471
  72.3 28.6 %collective-permute-start.13 = (bf16[4,256,256]{2,1,0:T(8,128)(2,1)S(1)}, bf16[4,256,256]{2,1,0:T(8,128)(2,1)S(1)}, u32[]{:S(2)}, u32[]{:S(2)}) collective-permute-start(bf16[4,256,256]{2,1,0:T(8,128)(2,1)S(1)} %get-tuple-element.74), channel_id=1, source_target_pairs={{0,3},{1,2},{2,1},{3,0},{4,7},{5,6},{6,5},{7,4},{8,11},{9,10},{10,... | collective-permute-start | bytes 1572872 | tf_op jit(solution)/shard_map/ppermute | solution.py:471
  72.7 19.9 %collective-permute-start.17 = (bf16[3,256,256]{2,1,0:T(8,128)(2,1)S(1)}, bf16[3,256,256]{2,1,0:T(8,128)(2,1)S(1)}, u32[]{:S(2)}, u32[]{:S(2)}) collective-permute-start(bf16[3,256,256]{2,1,0:T(8,128)(2,1)S(1)} %copy-done.7), channel_id=1, source_target_pairs={{0,12},{1,13},{2,14},{3,15},{4,8},{5,9},{6,10},{7,11},{8,4},{9,5},... | collective-permute-start | bytes 1179656 | tf_op jit(solution)/shard_map/ppermute | solution.py:471
  89.9 11.0 %copy-start.3 = (bf16[256,256]{1,0:T(8,128)(2,1)S(1)}, bf16[256,256]{1,0:T(8,128)(2,1)}, u32[]{:S(2)}) copy-start(bf16[256,256]{1,0:T(8,128)(2,1)} %constant.5.clone.refs_8_) | copy-start | bytes 393220
  89.9 11.0 %copy-start.5 = (s32[256]{0:T(256)S(1)}, s32[256]{0:T(256)}, u32[]{:S(2)}) copy-start(s32[256]{0:T(256)} %alive_ref.1) | copy-start | bytes 3076
  89.9 10.9 %collective-permute-start.15 = (bf16[3,256,256]{2,1,0:T(8,128)(2,1)S(1)}, bf16[3,256,256]{2,1,0:T(8,128)(2,1)S(1)}, u32[]{:S(2)}, u32[]{:S(2)}) collective-permute-start(bf16[3,256,256]{2,1,0:T(8,128)(2,1)S(1)} %get-tuple-element.78), channel_id=1, source_target_pairs={{0,4},{1,5},{2,6},{3,7},{4,0},{5,1},{6,2},{7,3},{8,12},{9,13},{10,... | collective-permute-start | bytes 1179656 | tf_op jit(solution)/shard_map/ppermute | solution.py:471

commit v4 on v3

--- a/solution.py
+++ b/solution.py
@@ -76,19 +76,23 @@
     return window(data_ref, row, column * width, STEP, width)
 
 
-def prepare_kernel(data_ref, table_ref, out_ref, block_ref, sems):
+def prepare_kernel(data_ref, table_ref, whole_ref, block_ref, out_ref, in_sems, out_sems):
     _, place = position()
     planes, _, _, width = out_ref.shape
     copies = []
     for plane in range(planes):
         source = window(data_ref, place * STEP, plane * TEAM * width, SEGMENT_LENGTH, TEAM * width)
-        copies.append(pltpu.make_async_copy(source, block_ref.at[plane], sems.at[plane]))
+        copies.append(pltpu.make_async_copy(source, block_ref.at[plane], in_sems.at[plane]))
         copies[plane].start()
     for plane in range(planes):
         copies[plane].wait()
         for member in range(TEAM):
             column = pl.ds(pl.multiple_of((place ^ member) * width, width), width)
             out_ref[plane, member] = transform(table_ref, block_ref[plane, :, column])
+        copies.append(pltpu.make_async_copy(out_ref.at[plane], whole_ref.at[plane], out_sems.at[plane]))
+        copies[-1].start()
+    for copy in copies[planes:]:
+        copy.wait()
 
 
 def prepare(data, table, count):
@@ -99,8 +103,11 @@
         in_specs=[pl.BlockSpec(memory_space=pl.ANY), pl.BlockSpec(memory_space=pltpu.VMEM)],
         scratch_shapes=[
             pltpu.VMEM((planes, SEGMENT_LENGTH, TEAM * width), jnp.bfloat16),
+            pltpu.VMEM((planes, TEAM, BINS, width), jnp.bfloat16),
+            pltpu.SemaphoreType.DMA((planes,)),
             pltpu.SemaphoreType.DMA((planes,)),
         ],
+        out_specs=pl.BlockSpec(memory_space=pl.ANY),
         out_shape=jax.ShapeDtypeStruct((planes, TEAM, BINS, width), jnp.bfloat16),
         compiler_params=pltpu.CompilerParams(vmem_limit_bytes=LARGE),
         name="prepare",
@@ -389,7 +396,7 @@
     return [src[:, k * SHARE : (k + 1) * SHARE] for k in range(TEAM)]
 
 
-BATCH = 4
+BATCH = 8
 
 
 def correlate_kernel(relative, left_ref, whole_ref, *refs):
@@ -402,30 +409,26 @@
     pad = DEPTH - SEGMENT_TALLY * rows
     alive = alive_ref[...].astype(jnp.float32)
 
-    @pl.loop(0, TILES // BATCH)
-    def _(step):
-        for k in range(BATCH):
-            index = step * BATCH + k
-            start = pl.multiple_of(index * rows, rows)
-            tile = pl.ds(start, rows)
-            right_ref[index, DEPTH - pad :, :] = jnp.zeros((pad, width), jnp.bfloat16)
-            for plane in range(TEAM):
-                for member in range(TEAM):
-                    at = pl.multiple_of(plane * span + (member ^ place) * 2 * rows, rows)
-                    piece = other_refs[member - 1][plane, tile, :] if member else whole_ref[plane, 0, tile, :]
-                    right_ref[index, pl.ds(at, rows), :] = piece
-                for j in range(SPLIT // TEAM):
-                    at = pl.multiple_of((plane ^ mine) * span + (2 * j + 1) * rows, rows)
-                    right_ref[index, pl.ds(at, rows), :] = split_refs[plane][j, tile, :]
-            right = right_ref[index]
-            power = jnp.square(right.astype(jnp.float32)).reshape(DEPTH // rows, rows, width)
-            power = jnp.sum(power, axis=0)
-            level = (power[:SUB] + power[SUB:]) / SEGMENT_TALLY
-            factor = alive / jnp.sqrt(level + 0.01)
-            factor = jnp.concatenate([factor, factor], axis=0)[None]
-            cross = jnp.dot(left_ref[index], right, preferred_element_type=jnp.float32)
-            cross = cross.reshape(SOURCES, rows, width)
-            cross_ref[:, tile, :] = jnp.where(factor > 0.0, cross * factor, 0.0).astype(jnp.bfloat16)
+    for index in range(TILES):
+        tile = slice(index * rows, (index + 1) * rows)
+        right_ref[index, DEPTH - pad :, :] = jnp.zeros((pad, width), jnp.bfloat16)
+        for plane in range(TEAM):
+            for member in range(TEAM):
+                at = pl.multiple_of(plane * span + (member ^ place) * 2 * rows, rows)
+                piece = other_refs[member - 1][plane, tile, :] if member else whole_ref[plane, 0, tile, :]
+                right_ref[index, pl.ds(at, rows), :] = piece
+            for j in range(SPLIT // TEAM):
+                at = pl.multiple_of((plane ^ mine) * span + (2 * j + 1) * rows, rows)
+                right_ref[index, pl.ds(at, rows), :] = split_refs[plane][j, tile, :]
+        right = right_ref[index]
+        power = jnp.square(right.astype(jnp.float32)).reshape(DEPTH // rows, rows, width)
+        power = jnp.sum(power, axis=0)
+        level = (power[:SUB] + power[SUB:]) / SEGMENT_TALLY
+        factor = alive / jnp.sqrt(level + 0.01)
+        factor = jnp.concatenate([factor, factor], axis=0)[None]
+        cross = jnp.dot(left_ref[index], right, preferred_element_type=jnp.float32)
+        cross = cross.reshape(SOURCES, rows, width)
+        cross_ref[:, tile, :] = jnp.where(factor > 0.0, cross * factor, 0.0).astype(jnp.bfloat16)
 
     def copy(step):
         part = pl.ds(step * BATCH, BATCH)

time: 108 us -> 106 us (0.981)
  Pallas kernels: 34.7 us -> 32.9 us
    pallas_call x1, Pallas kernels: 6.74 us -> 5.4 us  [correlate(): pl.pallas_call(functools.partial(correlate_kernel, relative), out_specs=p...]
where the time goes in v4:
time: 106 us
  waiting for transfers between devices  49.1 us (46%)
  Pallas kernels  32.9 us (31%)
  starting transfers between devices  21.5 us (20%)
  local copies, waits for them, and re-layouts  2.12 us (2%)
    ppermute x18, waiting for transfers between devices, body(): lax.ppermute(x, 'chan', [(i, i ^ k) for i in range(count)])  49.1 us
    ppermute x18, starting transfers between devices, body(): lax.ppermute(x, 'chan', [(i, i ^ k) for i in range(count)])  15.2 us
    pallas_call x2, Pallas kernels, halves(): pl.pallas_call(functools.partial(halves_kernel, planes), in_specs=[pl.Blo...  7.95 us
    all_to_all x1, starting transfers between devices, body(): lax.all_to_all(whole, 'chan', 0, 0, tiled=True, axis_index_groups=across)  6.33 us
    pallas_call x1, Pallas kernels, pick(): pl.pallas_call(functools.partial(pick_kernel, width), grid=(count // TEAM...  6.12 us
    pallas_call x1, Pallas kernels, correlate(): pl.pallas_call(functools.partial(correlate_kernel, relative), out_specs=p...  5.4 us
    pallas_call x1, Pallas kernels, prepare(): pl.pallas_call(prepare_kernel, in_specs=[pl.BlockSpec(memory_space=pl.ANY...  4.84 us
    pallas_call x1, Pallas kernels, lend(): pl.pallas_call(lend_kernel, in_specs=[pl.BlockSpec(memory_space=pl.ANY)],...  2.78 us
  transfers between devices with their start and end apart: 19, of which 9 were waited for; matrix products, arithmetic and copies ran while one was open for 0% of the time, Pallas kernels for 21%

profile of v4, /device:TPU:0, one launch (start us, length us, event | category | flops | bytes accessed | tf_op | source)
XLA Modules:
  0.0 105.8 jit_solution(18245847245690647067)
XLA Ops:
  0.0 4.8 %prepare.1 = bf16[4,4,256,256]{3,2,1,0:T(8,128)(2,1)} custom-call(bf16[896,4096]{1,0:T(8,128)(2,1)} %data_ref.5, bf16[256,512]{1,0:T(8,128)(2,1)} %constant.4.clone.table_ref.refs_4_), custom_call_target="tpu_custom_call" | custom-call | tf_op jit(solution)/shard_map/prepare/pallas_call | solution.py:101
  4.9 6.3 %all-to-all-start = ((bf16[4,4,256,256]{3,2,1,0:T(8,128)(2,1)}), bf16[4,4,256,256]{3,2,1,0:T(8,128)(2,1)S(1)}, u32[]{:S(2)}, u32[]{:S(2)}) async-start(bf16[4,4,256,256]{3,2,1,0:T(8,128)(2,1)} %prepare.1), calls=%async_computation | async-start | bytes 4194304 | tf_op jit(solution)/shard_map/all_to_all | solution.py:482
  11.2 2.8 %lend.1 = bf16[8,384,256]{2,1,0:T(8,128)(2,1)} custom-call(bf16[896,4096]{1,0:T(8,128)(2,1)} %data_ref.5), custom_call_target="tpu_custom_call" | custom-call | tf_op jit(solution)/shard_map/lend/pallas_call | solution.py:150
  14.1 6.1 %pick.1 = (bf16[8,1024]{1,0:T(8,128)(2,1)}, bf16[8,1024]{1,0:T(8,128)(2,1)}, bf16[8,1024]{1,0:T(8,128)(2,1)}, bf16[8,1024]{1,0:T(8,128)(2,1)}) custom-call(s32[2,16]{1,0:T(2,128)} %sources_ref.1, s32[256]{0:T(256)} %alive_ref.1, bf16[896,4096]{1,0:T(8,128)(2,1)} %data_ref.5), custom_call_target="tpu_custom_call" | custom-call | tf_op jit(solution)/shard_map/pick/pallas_call | solution.py:272
  20.2 0.5 collective-permute-start.1
  20.7 1.5 %collective-permute-start.2 = (bf16[8,1024]{1,0:T(8,128)(2,1)}, bf16[8,1024]{1,0:T(8,128)(2,1)S(1)}, u32[]{:S(2)}, u32[]{:S(2)}) collective-permute-start(bf16[8,1024]{1,0:T(8,128)(2,1)} %get-tuple-element.54), channel_id=1, source_target_pairs={{0,2},{1,3},{2,0},{3,1},{4,6},{5,7},{6,4},{7,5},{8,10},{9,11},{10,... | collective-permute-start | bytes 49160 | tf_op jit(solution)/shard_map/ppermute | solution.py:474
  22.2 2.4 %collective-permute-done.2.refs_2_ = bf16[8,1024]{1,0:T(8,128)(2,1)S(1)} collective-permute-done((bf16[8,1024]{1,0:T(8,128)(2,1)}, bf16[8,1024]{1,0:T(8,128)(2,1)S(1)}, u32[]{:S(2)}, u32[]{:S(2)}) %collective-permute-start.2) | collective-permute-done | bytes 16416 | tf_op jit(solution)/shard_map/ppermute | solution.py:474
  24.6 1.1 %collective-permute-done.3.refs_3_ = bf16[8,1024]{1,0:T(8,128)(2,1)S(1)} collective-permute-done((bf16[8,1024]{1,0:T(8,128)(2,1)}, bf16[8,1024]{1,0:T(8,128)(2,1)S(1)}, u32[]{:S(2)}, u32[]{:S(2)}) %collective-permute-start.3) | collective-permute-done | bytes 16416 | tf_op jit(solution)/shard_map/ppermute | solution.py:474
  25.7 0.6 copy-done.11
  26.3 1.8 %source_spectra.1.refs_0_ = bf16[64,256]{1,0:T(8,128)(2,1)} custom-call(bf16[8,1024]{1,0:T(8,128)(2,1)} %get-tuple-element.52.refs_0_, bf16[8,1024]{1,0:T(8,128)(2,1)} %copy-done.9, bf16[8,1024]{1,0:T(8,128)(2,1)} %copy-done.10, bf16[8,1024]{1,0:T(8,128)(2,1)} %copy-done.11, bf16[256,512]{1,0:T(8,128)(2,1)} %constant.4.clone.table_ref.refs_4_), custom_call_target="tpu_custom_call" | custom-call | tf_op jit(solution)/shard_map/source_spectra/pallas_call | solution.py:309
  28.1 4.0 %halves.2 = (bf16[2,512,256]{2,1,0:T(8,128)(2,1)}, bf16[2,512,256]{2,1,0:T(8,128)(2,1)}) custom-call(bf16[896,4096]{1,0:T(8,128)(2,1)} %data_ref.5, bf16[8,384,256]{2,1,0:T(8,128)(2,1)} %collective-permute-done.lent_ref, bf16[256,512]{1,0:T(8,128)(2,1)} %constant.4.clone.table_ref.refs_4_), custom_call_target="tpu_custom_call" | custom-call | tf_op jit(solution)/shard_map/halves/pallas_call | solution.py:191
  32.1 1.2 %collective-permute-start.7 = (bf16[2,512,256]{2,1,0:T(8,128)(2,1)}, bf16[2,512,256]{2,1,0:T(8,128)(2,1)S(1)}, u32[]{:S(2)}, u32[]{:S(2)}) collective-permute-start(bf16[2,512,256]{2,1,0:T(8,128)(2,1)} %get-tuple-element.61), channel_id=1, source_target_pairs={{0,2},{1,3},{2,0},{3,1},{4,6},{5,7},{6,4},{7,5},{8,10},{9,11},{10,... | collective-permute-start | bytes 1572872 | tf_op jit(solution)/shard_map/ppermute | solution.py:474
  33.3 4.0 %halves.3 = (bf16[2,512,256]{2,1,0:T(8,128)(2,1)}, bf16[2,512,256]{2,1,0:T(8,128)(2,1)}) custom-call(bf16[896,4096]{1,0:T(8,128)(2,1)} %data_ref.5, bf16[8,384,256]{2,1,0:T(8,128)(2,1)} %collective-permute-done.lent_ref, bf16[256,512]{1,0:T(8,128)(2,1)} %constant.4.clone.table_ref.refs_4_), custom_call_target="tpu_custom_call" | custom-call | tf_op jit(solution)/shard_map/halves/pallas_call | solution.py:191
  37.3 1.0 collective-permute-start.14
  38.3 3.8 %collective-permute-start.6 = (bf16[64,256]{1,0:T(8,128)(2,1)S(1)}, bf16[64,256]{1,0:T(8,128)(2,1)S(1)}, u32[]{:S(2)}, u32[]{:S(2)}) collective-permute-start(bf16[64,256]{1,0:T(8,128)(2,1)S(1)} %copy-done.4), channel_id=1, source_target_pairs={{0,12},{1,13},{2,14},{3,15},{4,8},{5,9},{6,10},{7,11},{8,4},{9,5},... | collective-permute-start | bytes 98312 | tf_op jit(solution)/shard_map/ppermute | solution.py:474
  42.1 0.6 collective-permute-start.4
  42.7 4.5 %collective-permute-done.7.got_ref = bf16[2,512,256]{2,1,0:T(8,128)(2,1)S(1)} collective-permute-done((bf16[2,512,256]{2,1,0:T(8,128)(2,1)}, bf16[2,512,256]{2,1,0:T(8,128)(2,1)S(1)}, u32[]{:S(2)}, u32[]{:S(2)}) %collective-permute-start.7) | collective-permute-done | bytes 524320 | tf_op jit(solution)/shard_map/ppermute | solution.py:474
  47.2 0.4 straddle.2
  47.6 0.7 copy-done.6
  48.3 0.7 copy-done.8
  49.1 1.4 %collective-permute-done.6.refs_3_ = bf16[64,256]{1,0:T(8,128)(2,1)S(1)} collective-permute-done((bf16[64,256]{1,0:T(8,128)(2,1)S(1)}, bf16[64,256]{1,0:T(8,128)(2,1)S(1)}, u32[]{:S(2)}, u32[]{:S(2)}) %collective-permute-start.6) | collective-permute-done | bytes 32800 | tf_op jit(solution)/shard_map/ppermute | solution.py:474
  50.5 11.7 %collective-permute-done.5.refs_2_ = bf16[64,256]{1,0:T(8,128)(2,1)S(1)} collective-permute-done((bf16[64,256]{1,0:T(8,128)(2,1)S(1)}, bf16[64,256]{1,0:T(8,128)(2,1)S(1)}, u32[]{:S(2)}, u32[]{:S(2)}) %collective-permute-start.5) | collective-permute-done | bytes 32800 | tf_op jit(solution)/shard_map/ppermute | solution.py:474
  62.6 0.4 whiten.1.refs_0_
  63.1 1.6 %collective-permute-start.9 = (bf16[16,8,512]{2,1,0:T(8,128)(2,1)S(1)}, bf16[16,8,512]{2,1,0:T(8,128)(2,1)S(1)}, u32[]{:S(2)}, u32[]{:S(2)}) collective-permute-start(bf16[16,8,512]{2,1,0:T(8,128)(2,1)S(1)} %whiten.1.refs_0_), channel_id=1, source_target_pairs={{0,2},{1,3},{2,0},{3,1},{4,6},{5,7},{6,4},{7,5},{8,10},{9,11},{10,... | collective-permute-start | bytes 393224 | tf_op jit(solution)/shard_map/ppermute | solution.py:474
  65.2 3.6 %collective-permute-done.10.refs_3_ = bf16[16,8,512]{2,1,0:T(8,128)(2,1)S(1)} collective-permute-done((bf16[16,8,512]{2,1,0:T(8,128)(2,1)S(1)}, bf16[16,8,512]{2,1,0:T(8,128)(2,1)S(1)}, u32[]{:S(2)}, u32[]{:S(2)}) %collective-permute-start.10) | collective-permute-done | bytes 131104 | tf_op jit(solution)/shard_map/ppermute | solution.py:474
  68.8 1.6 %collective-permute-start.12 = (bf16[4,256,256]{2,1,0:T(8,128)(2,1)S(1)}, bf16[4,256,256]{2,1,0:T(8,128)(2,1)S(1)}, u32[]{:S(2)}, u32[]{:S(2)}) collective-permute-start(bf16[4,256,256]{2,1,0:T(8,128)(2,1)S(1)} %get-tuple-element.73), channel_id=1, source_target_pairs={{0,2},{1,3},{2,0},{3,1},{4,6},{5,7},{6,4},{7,5},{8,10},{9,11},{10,... | collective-permute-start | bytes 1572872 | tf_op jit(solution)/shard_map/ppermute | solution.py:474
  70.4 1.4 %collective-permute-done.9.refs_2_ = bf16[16,8,512]{2,1,0:T(8,128)(2,1)S(1)} collective-permute-done((bf16[16,8,512]{2,1,0:T(8,128)(2,1)S(1)}, bf16[16,8,512]{2,1,0:T(8,128)(2,1)S(1)}, u32[]{:S(2)}, u32[]{:S(2)}) %collective-permute-start.9) | collective-permute-done | bytes 131104 | tf_op jit(solution)/shard_map/ppermute | solution.py:474
  72.2 2.4 %collective-permute-start.17 = (bf16[3,256,256]{2,1,0:T(8,128)(2,1)S(1)}, bf16[3,256,256]{2,1,0:T(8,128)(2,1)S(1)}, u32[]{:S(2)}, u32[]{:S(2)}) collective-permute-start(bf16[3,256,256]{2,1,0:T(8,128)(2,1)S(1)} %copy-done.7), channel_id=1, source_target_pairs={{0,12},{1,13},{2,14},{3,15},{4,8},{5,9},{6,10},{7,11},{8,4},{9,5},... | collective-permute-start | bytes 1179656 | tf_op jit(solution)/shard_map/ppermute | solution.py:474
  74.6 14.8 %collective-permute-done.16.refs_5_ = bf16[3,256,256]{2,1,0:T(8,128)(2,1)S(1)} collective-permute-done((bf16[3,256,256]{2,1,0:T(8,128)(2,1)}, bf16[3,256,256]{2,1,0:T(8,128)(2,1)S(1)}, u32[]{:S(2)}, u32[]{:S(2)}) %collective-permute-start.16) | collective-permute-done | bytes 393248 | tf_op jit(solution)/shard_map/ppermute | solution.py:474
  89.4 2.7 %left.1.left_ref = bf16[16,512,512]{2,1,0:T(8,128)(2,1)S(1)} custom-call(bf16[16,8,512]{2,1,0:T(8,128)(2,1)S(1)} %whiten.1.refs_0_, bf16[16,8,512]{2,1,0:T(8,128)(2,1)S(1)} %collective-permute-done.8.refs_1_, bf16[16,8,512]{2,1,0:T(8,128)(2,1)S(1)} %collective-permute-done.9.refs_2_, bf16[16,8,512]{2,1,0:T(8,128)(2,1)S(1)} %collective-permute-done.10.refs_3_), custom_call_target="tpu_custom_call" | custom-call | bytes 1048576 | tf_op jit(solution)/shard_map/left/pallas_call | solution.py:373
  92.1 8.3 %collective-permute-done.15.refs_4_ = bf16[3,256,256]{2,1,0:T(8,128)(2,1)S(1)} collective-permute-done((bf16[3,256,256]{2,1,0:T(8,128)(2,1)S(1)}, bf16[3,256,256]{2,1,0:T(8,128)(2,1)S(1)}, u32[]{:S(2)}, u32[]{:S(2)}) %collective-permute-start.15) | collective-permute-done | bytes 393248 | tf_op jit(solution)/shard_map/ppermute | solution.py:474
  100.4 5.4 %correlate.1 = bf16[32,256,256]{2,1,0:T(8,128)(2,1)} custom-call(bf16[16,512,512]{2,1,0:T(8,128)(2,1)S(1)} %left.1.left_ref, bf16[4,4,256,256]{3,2,1,0:T(8,128)(2,1)S(1)} %all-to-all-done.whole_ref, bf16[4,256,256]{2,1,0:T(8,128)(2,1)S(1)} %collective-permute-done.11.refs_0_, bf16[4,256,256]{2,1,0:T(8,128)(2,1)S(1)} %collective-permute-done.12.refs_1_, ...), custom_call_target="tpu_custom_call" | custom-call | tf_op jit(solution)/shard_map/correlate/pallas_call | solution.py:453
  (42 shorter events, 1.5 us)
Async XLA Ops:
  4.9 57.3 %all-to-all-start = ((bf16[4,4,256,256]{3,2,1,0:T(8,128)(2,1)}), bf16[4,4,256,256]{3,2,1,0:T(8,128)(2,1)S(1)}, u32[]{:S(2)}, u32[]{:S(2)}) async-start(bf16[4,4,256,256]{3,2,1,0:T(8,128)(2,1)} %prepare.1), calls=%async_computation | async-start | bytes 4194304 | tf_op jit(solution)/shard_map/all_to_all | solution.py:482
  14.0 14.1 %collective-permute-start = (bf16[8,384,256]{2,1,0:T(8,128)(2,1)}, bf16[8,384,256]{2,1,0:T(8,128)(2,1)}, u32[]{:S(2)}, u32[]{:S(2)}) collective-permute-start(bf16[8,384,256]{2,1,0:T(8,128)(2,1)} %lend.1), channel_id=1, source_target_pairs={{0,1},{1,0},{2,3},{3,2},{4,5},{5,4},{6,7},{7,6},{8,9},{9,8},{10,11... | collective-permute-start | bytes 4718600 | tf_op jit(solution)/shard_map/ppermute | solution.py:474
  20.2 2.0 %collective-permute-start.1 = (bf16[8,1024]{1,0:T(8,128)(2,1)}, bf16[8,1024]{1,0:T(8,128)(2,1)S(1)}, u32[]{:S(2)}, u32[]{:S(2)}) collective-permute-start(bf16[8,1024]{1,0:T(8,128)(2,1)} %get-tuple-element.53), channel_id=1, source_target_pairs={{0,1},{1,0},{2,3},{3,2},{4,5},{5,4},{6,7},{7,6},{8,9},{9,8},{10,11... | collective-permute-start | bytes 49160 | tf_op jit(solution)/shard_map/ppermute | solution.py:474
  20.7 3.9 %collective-permute-start.2 = (bf16[8,1024]{1,0:T(8,128)(2,1)}, bf16[8,1024]{1,0:T(8,128)(2,1)S(1)}, u32[]{:S(2)}, u32[]{:S(2)}) collective-permute-start(bf16[8,1024]{1,0:T(8,128)(2,1)} %get-tuple-element.54), channel_id=1, source_target_pairs={{0,2},{1,3},{2,0},{3,1},{4,6},{5,7},{6,4},{7,5},{8,10},{9,11},{10,... | collective-permute-start | bytes 49160 | tf_op jit(solution)/shard_map/ppermute | solution.py:474
  22.2 3.5 %collective-permute-start.3 = (bf16[8,1024]{1,0:T(8,128)(2,1)}, bf16[8,1024]{1,0:T(8,128)(2,1)S(1)}, u32[]{:S(2)}, u32[]{:S(2)}) collective-permute-start(bf16[8,1024]{1,0:T(8,128)(2,1)} %get-tuple-element.55), channel_id=1, source_target_pairs={{0,3},{1,2},{2,1},{3,0},{4,7},{5,6},{6,5},{7,4},{8,11},{9,10},{10,... | collective-permute-start | bytes 49160 | tf_op jit(solution)/shard_map/ppermute | solution.py:474
  22.2 3.5 %copy-start.9 = (bf16[8,1024]{1,0:T(8,128)(2,1)}, bf16[8,1024]{1,0:T(8,128)(2,1)S(1)}, u32[]{:S(2)}) copy-start(bf16[8,1024]{1,0:T(8,128)(2,1)S(1)} %collective-permute-done.1.refs_1_) | copy-start | bytes 49156
  24.6 1.1 %copy-start.10 = (bf16[8,1024]{1,0:T(8,128)(2,1)}, bf16[8,1024]{1,0:T(8,128)(2,1)S(1)}, u32[]{:S(2)}) copy-start(bf16[8,1024]{1,0:T(8,128)(2,1)S(1)} %collective-permute-done.2.refs_2_) | copy-start | bytes 49156
  25.7 0.6 copy-start.11
  32.1 6.2 %copy-start.4 = (bf16[64,256]{1,0:T(8,128)(2,1)S(1)}, bf16[64,256]{1,0:T(8,128)(2,1)}, u32[]{:S(2)}) copy-start(bf16[64,256]{1,0:T(8,128)(2,1)} %source_spectra.1.refs_0_) | copy-start | bytes 98308
  32.1 15.1 %copy-start = (bf16[256,512]{1,0:T(8,128)(2,1)S(1)}, bf16[256,512]{1,0:T(8,128)(2,1)}, u32[]{:S(2)}) copy-start(bf16[256,512]{1,0:T(8,128)(2,1)} %constant.4.clone.table_ref.refs_4_) | copy-start | bytes 786436
  32.1 15.1 %copy-start.2 = (bf16[2,512,256]{2,1,0:T(8,128)(2,1)S(1)}, bf16[2,512,256]{2,1,0:T(8,128)(2,1)}, u32[]{:S(2)}) copy-start(bf16[2,512,256]{2,1,0:T(8,128)(2,1)} %get-tuple-element.60.keep_ref) | copy-start | bytes 1572868
  32.1 15.1 %collective-permute-start.7 = (bf16[2,512,256]{2,1,0:T(8,128)(2,1)}, bf16[2,512,256]{2,1,0:T(8,128)(2,1)S(1)}, u32[]{:S(2)}, u32[]{:S(2)}) collective-permute-start(bf16[2,512,256]{2,1,0:T(8,128)(2,1)} %get-tuple-element.61), channel_id=1, source_target_pairs={{0,2},{1,3},{2,0},{3,1},{4,6},{5,7},{6,4},{7,5},{8,10},{9,11},{10,... | collective-permute-start | bytes 1572872 | tf_op jit(solution)/shard_map/ppermute | solution.py:474
  37.3 34.4 %copy-start.1 = (bf16[2,512,256]{2,1,0:T(8,128)(2,1)S(1)}, bf16[2,512,256]{2,1,0:T(8,128)(2,1)}, u32[]{:S(2)}) copy-start(bf16[2,512,256]{2,1,0:T(8,128)(2,1)} %get-tuple-element.75.keep_ref) | copy-start | bytes 1572868
  37.3 27.6 %collective-permute-start.14 = (bf16[2,512,256]{2,1,0:T(8,128)(2,1)}, bf16[2,512,256]{2,1,0:T(8,128)(2,1)S(1)}, u32[]{:S(2)}, u32[]{:S(2)}) collective-permute-start(bf16[2,512,256]{2,1,0:T(8,128)(2,1)} %get-tuple-element.76), channel_id=1, source_target_pairs={{0,2},{1,3},{2,0},{3,1},{4,6},{5,7},{6,4},{7,5},{8,10},{9,11},{10,... | collective-permute-start | bytes 1572872 | tf_op jit(solution)/shard_map/ppermute | solution.py:474
  38.3 12.2 %collective-permute-start.6 = (bf16[64,256]{1,0:T(8,128)(2,1)S(1)}, bf16[64,256]{1,0:T(8,128)(2,1)S(1)}, u32[]{:S(2)}, u32[]{:S(2)}) collective-permute-start(bf16[64,256]{1,0:T(8,128)(2,1)S(1)} %copy-done.4), channel_id=1, source_target_pairs={{0,12},{1,13},{2,14},{3,15},{4,8},{5,9},{6,10},{7,11},{8,4},{9,5},... | collective-permute-start | bytes 98312 | tf_op jit(solution)/shard_map/ppermute | solution.py:474
  42.1 20.1 %collective-permute-start.5 = (bf16[64,256]{1,0:T(8,128)(2,1)S(1)}, bf16[64,256]{1,0:T(8,128)(2,1)S(1)}, u32[]{:S(2)}, u32[]{:S(2)}) collective-permute-start(bf16[64,256]{1,0:T(8,128)(2,1)S(1)} %copy-done.4), channel_id=1, source_target_pairs={{0,8},{1,9},{2,10},{3,11},{4,12},{5,13},{6,14},{7,15},{8,0},{9,1},... | collective-permute-start | bytes 98312 | tf_op jit(solution)/shard_map/ppermute | solution.py:474
  42.1 20.1 %collective-permute-start.4 = (bf16[64,256]{1,0:T(8,128)(2,1)S(1)}, bf16[64,256]{1,0:T(8,128)(2,1)S(1)}, u32[]{:S(2)}, u32[]{:S(2)}) collective-permute-start(bf16[64,256]{1,0:T(8,128)(2,1)S(1)} %copy-done.4), channel_id=1, source_target_pairs={{0,4},{1,5},{2,6},{3,7},{4,0},{5,1},{6,2},{7,3},{8,12},{9,13},{10,... | collective-permute-start | bytes 98312 | tf_op jit(solution)/shard_map/ppermute | solution.py:474
  47.6 0.7 copy-start.6
  48.3 0.7 copy-start.8
  62.2 10.0 %copy-start.7 = (bf16[3,256,256]{2,1,0:T(8,128)(2,1)S(1)}, bf16[3,256,256]{2,1,0:T(8,128)(2,1)}, u32[]{:S(2)}) copy-start(bf16[3,256,256]{2,1,0:T(8,128)(2,1)} %copy-done.6) | copy-start | bytes 1179652
  62.2 27.2 %collective-permute-start.16 = (bf16[3,256,256]{2,1,0:T(8,128)(2,1)}, bf16[3,256,256]{2,1,0:T(8,128)(2,1)S(1)}, u32[]{:S(2)}, u32[]{:S(2)}) collective-permute-start(bf16[3,256,256]{2,1,0:T(8,128)(2,1)} %copy-done.8), channel_id=1, source_target_pairs={{0,8},{1,9},{2,10},{3,11},{4,12},{5,13},{6,14},{7,15},{8,0},{9,1},... | collective-permute-start | bytes 1179656 | tf_op jit(solution)/shard_map/ppermute | solution.py:474
  63.0 5.8 %collective-permute-start.10 = (bf16[16,8,512]{2,1,0:T(8,128)(2,1)S(1)}, bf16[16,8,512]{2,1,0:T(8,128)(2,1)S(1)}, u32[]{:S(2)}, u32[]{:S(2)}) collective-permute-start(bf16[16,8,512]{2,1,0:T(8,128)(2,1)S(1)} %whiten.1.refs_0_), channel_id=1, source_target_pairs={{0,3},{1,2},{2,1},{3,0},{4,7},{5,6},{6,5},{7,4},{8,11},{9,10},{10,... | collective-permute-start | bytes 393224 | tf_op jit(solution)/shard_map/ppermute | solution.py:474
  63.1 8.7 %collective-permute-start.9 = (bf16[16,8,512]{2,1,0:T(8,128)(2,1)S(1)}, bf16[16,8,512]{2,1,0:T(8,128)(2,1)S(1)}, u32[]{:S(2)}, u32[]{:S(2)}) collective-permute-start(bf16[16,8,512]{2,1,0:T(8,128)(2,1)S(1)} %whiten.1.refs_0_), channel_id=1, source_target_pairs={{0,2},{1,3},{2,0},{3,1},{4,6},{5,7},{6,4},{7,5},{8,10},{9,11},{10,... | collective-permute-start | bytes 393224 | tf_op jit(solution)/shard_map/ppermute | solution.py:474
  64.7 7.5 %collective-permute-start.8 = (bf16[16,8,512]{2,1,0:T(8,128)(2,1)S(1)}, bf16[16,8,512]{2,1,0:T(8,128)(2,1)S(1)}, u32[]{:S(2)}, u32[]{:S(2)}) collective-permute-start(bf16[16,8,512]{2,1,0:T(8,128)(2,1)S(1)} %whiten.1.refs_0_), channel_id=1, source_target_pairs={{0,1},{1,0},{2,3},{3,2},{4,5},{5,4},{6,7},{7,6},{8,9},{9,8},{10,11... | collective-permute-start | bytes 393224 | tf_op jit(solution)/shard_map/ppermute | solution.py:474
  64.9 35.4 %collective-permute-start.11 = (bf16[4,256,256]{2,1,0:T(8,128)(2,1)S(1)}, bf16[4,256,256]{2,1,0:T(8,128)(2,1)S(1)}, u32[]{:S(2)}, u32[]{:S(2)}) collective-permute-start(bf16[4,256,256]{2,1,0:T(8,128)(2,1)S(1)} %get-tuple-element.72), channel_id=1, source_target_pairs={{0,1},{1,0},{2,3},{3,2},{4,5},{5,4},{6,7},{7,6},{8,9},{9,8},{10,11... | collective-permute-start | bytes 1572872 | tf_op jit(solution)/shard_map/ppermute | solution.py:474
  68.8 31.6 %collective-permute-start.12 = (bf16[4,256,256]{2,1,0:T(8,128)(2,1)S(1)}, bf16[4,256,256]{2,1,0:T(8,128)(2,1)S(1)}, u32[]{:S(2)}, u32[]{:S(2)}) collective-permute-start(bf16[4,256,256]{2,1,0:T(8,128)(2,1)S(1)} %get-tuple-element.73), channel_id=1, source_target_pairs={{0,2},{1,3},{2,0},{3,1},{4,6},{5,7},{6,4},{7,5},{8,10},{9,11},{10,... | collective-permute-start | bytes 1572872 | tf_op jit(solution)/shard_map/ppermute | solution.py:474
  71.8 28.6 %collective-permute-start.13 = (bf16[4,256,256]{2,1,0:T(8,128)(2,1)S(1)}, bf16[4,256,256]{2,1,0:T(8,128)(2,1)S(1)}, u32[]{:S(2)}, u32[]{:S(2)}) collective-permute-start(bf16[4,256,256]{2,1,0:T(8,128)(2,1)S(1)} %get-tuple-element.74), channel_id=1, source_target_pairs={{0,3},{1,2},{2,1},{3,0},{4,7},{5,6},{6,5},{7,4},{8,11},{9,10},{10,... | collective-permute-start | bytes 1572872 | tf_op jit(solution)/shard_map/ppermute | solution.py:474
  72.2 19.9 %collective-permute-start.17 = (bf16[3,256,256]{2,1,0:T(8,128)(2,1)S(1)}, bf16[3,256,256]{2,1,0:T(8,128)(2,1)S(1)}, u32[]{:S(2)}, u32[]{:S(2)}) collective-permute-start(bf16[3,256,256]{2,1,0:T(8,128)(2,1)S(1)} %copy-done.7), channel_id=1, source_target_pairs={{0,12},{1,13},{2,14},{3,15},{4,8},{5,9},{6,10},{7,11},{8,4},{9,5},... | collective-permute-start | bytes 1179656 | tf_op jit(solution)/shard_map/ppermute | solution.py:474
  89.4 11.0 %copy-start.3 = (bf16[256,256]{1,0:T(8,128)(2,1)S(1)}, bf16[256,256]{1,0:T(8,128)(2,1)}, u32[]{:S(2)}) copy-start(bf16[256,256]{1,0:T(8,128)(2,1)} %constant.5.clone.refs_8_) | copy-start | bytes 393220
  89.4 11.0 %copy-start.5 = (s32[256]{0:T(256)S(1)}, s32[256]{0:T(256)}, u32[]{:S(2)}) copy-start(s32[256]{0:T(256)} %alive_ref.1) | copy-start | bytes 3076
  89.4 10.9 %collective-permute-start.15 = (bf16[3,256,256]{2,1,0:T(8,128)(2,1)S(1)}, bf16[3,256,256]{2,1,0:T(8,128)(2,1)S(1)}, u32[]{:S(2)}, u32[]{:S(2)}) collective-permute-start(bf16[3,256,256]{2,1,0:T(8,128)(2,1)S(1)} %get-tuple-element.78), channel_id=1, source_target_pairs={{0,4},{1,5},{2,6},{3,7},{4,0},{5,1},{6,2},{7,3},{8,12},{9,13},{10,... | collective-permute-start | bytes 1179656 | tf_op jit(solution)/shard_map/ppermute | solution.py:474

commit v5 on v4

--- a/solution.py
+++ b/solution.py
@@ -62,7 +62,7 @@
     return jnp.dot(table_ref[...], block, preferred_element_type=jnp.float32).astype(jnp.bfloat16)
 
 
-def free(size):
+def free():
     return pl.CostEstimate(flops=0, bytes_accessed=0, transcendentals=0)
 
 
@@ -78,7 +78,7 @@
 
 def prepare_kernel(data_ref, table_ref, whole_ref, block_ref, out_ref, in_sems, out_sems):
     _, place = position()
-    planes, _, _, width = out_ref.shape
+    planes, width = out_ref.shape[0] // 2, out_ref.shape[3]
     copies = []
     for plane in range(planes):
         source = window(data_ref, place * STEP, plane * TEAM * width, SEGMENT_LENGTH, TEAM * width)
@@ -86,10 +86,12 @@
         copies[plane].start()
     for plane in range(planes):
         copies[plane].wait()
-        for member in range(TEAM):
-            column = pl.ds(pl.multiple_of((place ^ member) * width, width), width)
-            out_ref[plane, member] = transform(table_ref, block_ref[plane, :, column])
-        copies.append(pltpu.make_async_copy(out_ref.at[plane], whole_ref.at[plane], out_sems.at[plane]))
+        for core in range(2):
+            for turn in range(2):
+                column = pl.ds(pl.multiple_of(((place // 2 ^ turn) * 2 + core) * width, width), width)
+                out_ref[plane * 2 + core, turn] = transform(table_ref, block_ref[plane, :, column])
+        part = pl.ds(plane * 2, 2)
+        copies.append(pltpu.make_async_copy(out_ref.at[part], whole_ref.at[part], out_sems.at[plane]))
         copies[-1].start()
     for copy in copies[planes:]:
         copy.wait()
@@ -103,29 +105,28 @@
         in_specs=[pl.BlockSpec(memory_space=pl.ANY), pl.BlockSpec(memory_space=pltpu.VMEM)],
         scratch_shapes=[
             pltpu.VMEM((planes, SEGMENT_LENGTH, TEAM * width), jnp.bfloat16),
-            pltpu.VMEM((planes, TEAM, BINS, width), jnp.bfloat16),
+            pltpu.VMEM((planes * 2, 2, BINS, width), jnp.bfloat16),
             pltpu.SemaphoreType.DMA((planes,)),
             pltpu.SemaphoreType.DMA((planes,)),
         ],
         out_specs=pl.BlockSpec(memory_space=pl.ANY),
-        out_shape=jax.ShapeDtypeStruct((planes, TEAM, BINS, width), jnp.bfloat16),
+        out_shape=jax.ShapeDtypeStruct((planes * 2, 2, BINS, width), jnp.bfloat16),
         compiler_params=pltpu.CompilerParams(vmem_limit_bytes=LARGE),
         name="prepare",
     )(data, table)
 
 
-def regroup_kernel(whole_ref, *out_refs):
-    for member, out_ref in enumerate(out_refs, 1):
-        out_ref[...] = whole_ref[:, member]
+def regroup_kernel(whole_ref, out_ref):
+    out_ref[...] = whole_ref[:, 1]
 
 
 def regroup(whole):
-    planes, _, rows, width = whole.shape
+    held, _, rows, width = whole.shape
     return pl.pallas_call(
         regroup_kernel,
-        out_shape=[jax.ShapeDtypeStruct((planes, rows, width), jnp.bfloat16)] * (TEAM - 1),
+        out_shape=jax.ShapeDtypeStruct((held, rows, width), jnp.bfloat16),
         compiler_params=pltpu.CompilerParams(vmem_limit_bytes=16 << 20),
-        cost_estimate=free(1 << 20),
+        cost_estimate=free(),
         name="regroup",
     )(whole)
 
@@ -153,7 +154,7 @@
         scratch_shapes=[pltpu.SemaphoreType.DMA((count // 2, STRADDLE // STEP))],
         out_shape=jax.ShapeDtypeStruct((count // 2, STRADDLE, width), jnp.bfloat16),
         compiler_params=pltpu.CompilerParams(vmem_limit_bytes=LARGE),
-        cost_estimate=free(1 << 20),
+        cost_estimate=free(),
         name="lend",
     )(data)
 
@@ -201,7 +202,7 @@
         ],
         out_shape=[shape, shape],
         compiler_params=pltpu.CompilerParams(vmem_limit_bytes=LARGE),
-        cost_estimate=free(1 << 20),
+        cost_estimate=free(),
         name="halves",
     )(data, lent, table)
 
@@ -225,7 +226,7 @@
         out_shape=[shape] * planes,
         scratch_shapes=[pltpu.VMEM((planes, SEGMENT_LENGTH, width), jnp.bfloat16)],
         compiler_params=pltpu.CompilerParams(vmem_limit_bytes=16 << 20),
-        cost_estimate=free(1 << 20),
+        cost_estimate=free(),
         name="straddle",
     )(keep, got, table)
 
@@ -281,7 +282,7 @@
         scratch_shapes=[pltpu.VMEM((HELD, 128), jnp.float32), pltpu.VMEM((SOURCES, PACKED), jnp.float32)],
         out_shape=[jax.ShapeDtypeStruct((SHARE, PACKED), jnp.bfloat16)] * TEAM,
         compiler_params=pltpu.CompilerParams(vmem_limit_bytes=LARGE),
-        cost_estimate=free(1 << 20),
+        cost_estimate=free(),
         name="pick",
     )(sources, alive, data)
 
@@ -310,7 +311,7 @@
         sources_kernel,
         scratch_shapes=[pltpu.VMEM((SHARE, TEAM * HELD), jnp.float32)],
         out_shape=jax.ShapeDtypeStruct(((TEAM_WINDOWS + 1) * SHARE, BINS), jnp.bfloat16),
-        cost_estimate=free(1 << 18),
+        cost_estimate=free(),
         name="source_spectra",
     )(*picked, table)
 
@@ -352,14 +353,15 @@
         scratch_shapes=[pltpu.VMEM((TEAM, TEAM_WINDOWS * SHARE, BINS), jnp.float32)],
         out_shape=jax.ShapeDtypeStruct((TILES, SHARE, DEPTH), jnp.bfloat16),
         compiler_params=pltpu.CompilerParams(vmem_limit_bytes=16 << 20),
-        cost_estimate=free(1 << 18),
+        cost_estimate=free(),
         name="whiten",
     )(*spectra)
 
 
 def left_kernel(*refs):
     src_refs, left_ref = refs[:-1], refs[-1]
-    src = jnp.concatenate([ref[0].astype(jnp.float32) for ref in src_refs], axis=0)
+    src = [ref[i, 0].astype(jnp.float32) for ref in src_refs for i in range(ref.shape[0])]
+    src = jnp.concatenate(src, axis=0)
     lane = lax.broadcasted_iota(jnp.int32, (SOURCES, DEPTH), 1)
     turned = jnp.where(lane % (2 * SUB) < SUB, -pltpu.roll(src, DEPTH - SUB, 1), pltpu.roll(src, SUB, 1))
     row = lax.broadcasted_iota(jnp.int32, (1, 2 * SUB, DEPTH), 1)
@@ -373,7 +375,7 @@
     return pl.pallas_call(
         left_kernel,
         grid=(TILES,),
-        in_specs=[pl.BlockSpec((1, SHARE, DEPTH), lambda i: (i, 0, 0))] * TEAM,
+        in_specs=[pl.BlockSpec((part.shape[0], 1, SHARE, DEPTH), lambda i: (0, i, 0, 0)) for part in src],
         out_specs=pl.BlockSpec((1, SOURCES * 2 * SUB, DEPTH), lambda i: (i, 0, 0)),
         out_shape=jax.ShapeDtypeStruct((TILES, SOURCES * 2 * SUB, DEPTH), jnp.bfloat16),
         compiler_params=pltpu.CompilerParams(vmem_limit_bytes=16 << 20),
@@ -393,15 +395,14 @@
     src = jnp.transpose(src.reshape(SOURCES, SEGMENT_TALLY, TILES, 2 * SUB), (2, 0, 1, 3))
     src = src.reshape(TILES, SOURCES, SEGMENT_TALLY * 2 * SUB)
     src = jnp.pad(src, ((0, 0), (0, 0), (0, DEPTH - SEGMENT_TALLY * 2 * SUB)))
-    return [src[:, k * SHARE : (k + 1) * SHARE] for k in range(TEAM)]
+    return [src[None, :, k * SHARE : (k + 1) * SHARE] for k in range(TEAM)]
 
 
 BATCH = 8
 
 
-def correlate_kernel(relative, left_ref, whole_ref, *refs):
-    other_refs, split_refs = refs[: TEAM - 1], refs[TEAM - 1 : 2 * TEAM - 1]
-    alive_ref, inverse_ref, out_ref, right_ref, cross_ref, done_ref, sems = refs[2 * TEAM - 1 :]
+def correlate_kernel(relative, left_ref, whole_ref, other_ref, *refs):
+    split_refs, (alive_ref, inverse_ref, out_ref, right_ref, cross_ref, done_ref, sems) = refs[:TEAM], refs[TEAM:]
     mine, place = position() if relative else (0, 0)
     width = right_ref.shape[2]
     rows = 2 * SUB
@@ -413,10 +414,12 @@
         tile = slice(index * rows, (index + 1) * rows)
         right_ref[index, DEPTH - pad :, :] = jnp.zeros((pad, width), jnp.bfloat16)
         for plane in range(TEAM):
-            for member in range(TEAM):
-                at = pl.multiple_of(plane * span + (member ^ place) * 2 * rows, rows)
-                piece = other_refs[member - 1][plane, tile, :] if member else whole_ref[plane, 0, tile, :]
-                right_ref[index, pl.ds(at, rows), :] = piece
+            for core in range(2):
+                at = plane * span + core * 2 * rows
+                mine_at = pl.multiple_of(at + place // 2 * 4 * rows, rows)
+                other_at = pl.multiple_of(at + (1 - place // 2) * 4 * rows, rows)
+                right_ref[index, pl.ds(mine_at, rows), :] = whole_ref[plane * 2 + core, 0, tile, :]
+                right_ref[index, pl.ds(other_at, rows), :] = other_ref[plane * 2 + core, tile, :]
             for j in range(SPLIT // TEAM):
                 at = pl.multiple_of((plane ^ mine) * span + (2 * j + 1) * rows, rows)
                 right_ref[index, pl.ds(at, rows), :] = split_refs[plane][j, tile, :]
@@ -448,7 +451,7 @@
         copy(step).wait()
 
 
-def correlate(relative, left, whole, others, split, alive, inverse):
+def correlate(relative, left, whole, other, split, alive, inverse):
     width = whole.shape[3]
     return pl.pallas_call(
         functools.partial(correlate_kernel, relative),
@@ -462,7 +465,7 @@
         out_shape=jax.ShapeDtypeStruct((SOURCES, LAGS, width), jnp.bfloat16),
         compiler_params=pltpu.CompilerParams(vmem_limit_bytes=18 << 20),
         name="correlate",
-    )(left, whole, *others, *split, alive, inverse)
+    )(left, whole, other, *split, alive, inverse)
 
 
 def body(data, alive, sources):
@@ -473,7 +476,7 @@
     if relative:
         swap = lambda x, k: lax.ppermute(x, "chan", [(i, i ^ k) for i in range(count)])
         team = range(1, TEAM)
-        across = [[z * TEAM + p for z in range(count // TEAM)] for p in range(TEAM)]
+        across = [[z * TEAM + y * 2 + core for z in range(count // TEAM) for core in range(2)] for y in range(2)]
         whole = prepare(data, table, count)
         data, whole = lax.optimization_barrier((data, whole))
         lent = lend(data, count)
@@ -489,14 +492,16 @@
         arrived = [swap(spectra, k * TEAM) for k in team]
         keep_near, give_near = halves((0, 1), data, lent, table, count)
         far = straddle(keep_far, swap(give_far, 2), table)
-        arrived, whole, far = lax.optimization_barrier((arrived, whole, far))
-        others = regroup(whole)
-        src = whiten([spectra] + arrived)
-        keep_near, src, others = lax.optimization_barrier((keep_near, src, others))
-        others = [swap(others[k - 1], k) for k in team]
-        near = straddle(keep_near, swap(give_near, 2), table)
+        got_near = swap(give_near, 2)
+        arrived, whole, far, got_near = lax.optimization_barrier((arrived, whole, far, got_near))
+        other = regroup(whole)
+        src = whiten([spectra] + arrived)[None]
+        keep_near, src, other = lax.optimization_barrier((keep_near, src, other))
+        src = jnp.concatenate([src, swap(src, 1)])
+        near = straddle(keep_near, got_near, table)
+        other = swap(other, 2)
+        src = [src, swap(src, 2)]
         split = [near[0], swap(near[1], TEAM), swap(far[0], 2 * TEAM), swap(far[1], 3 * TEAM)]
-        src = [src] + [swap(src, k) for k in team]
     else:
         me = lax.axis_index("chan")
         ids = sources.reshape(-1)
@@ -511,12 +516,12 @@
         blocks = blocks.reshape(SEGMENT_TALLY, SEGMENT_LENGTH, width)
         spectra = jnp.einsum("kt,wtc->wkc", table, blocks, preferred_element_type=jnp.float32)
         spectra = spectra.astype(jnp.bfloat16).reshape(TEAM, TEAM_WINDOWS, BINS, width)
-        whole = spectra[:, 0:1]
-        others = [spectra[:, 2 * k] for k in range(1, TEAM)]
+        whole = spectra[:, 0:3:2].reshape(2 * TEAM, 1, BINS, width)
+        other = spectra[:, 4:7:2].reshape(2 * TEAM, BINS, width)
         split = [spectra[z, 1::2] for z in range(TEAM)]
         src = whiten_all(jnp.transpose(picked, (2, 0, 1)), alive_sources, table)
     left = left_factor(src)
-    out = correlate(relative, left, whole, others, split, alive[None, :], inverse_table())
+    out = correlate(relative, left, whole, other, split, alive[None, :], inverse_table())
     return out.reshape(ROUNDS, SRC, LAGS, width)
 
 

time: 106 us -> 106 us (level)
  the two profiles are of different devices: /device:TPU:0 before, /device:TPU:9 now
where the time goes in v5:
time: 106 us
  waiting for transfers between devices  50.4 us (48%)
  Pallas kernels  33 us (31%)
  starting transfers between devices  20.1 us (19%)
  local copies, waits for them, and re-layouts  2.16 us (2%)
    ppermute x15, waiting for transfers between devices, body(): lax.ppermute(x, 'chan', [(i, i ^ k) for i in range(count)])  50.4 us
    ppermute x15, starting transfers between devices, body(): lax.ppermute(x, 'chan', [(i, i ^ k) for i in range(count)])  14.4 us
    pallas_call x2, Pallas kernels, halves(): pl.pallas_call(functools.partial(halves_kernel, planes), in_specs=[pl.Blo...  7.96 us
    pallas_call x1, Pallas kernels, pick(): pl.pallas_call(functools.partial(pick_kernel, width), grid=(count // TEAM...  6.12 us
    all_to_all x1, starting transfers between devices, body(): lax.all_to_all(whole, 'chan', 0, 0, tiled=True, axis_index_groups=across)  5.64 us
    pallas_call x1, Pallas kernels, correlate(): pl.pallas_call(functools.partial(correlate_kernel, relative), out_specs=p...  5.4 us
    pallas_call x1, Pallas kernels, prepare(): pl.pallas_call(prepare_kernel, in_specs=[pl.BlockSpec(memory_space=pl.ANY...  4.86 us
    pallas_call x1, Pallas kernels, left_factor(): pl.pallas_call(left_kernel, grid=(TILES,), in_specs=[pl.BlockSpec((part.s...  2.8 us
  transfers between devices with their start and end apart: 16, of which 6 were waited for; matrix products, arithmetic and copies ran while one was open for 0% of the time, Pallas kernels for 21%

profile of v5, /device:TPU:9, one launch (start us, length us, event | category | flops | bytes accessed | tf_op | source)
XLA Modules:
  0.0 105.8 jit_solution(17693591575108521789)
XLA Ops:
  0.0 4.9 %prepare.1 = bf16[8,2,256,256]{3,2,1,0:T(8,128)(2,1)} custom-call(bf16[896,4096]{1,0:T(8,128)(2,1)} %data_ref.5, bf16[256,512]{1,0:T(8,128)(2,1)} %constant.4.clone.table_ref.refs_4_), custom_call_target="tpu_custom_call" | custom-call | tf_op jit(solution)/shard_map/prepare/pallas_call | solution.py:103
  4.9 5.6 %all-to-all-start = ((bf16[8,2,256,256]{3,2,1,0:T(8,128)(2,1)}), bf16[8,2,256,256]{3,2,1,0:T(8,128)(2,1)S(1)}, u32[]{:S(2)}, u32[]{:S(2)}) async-start(bf16[8,2,256,256]{3,2,1,0:T(8,128)(2,1)} %prepare.1), calls=%async_computation | async-start | bytes 4194304 | tf_op jit(solution)/shard_map/all_to_all | solution.py:485
  10.5 2.8 %lend.1 = bf16[8,384,256]{2,1,0:T(8,128)(2,1)} custom-call(bf16[896,4096]{1,0:T(8,128)(2,1)} %data_ref.5), custom_call_target="tpu_custom_call" | custom-call | tf_op jit(solution)/shard_map/lend/pallas_call | solution.py:151
  13.3 0.4 collective-permute-start
  13.7 6.1 %pick.1 = (bf16[8,1024]{1,0:T(8,128)(2,1)}, bf16[8,1024]{1,0:T(8,128)(2,1)}, bf16[8,1024]{1,0:T(8,128)(2,1)}, bf16[8,1024]{1,0:T(8,128)(2,1)}) custom-call(s32[2,16]{1,0:T(2,128)} %sources_ref.1, s32[256]{0:T(256)} %alive_ref.1, bf16[896,4096]{1,0:T(8,128)(2,1)} %data_ref.5), custom_call_target="tpu_custom_call" | custom-call | tf_op jit(solution)/shard_map/pick/pallas_call | solution.py:273
  20.0 1.2 %collective-permute-start.2 = (bf16[8,1024]{1,0:T(8,128)(2,1)}, bf16[8,1024]{1,0:T(8,128)(2,1)S(1)}, u32[]{:S(2)}, u32[]{:S(2)}) collective-permute-start(bf16[8,1024]{1,0:T(8,128)(2,1)} %get-tuple-element.50), channel_id=1, source_target_pairs={{0,2},{1,3},{2,0},{3,1},{4,6},{5,7},{6,4},{7,5},{8,10},{9,11},{10,... | collective-permute-start | bytes 49160 | tf_op jit(solution)/shard_map/ppermute | solution.py:477
  21.2 0.7 collective-permute-start.3
  22.0 0.8 collective-permute-done.2.refs_2_
  22.8 2.3 %collective-permute-done.3.refs_3_ = bf16[8,1024]{1,0:T(8,128)(2,1)S(1)} collective-permute-done((bf16[8,1024]{1,0:T(8,128)(2,1)}, bf16[8,1024]{1,0:T(8,128)(2,1)S(1)}, u32[]{:S(2)}, u32[]{:S(2)}) %collective-permute-start.3) | collective-permute-done | bytes 16416 | tf_op jit(solution)/shard_map/ppermute | solution.py:477
  25.1 0.6 copy-done.12
  25.7 1.8 %source_spectra.1.refs_0_ = bf16[64,256]{1,0:T(8,128)(2,1)} custom-call(bf16[8,1024]{1,0:T(8,128)(2,1)} %get-tuple-element.48.refs_0_, bf16[8,1024]{1,0:T(8,128)(2,1)} %copy-done.10, bf16[8,1024]{1,0:T(8,128)(2,1)} %copy-done.11, bf16[8,1024]{1,0:T(8,128)(2,1)} %copy-done.12, bf16[256,512]{1,0:T(8,128)(2,1)} %constant.4.clone.table_ref.refs_4_), custom_call_target="tpu_custom_call" | custom-call | tf_op jit(solution)/shard_map/source_spectra/pallas_call | solution.py:310
  27.5 4.0 %halves.2 = (bf16[2,512,256]{2,1,0:T(8,128)(2,1)}, bf16[2,512,256]{2,1,0:T(8,128)(2,1)}) custom-call(bf16[896,4096]{1,0:T(8,128)(2,1)} %data_ref.5, bf16[8,384,256]{2,1,0:T(8,128)(2,1)} %collective-permute-done.lent_ref, bf16[256,512]{1,0:T(8,128)(2,1)} %constant.4.clone.table_ref.refs_4_), custom_call_target="tpu_custom_call" | custom-call | tf_op jit(solution)/shard_map/halves/pallas_call | solution.py:192
  31.5 0.4 collective-permute-start.7
  31.9 4.0 %halves.3 = (bf16[2,512,256]{2,1,0:T(8,128)(2,1)}, bf16[2,512,256]{2,1,0:T(8,128)(2,1)}) custom-call(bf16[896,4096]{1,0:T(8,128)(2,1)} %data_ref.5, bf16[8,384,256]{2,1,0:T(8,128)(2,1)} %collective-permute-done.lent_ref, bf16[256,512]{1,0:T(8,128)(2,1)} %constant.4.clone.table_ref.refs_4_), custom_call_target="tpu_custom_call" | custom-call | tf_op jit(solution)/shard_map/halves/pallas_call | solution.py:192
  35.9 1.2 %collective-permute-start.8 = (bf16[2,512,256]{2,1,0:T(8,128)(2,1)}, bf16[2,512,256]{2,1,0:T(8,128)(2,1)S(1)}, u32[]{:S(2)}, u32[]{:S(2)}) collective-permute-start(bf16[2,512,256]{2,1,0:T(8,128)(2,1)} %get-tuple-element.60), channel_id=1, source_target_pairs={{0,2},{1,3},{2,0},{3,1},{4,6},{5,7},{6,4},{7,5},{8,10},{9,11},{10,... | collective-permute-start | bytes 1572872 | tf_op jit(solution)/shard_map/ppermute | solution.py:477
  37.1 1.2 %collective-permute-start.6 = (bf16[64,256]{1,0:T(8,128)(2,1)S(1)}, bf16[64,256]{1,0:T(8,128)(2,1)S(1)}, u32[]{:S(2)}, u32[]{:S(2)}) collective-permute-start(bf16[64,256]{1,0:T(8,128)(2,1)S(1)} %copy-done.4), channel_id=1, source_target_pairs={{0,12},{1,13},{2,14},{3,15},{4,8},{5,9},{6,10},{7,11},{8,4},{9,5},... | collective-permute-start | bytes 98312 | tf_op jit(solution)/shard_map/ppermute | solution.py:477
  38.3 0.9 collective-permute-start.5
  39.2 1.2 %collective-permute-start.4 = (bf16[64,256]{1,0:T(8,128)(2,1)S(1)}, bf16[64,256]{1,0:T(8,128)(2,1)S(1)}, u32[]{:S(2)}, u32[]{:S(2)}) collective-permute-start(bf16[64,256]{1,0:T(8,128)(2,1)S(1)} %copy-done.4), channel_id=1, source_target_pairs={{0,4},{1,5},{2,6},{3,7},{4,0},{5,1},{6,2},{7,3},{8,12},{9,13},{10,... | collective-permute-start | bytes 98312 | tf_op jit(solution)/shard_map/ppermute | solution.py:477
  40.4 4.6 %collective-permute-done.7.got_ref = bf16[2,512,256]{2,1,0:T(8,128)(2,1)S(1)} collective-permute-done((bf16[2,512,256]{2,1,0:T(8,128)(2,1)}, bf16[2,512,256]{2,1,0:T(8,128)(2,1)S(1)}, u32[]{:S(2)}, u32[]{:S(2)}) %collective-permute-start.7) | collective-permute-done | bytes 524320 | tf_op jit(solution)/shard_map/ppermute | solution.py:477
  45.3 0.7 copy-done.6
  46.1 0.8 copy-done.8
  46.8 12.6 %collective-permute-done.6.refs_3_ = bf16[64,256]{1,0:T(8,128)(2,1)S(1)} collective-permute-done((bf16[64,256]{1,0:T(8,128)(2,1)S(1)}, bf16[64,256]{1,0:T(8,128)(2,1)S(1)}, u32[]{:S(2)}, u32[]{:S(2)}) %collective-permute-start.6) | collective-permute-done | bytes 32800 | tf_op jit(solution)/shard_map/ppermute | solution.py:477
  59.5 0.4 whiten.1
  60.0 1.3 %collective-permute-start.11 = (bf16[8,256,256]{2,1,0:T(8,128)(2,1)S(1)}, bf16[8,256,256]{2,1,0:T(8,128)(2,1)S(1)}, u32[]{:S(2)}, u32[]{:S(2)}) collective-permute-start(bf16[8,256,256]{2,1,0:T(8,128)(2,1)S(1)} %regroup.1), channel_id=1, source_target_pairs={{0,2},{1,3},{2,0},{3,1},{4,6},{5,7},{6,4},{7,5},{8,10},{9,11},{10,... | collective-permute-start | bytes 3145736 | tf_op jit(solution)/shard_map/ppermute | solution.py:477
  61.3 1.8 %collective-permute-start.9 = (bf16[1,16,8,512]{3,2,1,0:T(8,128)(2,1)S(1)}, bf16[1,16,8,512]{3,2,1,0:T(8,128)(2,1)S(1)}, u32[]{:S(2)}, u32[]{:S(2)}) collective-permute-start(bf16[1,16,8,512]{3,2,1,0:T(8,128)(2,1)S(1)} %bitcast.3), channel_id=1, source_target_pairs={{0,1},{1,0},{2,3},{3,2},{4,5},{5,4},{6,7},{7,6},{8,9},{9,8},{10,11... | collective-permute-start | bytes 393224 | tf_op jit(solution)/shard_map/ppermute | solution.py:477
  63.1 1.3 %collective-permute-start.13 = (bf16[3,256,256]{2,1,0:T(8,128)(2,1)S(1)}, bf16[3,256,256]{2,1,0:T(8,128)(2,1)S(1)}, u32[]{:S(2)}, u32[]{:S(2)}) collective-permute-start(bf16[3,256,256]{2,1,0:T(8,128)(2,1)S(1)} %copy-done.9), channel_id=1, source_target_pairs={{0,8},{1,9},{2,10},{3,11},{4,12},{5,13},{6,14},{7,15},{8,0},{9,1},... | collective-permute-start | bytes 1179656 | tf_op jit(solution)/shard_map/ppermute | solution.py:477
  64.4 1.4 %collective-permute-start.14 = (bf16[3,256,256]{2,1,0:T(8,128)(2,1)S(1)}, bf16[3,256,256]{2,1,0:T(8,128)(2,1)S(1)}, u32[]{:S(2)}, u32[]{:S(2)}) collective-permute-start(bf16[3,256,256]{2,1,0:T(8,128)(2,1)S(1)} %copy-done.7), channel_id=1, source_target_pairs={{0,12},{1,13},{2,14},{3,15},{4,8},{5,9},{6,10},{7,11},{8,4},{9,5},... | collective-permute-start | bytes 1179656 | tf_op jit(solution)/shard_map/ppermute | solution.py:477
  66.2 0.9 collective-permute-start.12
  67.5 21.3 %collective-permute-done.10.refs_1_ = bf16[2,16,8,512]{3,2,1,0:T(8,128)(2,1)S(1)} collective-permute-done((bf16[2,16,8,512]{3,2,1,0:T(8,128)(2,1)S(1)}, bf16[2,16,8,512]{3,2,1,0:T(8,128)(2,1)S(1)}, u32[]{:S(2)}, u32[]{:S(2)}) %collective-permute-start.10) | collective-permute-done | bytes 262176 | tf_op jit(solution)/shard_map/ppermute | solution.py:477
  88.8 2.8 %left.1.left_ref = bf16[16,512,512]{2,1,0:T(8,128)(2,1)S(1)} custom-call(bf16[2,16,8,512]{3,2,1,0:T(8,128)(2,1)S(1)} %constant_dynamic-update-slice_fusion.refs_0_, bf16[2,16,8,512]{3,2,1,0:T(8,128)(2,1)S(1)} %collective-permute-done.10.refs_1_), custom_call_target="tpu_custom_call" | custom-call | bytes 1048576 | tf_op jit(solution)/shard_map/left/pallas_call | solution.py:375
  91.6 8.8 %collective-permute-done.14.refs_3_ = bf16[3,256,256]{2,1,0:T(8,128)(2,1)S(1)} collective-permute-done((bf16[3,256,256]{2,1,0:T(8,128)(2,1)S(1)}, bf16[3,256,256]{2,1,0:T(8,128)(2,1)S(1)}, u32[]{:S(2)}, u32[]{:S(2)}) %collective-permute-start.14) | collective-permute-done | bytes 393248 | tf_op jit(solution)/shard_map/ppermute | solution.py:477
  100.4 5.4 %correlate.1 = bf16[32,256,256]{2,1,0:T(8,128)(2,1)} custom-call(bf16[16,512,512]{2,1,0:T(8,128)(2,1)S(1)} %left.1.left_ref, bf16[8,2,256,256]{3,2,1,0:T(8,128)(2,1)S(1)} %all-to-all-done.whole_ref, bf16[8,256,256]{2,1,0:T(8,128)(2,1)S(1)} %collective-permute-done.11.other_ref, bf16[3,256,256]{2,1,0:T(8,128)(2,1)S(1)} %get-tuple-element.69.refs_0_, ...), custom_call_target="tpu_custom_call" | custom-call | tf_op jit(solution)/shard_map/correlate/pallas_call | solution.py:456
  (40 shorter events, 1.4 us)
Async XLA Ops:
  4.9 54.6 %all-to-all-start = ((bf16[8,2,256,256]{3,2,1,0:T(8,128)(2,1)}), bf16[8,2,256,256]{3,2,1,0:T(8,128)(2,1)S(1)}, u32[]{:S(2)}, u32[]{:S(2)}) async-start(bf16[8,2,256,256]{3,2,1,0:T(8,128)(2,1)} %prepare.1), calls=%async_computation | async-start | bytes 4194304 | tf_op jit(solution)/shard_map/all_to_all | solution.py:485
  13.3 14.2 %collective-permute-start = (bf16[8,384,256]{2,1,0:T(8,128)(2,1)}, bf16[8,384,256]{2,1,0:T(8,128)(2,1)}, u32[]{:S(2)}, u32[]{:S(2)}) collective-permute-start(bf16[8,384,256]{2,1,0:T(8,128)(2,1)} %lend.1), channel_id=1, source_target_pairs={{0,1},{1,0},{2,3},{3,2},{4,5},{5,4},{6,7},{7,6},{8,9},{9,8},{10,11... | collective-permute-start | bytes 4718600 | tf_op jit(solution)/shard_map/ppermute | solution.py:477
  19.8 2.1 %collective-permute-start.1 = (bf16[8,1024]{1,0:T(8,128)(2,1)}, bf16[8,1024]{1,0:T(8,128)(2,1)S(1)}, u32[]{:S(2)}, u32[]{:S(2)}) collective-permute-start(bf16[8,1024]{1,0:T(8,128)(2,1)} %get-tuple-element.49), channel_id=1, source_target_pairs={{0,1},{1,0},{2,3},{3,2},{4,5},{5,4},{6,7},{7,6},{8,9},{9,8},{10,11... | collective-permute-start | bytes 49160 | tf_op jit(solution)/shard_map/ppermute | solution.py:477
  20.0 2.8 %collective-permute-start.2 = (bf16[8,1024]{1,0:T(8,128)(2,1)}, bf16[8,1024]{1,0:T(8,128)(2,1)S(1)}, u32[]{:S(2)}, u32[]{:S(2)}) collective-permute-start(bf16[8,1024]{1,0:T(8,128)(2,1)} %get-tuple-element.50), channel_id=1, source_target_pairs={{0,2},{1,3},{2,0},{3,1},{4,6},{5,7},{6,4},{7,5},{8,10},{9,11},{10,... | collective-permute-start | bytes 49160 | tf_op jit(solution)/shard_map/ppermute | solution.py:477
  21.2 3.8 %collective-permute-start.3 = (bf16[8,1024]{1,0:T(8,128)(2,1)}, bf16[8,1024]{1,0:T(8,128)(2,1)S(1)}, u32[]{:S(2)}, u32[]{:S(2)}) collective-permute-start(bf16[8,1024]{1,0:T(8,128)(2,1)} %get-tuple-element.51), channel_id=1, source_target_pairs={{0,3},{1,2},{2,1},{3,0},{4,7},{5,6},{6,5},{7,4},{8,11},{9,10},{10,... | collective-permute-start | bytes 49160 | tf_op jit(solution)/shard_map/ppermute | solution.py:477
  22.0 3.1 %copy-start.10 = (bf16[8,1024]{1,0:T(8,128)(2,1)}, bf16[8,1024]{1,0:T(8,128)(2,1)S(1)}, u32[]{:S(2)}) copy-start(bf16[8,1024]{1,0:T(8,128)(2,1)S(1)} %collective-permute-done.1.refs_1_) | copy-start | bytes 49156
  22.8 2.3 %copy-start.11 = (bf16[8,1024]{1,0:T(8,128)(2,1)}, bf16[8,1024]{1,0:T(8,128)(2,1)S(1)}, u32[]{:S(2)}) copy-start(bf16[8,1024]{1,0:T(8,128)(2,1)S(1)} %collective-permute-done.2.refs_2_) | copy-start | bytes 49156
  25.1 0.6 copy-start.12
  31.5 5.6 %copy-start.4 = (bf16[64,256]{1,0:T(8,128)(2,1)S(1)}, bf16[64,256]{1,0:T(8,128)(2,1)}, u32[]{:S(2)}) copy-start(bf16[64,256]{1,0:T(8,128)(2,1)} %source_spectra.1.refs_0_) | copy-start | bytes 98308
  31.5 13.4 %copy-start = (bf16[256,512]{1,0:T(8,128)(2,1)S(1)}, bf16[256,512]{1,0:T(8,128)(2,1)}, u32[]{:S(2)}) copy-start(bf16[256,512]{1,0:T(8,128)(2,1)} %constant.4.clone.table_ref.refs_4_) | copy-start | bytes 786436
  31.5 13.4 %copy-start.2 = (bf16[2,512,256]{2,1,0:T(8,128)(2,1)S(1)}, bf16[2,512,256]{2,1,0:T(8,128)(2,1)}, u32[]{:S(2)}) copy-start(bf16[2,512,256]{2,1,0:T(8,128)(2,1)} %get-tuple-element.56.keep_ref) | copy-start | bytes 1572868
  31.5 13.4 %collective-permute-start.7 = (bf16[2,512,256]{2,1,0:T(8,128)(2,1)}, bf16[2,512,256]{2,1,0:T(8,128)(2,1)S(1)}, u32[]{:S(2)}, u32[]{:S(2)}) collective-permute-start(bf16[2,512,256]{2,1,0:T(8,128)(2,1)} %get-tuple-element.57), channel_id=1, source_target_pairs={{0,2},{1,3},{2,0},{3,1},{4,6},{5,7},{6,4},{7,5},{8,10},{9,11},{10,... | collective-permute-start | bytes 1572872 | tf_op jit(solution)/shard_map/ppermute | solution.py:477
  35.9 23.5 %collective-permute-start.8 = (bf16[2,512,256]{2,1,0:T(8,128)(2,1)}, bf16[2,512,256]{2,1,0:T(8,128)(2,1)S(1)}, u32[]{:S(2)}, u32[]{:S(2)}) collective-permute-start(bf16[2,512,256]{2,1,0:T(8,128)(2,1)} %get-tuple-element.60), channel_id=1, source_target_pairs={{0,2},{1,3},{2,0},{3,1},{4,6},{5,7},{6,4},{7,5},{8,10},{9,11},{10,... | collective-permute-start | bytes 1572872 | tf_op jit(solution)/shard_map/ppermute | solution.py:477
  37.1 22.3 %collective-permute-start.6 = (bf16[64,256]{1,0:T(8,128)(2,1)S(1)}, bf16[64,256]{1,0:T(8,128)(2,1)S(1)}, u32[]{:S(2)}, u32[]{:S(2)}) collective-permute-start(bf16[64,256]{1,0:T(8,128)(2,1)S(1)} %copy-done.4), channel_id=1, source_target_pairs={{0,12},{1,13},{2,14},{3,15},{4,8},{5,9},{6,10},{7,11},{8,4},{9,5},... | collective-permute-start | bytes 98312 | tf_op jit(solution)/shard_map/ppermute | solution.py:477
  38.3 21.1 %collective-permute-start.5 = (bf16[64,256]{1,0:T(8,128)(2,1)S(1)}, bf16[64,256]{1,0:T(8,128)(2,1)S(1)}, u32[]{:S(2)}, u32[]{:S(2)}) collective-permute-start(bf16[64,256]{1,0:T(8,128)(2,1)S(1)} %copy-done.4), channel_id=1, source_target_pairs={{0,8},{1,9},{2,10},{3,11},{4,12},{5,13},{6,14},{7,15},{8,0},{9,1},... | collective-permute-start | bytes 98312 | tf_op jit(solution)/shard_map/ppermute | solution.py:477
  39.2 20.2 %collective-permute-start.4 = (bf16[64,256]{1,0:T(8,128)(2,1)S(1)}, bf16[64,256]{1,0:T(8,128)(2,1)S(1)}, u32[]{:S(2)}, u32[]{:S(2)}) collective-permute-start(bf16[64,256]{1,0:T(8,128)(2,1)S(1)} %copy-done.4), channel_id=1, source_target_pairs={{0,4},{1,5},{2,6},{3,7},{4,0},{5,1},{6,2},{7,3},{8,12},{9,13},{10,... | collective-permute-start | bytes 98312 | tf_op jit(solution)/shard_map/ppermute | solution.py:477
  44.9 20.9 %copy-start.1 = (bf16[2,512,256]{2,1,0:T(8,128)(2,1)S(1)}, bf16[2,512,256]{2,1,0:T(8,128)(2,1)}, u32[]{:S(2)}) copy-start(bf16[2,512,256]{2,1,0:T(8,128)(2,1)} %get-tuple-element.67.keep_ref) | copy-start | bytes 1572868
  45.3 0.7 copy-start.6
  46.1 0.8 copy-start.8
  59.4 3.6 %copy-start.9 = (bf16[3,256,256]{2,1,0:T(8,128)(2,1)S(1)}, bf16[3,256,256]{2,1,0:T(8,128)(2,1)}, u32[]{:S(2)}) copy-start(bf16[3,256,256]{2,1,0:T(8,128)(2,1)} %copy-done.8) | copy-start | bytes 1179652
  59.5 5.0 %copy-start.7 = (bf16[3,256,256]{2,1,0:T(8,128)(2,1)S(1)}, bf16[3,256,256]{2,1,0:T(8,128)(2,1)}, u32[]{:S(2)}) copy-start(bf16[3,256,256]{2,1,0:T(8,128)(2,1)} %copy-done.6) | copy-start | bytes 1179652
  60.0 40.4 %collective-permute-start.11 = (bf16[8,256,256]{2,1,0:T(8,128)(2,1)S(1)}, bf16[8,256,256]{2,1,0:T(8,128)(2,1)S(1)}, u32[]{:S(2)}, u32[]{:S(2)}) collective-permute-start(bf16[8,256,256]{2,1,0:T(8,128)(2,1)S(1)} %regroup.1), channel_id=1, source_target_pairs={{0,2},{1,3},{2,0},{3,1},{4,6},{5,7},{6,4},{7,5},{8,10},{9,11},{10,... | collective-permute-start | bytes 3145736 | tf_op jit(solution)/shard_map/ppermute | solution.py:477
  61.3 5.8 %collective-permute-start.9 = (bf16[1,16,8,512]{3,2,1,0:T(8,128)(2,1)S(1)}, bf16[1,16,8,512]{3,2,1,0:T(8,128)(2,1)S(1)}, u32[]{:S(2)}, u32[]{:S(2)}) collective-permute-start(bf16[1,16,8,512]{3,2,1,0:T(8,128)(2,1)S(1)} %bitcast.3), channel_id=1, source_target_pairs={{0,1},{1,0},{2,3},{3,2},{4,5},{5,4},{6,7},{7,6},{8,9},{9,8},{10,11... | collective-permute-start | bytes 393224 | tf_op jit(solution)/shard_map/ppermute | solution.py:477
  63.1 28.5 %collective-permute-start.13 = (bf16[3,256,256]{2,1,0:T(8,128)(2,1)S(1)}, bf16[3,256,256]{2,1,0:T(8,128)(2,1)S(1)}, u32[]{:S(2)}, u32[]{:S(2)}) collective-permute-start(bf16[3,256,256]{2,1,0:T(8,128)(2,1)S(1)} %copy-done.9), channel_id=1, source_target_pairs={{0,8},{1,9},{2,10},{3,11},{4,12},{5,13},{6,14},{7,15},{8,0},{9,1},... | collective-permute-start | bytes 1179656 | tf_op jit(solution)/shard_map/ppermute | solution.py:477
  64.4 36.0 %collective-permute-start.14 = (bf16[3,256,256]{2,1,0:T(8,128)(2,1)S(1)}, bf16[3,256,256]{2,1,0:T(8,128)(2,1)S(1)}, u32[]{:S(2)}, u32[]{:S(2)}) collective-permute-start(bf16[3,256,256]{2,1,0:T(8,128)(2,1)S(1)} %copy-done.7), channel_id=1, source_target_pairs={{0,12},{1,13},{2,14},{3,15},{4,8},{5,9},{6,10},{7,11},{8,4},{9,5},... | collective-permute-start | bytes 1179656 | tf_op jit(solution)/shard_map/ppermute | solution.py:477
  66.2 34.2 %collective-permute-start.12 = (bf16[3,256,256]{2,1,0:T(8,128)(2,1)S(1)}, bf16[3,256,256]{2,1,0:T(8,128)(2,1)S(1)}, u32[]{:S(2)}, u32[]{:S(2)}) collective-permute-start(bf16[3,256,256]{2,1,0:T(8,128)(2,1)S(1)} %get-tuple-element.70), channel_id=1, source_target_pairs={{0,4},{1,5},{2,6},{3,7},{4,0},{5,1},{6,2},{7,3},{8,12},{9,13},{10,... | collective-permute-start | bytes 1179656 | tf_op jit(solution)/shard_map/ppermute | solution.py:477
  67.1 33.3 %copy-start.3 = (bf16[256,256]{1,0:T(8,128)(2,1)S(1)}, bf16[256,256]{1,0:T(8,128)(2,1)}, u32[]{:S(2)}) copy-start(bf16[256,256]{1,0:T(8,128)(2,1)} %constant.5.clone.refs_5_) | copy-start | bytes 393220
  67.2 33.3 %copy-start.5 = (s32[256]{0:T(256)S(1)}, s32[256]{0:T(256)}, u32[]{:S(2)}) copy-start(s32[256]{0:T(256)} %alive_ref.1) | copy-start | bytes 3076
  67.2 21.6 %collective-permute-start.10 = (bf16[2,16,8,512]{3,2,1,0:T(8,128)(2,1)S(1)}, bf16[2,16,8,512]{3,2,1,0:T(8,128)(2,1)S(1)}, u32[]{:S(2)}, u32[]{:S(2)}) collective-permute-start(bf16[2,16,8,512]{3,2,1,0:T(8,128)(2,1)S(1)} %constant_dynamic-update-slice_fusion.refs_0_), channel_id=1, source_target_pairs={{0,2},{1,3},{2,0},{3,1},{4,6},{5,7},{6,4},{7,5},{8,10},{9,11},{10,... | collective-permute-start | bytes 786440 | tf_op jit(solution)/shard_map/ppermute | solution.py:477

commit v6 on v4

--- a/solution.py
+++ b/solution.py
@@ -76,14 +76,17 @@
     return window(data_ref, row, column * width, STEP, width)
 
 
-def prepare_kernel(data_ref, table_ref, whole_ref, block_ref, out_ref, in_sems, out_sems):
+def prepare_kernel(data_ref, rows_ref, whole_ref, block_ref, out_ref, table_ref, in_sems, out_sems, sem):
     _, place = position()
     planes, _, _, width = out_ref.shape
     copies = []
+    table = pltpu.make_async_copy(rows_ref, table_ref, sem)
+    table.start()
     for plane in range(planes):
         source = window(data_ref, place * STEP, plane * TEAM * width, SEGMENT_LENGTH, TEAM * width)
         copies.append(pltpu.make_async_copy(source, block_ref.at[plane], in_sems.at[plane]))
         copies[plane].start()
+    table.wait()
     for plane in range(planes):
         copies[plane].wait()
         for member in range(TEAM):
@@ -100,12 +103,14 @@
     planes = count // TEAM
     return pl.pallas_call(
         prepare_kernel,
-        in_specs=[pl.BlockSpec(memory_space=pl.ANY), pl.BlockSpec(memory_space=pltpu.VMEM)],
+        in_specs=[pl.BlockSpec(memory_space=pl.ANY)] * 2,
         scratch_shapes=[
             pltpu.VMEM((planes, SEGMENT_LENGTH, TEAM * width), jnp.bfloat16),
             pltpu.VMEM((planes, TEAM, BINS, width), jnp.bfloat16),
+            pltpu.VMEM((BINS, SEGMENT_LENGTH), jnp.bfloat16),
             pltpu.SemaphoreType.DMA((planes,)),
             pltpu.SemaphoreType.DMA((planes,)),
+            pltpu.SemaphoreType.DMA,
         ],
         out_specs=pl.BlockSpec(memory_space=pl.ANY),
         out_shape=jax.ShapeDtypeStruct((planes, TEAM, BINS, width), jnp.bfloat16),

time: 106 us -> 105 us (level)
  transfers between devices with their start and end apart: 19 -> 19, of which waited for: 9 -> 9; matrix products, arithmetic and copies ran while one was open for 0% -> 0% of each run, Pallas kernels for 21% -> 22%
where the time goes in v6:
time: 105 us
  waiting for transfers between devices  49.2 us (47%)
  Pallas kernels  32 us (30%)
  starting transfers between devices  21.4 us (20%)
  local copies, waits for them, and re-layouts  2.12 us (2%)
    ppermute x18, waiting for transfers between devices, body(): lax.ppermute(x, 'chan', [(i, i ^ k) for i in range(count)])  49.2 us
    ppermute x18, starting transfers between devices, body(): lax.ppermute(x, 'chan', [(i, i ^ k) for i in range(count)])  15.1 us
    pallas_call x2, Pallas kernels, halves(): pl.pallas_call(functools.partial(halves_kernel, planes), in_specs=[pl.Blo...  7.95 us
    all_to_all x1, starting transfers between devices, body(): lax.all_to_all(whole, 'chan', 0, 0, tiled=True, axis_index_groups=across)  6.32 us
    pallas_call x1, Pallas kernels, pick(): pl.pallas_call(functools.partial(pick_kernel, width), grid=(count // TEAM...  6.12 us
    pallas_call x1, Pallas kernels, correlate(): pl.pallas_call(functools.partial(correlate_kernel, relative), out_specs=p...  5.39 us
    pallas_call x1, Pallas kernels, prepare(): pl.pallas_call(prepare_kernel, in_specs=[pl.BlockSpec(memory_space=pl.ANY...  3.99 us
    pallas_call x1, Pallas kernels, lend(): pl.pallas_call(lend_kernel, in_specs=[pl.BlockSpec(memory_space=pl.ANY)],...  2.78 us
  transfers between devices with their start and end apart: 19, of which 9 were waited for; matrix products, arithmetic and copies ran while one was open for 0% of the time, Pallas kernels for 22%

profile of v6, /device:TPU:0, one launch (start us, length us, event | category | flops | bytes accessed | tf_op | source)
XLA Modules:
  0.0 104.9 jit_solution(14061079666611090924)
XLA Ops:
  0.0 4.0 %prepare.1 = bf16[4,4,256,256]{3,2,1,0:T(8,128)(2,1)} custom-call(bf16[896,4096]{1,0:T(8,128)(2,1)} %data_ref.5, bf16[256,512]{1,0:T(8,128)(2,1)} %constant.4.clone.rows_ref.table_ref.refs_4_), custom_call_target="tpu_custom_call" | custom-call | tf_op jit(solution)/shard_map/prepare/pallas_call | solution.py:104
  4.0 6.3 %all-to-all-start = ((bf16[4,4,256,256]{3,2,1,0:T(8,128)(2,1)}), bf16[4,4,256,256]{3,2,1,0:T(8,128)(2,1)S(1)}, u32[]{:S(2)}, u32[]{:S(2)}) async-start(bf16[4,4,256,256]{3,2,1,0:T(8,128)(2,1)} %prepare.1), calls=%async_computation | async-start | bytes 4194304 | tf_op jit(solution)/shard_map/all_to_all | solution.py:487
  10.3 2.8 %lend.1 = bf16[8,384,256]{2,1,0:T(8,128)(2,1)} custom-call(bf16[896,4096]{1,0:T(8,128)(2,1)} %data_ref.5), custom_call_target="tpu_custom_call" | custom-call | tf_op jit(solution)/shard_map/lend/pallas_call | solution.py:155
  13.2 6.1 %pick.1 = (bf16[8,1024]{1,0:T(8,128)(2,1)}, bf16[8,1024]{1,0:T(8,128)(2,1)}, bf16[8,1024]{1,0:T(8,128)(2,1)}, bf16[8,1024]{1,0:T(8,128)(2,1)}) custom-call(s32[2,16]{1,0:T(2,128)} %sources_ref.1, s32[256]{0:T(256)} %alive_ref.1, bf16[896,4096]{1,0:T(8,128)(2,1)} %data_ref.5), custom_call_target="tpu_custom_call" | custom-call | tf_op jit(solution)/shard_map/pick/pallas_call | solution.py:277
  19.3 0.5 collective-permute-start.1
  19.8 1.5 %collective-permute-start.2 = (bf16[8,1024]{1,0:T(8,128)(2,1)}, bf16[8,1024]{1,0:T(8,128)(2,1)S(1)}, u32[]{:S(2)}, u32[]{:S(2)}) collective-permute-start(bf16[8,1024]{1,0:T(8,128)(2,1)} %get-tuple-element.54), channel_id=1, source_target_pairs={{0,2},{1,3},{2,0},{3,1},{4,6},{5,7},{6,4},{7,5},{8,10},{9,11},{10,... | collective-permute-start | bytes 49160 | tf_op jit(solution)/shard_map/ppermute | solution.py:479
  21.3 2.4 %collective-permute-done.2.refs_2_ = bf16[8,1024]{1,0:T(8,128)(2,1)S(1)} collective-permute-done((bf16[8,1024]{1,0:T(8,128)(2,1)}, bf16[8,1024]{1,0:T(8,128)(2,1)S(1)}, u32[]{:S(2)}, u32[]{:S(2)}) %collective-permute-start.2) | collective-permute-done | bytes 16416 | tf_op jit(solution)/shard_map/ppermute | solution.py:479
  23.8 1.1 %collective-permute-done.3.refs_3_ = bf16[8,1024]{1,0:T(8,128)(2,1)S(1)} collective-permute-done((bf16[8,1024]{1,0:T(8,128)(2,1)}, bf16[8,1024]{1,0:T(8,128)(2,1)S(1)}, u32[]{:S(2)}, u32[]{:S(2)}) %collective-permute-start.3) | collective-permute-done | bytes 16416 | tf_op jit(solution)/shard_map/ppermute | solution.py:479
  24.8 0.6 copy-done.11
  25.4 1.8 %source_spectra.1.refs_0_ = bf16[64,256]{1,0:T(8,128)(2,1)} custom-call(bf16[8,1024]{1,0:T(8,128)(2,1)} %get-tuple-element.52.refs_0_, bf16[8,1024]{1,0:T(8,128)(2,1)} %copy-done.9, bf16[8,1024]{1,0:T(8,128)(2,1)} %copy-done.10, bf16[8,1024]{1,0:T(8,128)(2,1)} %copy-done.11, bf16[256,512]{1,0:T(8,128)(2,1)} %constant.4.clone.rows_ref.table_ref.refs_4_), custom_call_target="tpu_custom_call" | custom-call | tf_op jit(solution)/shard_map/source_spectra/pallas_call | solution.py:314
  27.3 4.0 %halves.2 = (bf16[2,512,256]{2,1,0:T(8,128)(2,1)}, bf16[2,512,256]{2,1,0:T(8,128)(2,1)}) custom-call(bf16[896,4096]{1,0:T(8,128)(2,1)} %data_ref.5, bf16[8,384,256]{2,1,0:T(8,128)(2,1)} %collective-permute-done.lent_ref, bf16[256,512]{1,0:T(8,128)(2,1)} %constant.4.clone.rows_ref.table_ref.refs_4_), custom_call_target="tpu_custom_call" | custom-call | tf_op jit(solution)/shard_map/halves/pallas_call | solution.py:196
  31.3 1.2 %collective-permute-start.7 = (bf16[2,512,256]{2,1,0:T(8,128)(2,1)}, bf16[2,512,256]{2,1,0:T(8,128)(2,1)S(1)}, u32[]{:S(2)}, u32[]{:S(2)}) collective-permute-start(bf16[2,512,256]{2,1,0:T(8,128)(2,1)} %get-tuple-element.61), channel_id=1, source_target_pairs={{0,2},{1,3},{2,0},{3,1},{4,6},{5,7},{6,4},{7,5},{8,10},{9,11},{10,... | collective-permute-start | bytes 1572872 | tf_op jit(solution)/shard_map/ppermute | solution.py:479
  32.5 4.0 %halves.3 = (bf16[2,512,256]{2,1,0:T(8,128)(2,1)}, bf16[2,512,256]{2,1,0:T(8,128)(2,1)}) custom-call(bf16[896,4096]{1,0:T(8,128)(2,1)} %data_ref.5, bf16[8,384,256]{2,1,0:T(8,128)(2,1)} %collective-permute-done.lent_ref, bf16[256,512]{1,0:T(8,128)(2,1)} %constant.4.clone.rows_ref.table_ref.refs_4_), custom_call_target="tpu_custom_call" | custom-call | tf_op jit(solution)/shard_map/halves/pallas_call | solution.py:196
  36.5 1.0 collective-permute-start.14
  37.4 3.8 %collective-permute-start.6 = (bf16[64,256]{1,0:T(8,128)(2,1)S(1)}, bf16[64,256]{1,0:T(8,128)(2,1)S(1)}, u32[]{:S(2)}, u32[]{:S(2)}) collective-permute-start(bf16[64,256]{1,0:T(8,128)(2,1)S(1)} %copy-done.4), channel_id=1, source_target_pairs={{0,12},{1,13},{2,14},{3,15},{4,8},{5,9},{6,10},{7,11},{8,4},{9,5},... | collective-permute-start | bytes 98312 | tf_op jit(solution)/shard_map/ppermute | solution.py:479
  41.3 0.6 collective-permute-start.4
  41.8 4.5 %collective-permute-done.7.got_ref = bf16[2,512,256]{2,1,0:T(8,128)(2,1)S(1)} collective-permute-done((bf16[2,512,256]{2,1,0:T(8,128)(2,1)}, bf16[2,512,256]{2,1,0:T(8,128)(2,1)S(1)}, u32[]{:S(2)}, u32[]{:S(2)}) %collective-permute-start.7) | collective-permute-done | bytes 524320 | tf_op jit(solution)/shard_map/ppermute | solution.py:479
  46.3 0.4 straddle.2
  46.7 0.7 copy-done.6
  47.5 0.7 copy-done.8
  48.2 1.4 %collective-permute-done.6.refs_3_ = bf16[64,256]{1,0:T(8,128)(2,1)S(1)} collective-permute-done((bf16[64,256]{1,0:T(8,128)(2,1)S(1)}, bf16[64,256]{1,0:T(8,128)(2,1)S(1)}, u32[]{:S(2)}, u32[]{:S(2)}) %collective-permute-start.6) | collective-permute-done | bytes 32800 | tf_op jit(solution)/shard_map/ppermute | solution.py:479
  49.7 11.7 %collective-permute-done.5.refs_2_ = bf16[64,256]{1,0:T(8,128)(2,1)S(1)} collective-permute-done((bf16[64,256]{1,0:T(8,128)(2,1)S(1)}, bf16[64,256]{1,0:T(8,128)(2,1)S(1)}, u32[]{:S(2)}, u32[]{:S(2)}) %collective-permute-start.5) | collective-permute-done | bytes 32800 | tf_op jit(solution)/shard_map/ppermute | solution.py:479
  61.7 0.4 whiten.1.refs_0_
  62.2 1.6 %collective-permute-start.9 = (bf16[16,8,512]{2,1,0:T(8,128)(2,1)S(1)}, bf16[16,8,512]{2,1,0:T(8,128)(2,1)S(1)}, u32[]{:S(2)}, u32[]{:S(2)}) collective-permute-start(bf16[16,8,512]{2,1,0:T(8,128)(2,1)S(1)} %whiten.1.refs_0_), channel_id=1, source_target_pairs={{0,2},{1,3},{2,0},{3,1},{4,6},{5,7},{6,4},{7,5},{8,10},{9,11},{10,... | collective-permute-start | bytes 393224 | tf_op jit(solution)/shard_map/ppermute | solution.py:479
  64.3 3.6 %collective-permute-done.10.refs_3_ = bf16[16,8,512]{2,1,0:T(8,128)(2,1)S(1)} collective-permute-done((bf16[16,8,512]{2,1,0:T(8,128)(2,1)S(1)}, bf16[16,8,512]{2,1,0:T(8,128)(2,1)S(1)}, u32[]{:S(2)}, u32[]{:S(2)}) %collective-permute-start.10) | collective-permute-done | bytes 131104 | tf_op jit(solution)/shard_map/ppermute | solution.py:479
  67.9 1.6 %collective-permute-start.12 = (bf16[4,256,256]{2,1,0:T(8,128)(2,1)S(1)}, bf16[4,256,256]{2,1,0:T(8,128)(2,1)S(1)}, u32[]{:S(2)}, u32[]{:S(2)}) collective-permute-start(bf16[4,256,256]{2,1,0:T(8,128)(2,1)S(1)} %get-tuple-element.73), channel_id=1, source_target_pairs={{0,2},{1,3},{2,0},{3,1},{4,6},{5,7},{6,4},{7,5},{8,10},{9,11},{10,... | collective-permute-start | bytes 1572872 | tf_op jit(solution)/shard_map/ppermute | solution.py:479
  69.5 1.4 %collective-permute-done.9.refs_2_ = bf16[16,8,512]{2,1,0:T(8,128)(2,1)S(1)} collective-permute-done((bf16[16,8,512]{2,1,0:T(8,128)(2,1)S(1)}, bf16[16,8,512]{2,1,0:T(8,128)(2,1)S(1)}, u32[]{:S(2)}, u32[]{:S(2)}) %collective-permute-start.9) | collective-permute-done | bytes 131104 | tf_op jit(solution)/shard_map/ppermute | solution.py:479
  71.3 2.4 %collective-permute-start.17 = (bf16[3,256,256]{2,1,0:T(8,128)(2,1)S(1)}, bf16[3,256,256]{2,1,0:T(8,128)(2,1)S(1)}, u32[]{:S(2)}, u32[]{:S(2)}) collective-permute-start(bf16[3,256,256]{2,1,0:T(8,128)(2,1)S(1)} %copy-done.7), channel_id=1, source_target_pairs={{0,12},{1,13},{2,14},{3,15},{4,8},{5,9},{6,10},{7,11},{8,4},{9,5},... | collective-permute-start | bytes 1179656 | tf_op jit(solution)/shard_map/ppermute | solution.py:479
  73.7 14.8 %collective-permute-done.16.refs_5_ = bf16[3,256,256]{2,1,0:T(8,128)(2,1)S(1)} collective-permute-done((bf16[3,256,256]{2,1,0:T(8,128)(2,1)}, bf16[3,256,256]{2,1,0:T(8,128)(2,1)S(1)}, u32[]{:S(2)}, u32[]{:S(2)}) %collective-permute-start.16) | collective-permute-done | bytes 393248 | tf_op jit(solution)/shard_map/ppermute | solution.py:479
  88.6 2.7 %left.1.left_ref = bf16[16,512,512]{2,1,0:T(8,128)(2,1)S(1)} custom-call(bf16[16,8,512]{2,1,0:T(8,128)(2,1)S(1)} %whiten.1.refs_0_, bf16[16,8,512]{2,1,0:T(8,128)(2,1)S(1)} %collective-permute-done.8.refs_1_, bf16[16,8,512]{2,1,0:T(8,128)(2,1)S(1)} %collective-permute-done.9.refs_2_, bf16[16,8,512]{2,1,0:T(8,128)(2,1)S(1)} %collective-permute-done.10.refs_3_), custom_call_target="tpu_custom_call" | custom-call | bytes 1048576 | tf_op jit(solution)/shard_map/left/pallas_call | solution.py:378
  91.2 8.3 %collective-permute-done.15.refs_4_ = bf16[3,256,256]{2,1,0:T(8,128)(2,1)S(1)} collective-permute-done((bf16[3,256,256]{2,1,0:T(8,128)(2,1)S(1)}, bf16[3,256,256]{2,1,0:T(8,128)(2,1)S(1)}, u32[]{:S(2)}, u32[]{:S(2)}) %collective-permute-start.15) | collective-permute-done | bytes 393248 | tf_op jit(solution)/shard_map/ppermute | solution.py:479
  99.5 5.4 %correlate.1 = bf16[32,256,256]{2,1,0:T(8,128)(2,1)} custom-call(bf16[16,512,512]{2,1,0:T(8,128)(2,1)S(1)} %left.1.left_ref, bf16[4,4,256,256]{3,2,1,0:T(8,128)(2,1)S(1)} %all-to-all-done.whole_ref, bf16[4,256,256]{2,1,0:T(8,128)(2,1)S(1)} %collective-permute-done.11.refs_0_, bf16[4,256,256]{2,1,0:T(8,128)(2,1)S(1)} %collective-permute-done.12.refs_1_, ...), custom_call_target="tpu_custom_call" | custom-call | tf_op jit(solution)/shard_map/correlate/pallas_call | solution.py:458
  (42 shorter events, 1.5 us)
Async XLA Ops:
  4.0 57.3 %all-to-all-start = ((bf16[4,4,256,256]{3,2,1,0:T(8,128)(2,1)}), bf16[4,4,256,256]{3,2,1,0:T(8,128)(2,1)S(1)}, u32[]{:S(2)}, u32[]{:S(2)}) async-start(bf16[4,4,256,256]{3,2,1,0:T(8,128)(2,1)} %prepare.1), calls=%async_computation | async-start | bytes 4194304 | tf_op jit(solution)/shard_map/all_to_all | solution.py:487
  13.1 14.2 %collective-permute-start = (bf16[8,384,256]{2,1,0:T(8,128)(2,1)}, bf16[8,384,256]{2,1,0:T(8,128)(2,1)}, u32[]{:S(2)}, u32[]{:S(2)}) collective-permute-start(bf16[8,384,256]{2,1,0:T(8,128)(2,1)} %lend.1), channel_id=1, source_target_pairs={{0,1},{1,0},{2,3},{3,2},{4,5},{5,4},{6,7},{7,6},{8,9},{9,8},{10,11... | collective-permute-start | bytes 4718600 | tf_op jit(solution)/shard_map/ppermute | solution.py:479
  19.3 2.0 %collective-permute-start.1 = (bf16[8,1024]{1,0:T(8,128)(2,1)}, bf16[8,1024]{1,0:T(8,128)(2,1)S(1)}, u32[]{:S(2)}, u32[]{:S(2)}) collective-permute-start(bf16[8,1024]{1,0:T(8,128)(2,1)} %get-tuple-element.53), channel_id=1, source_target_pairs={{0,1},{1,0},{2,3},{3,2},{4,5},{5,4},{6,7},{7,6},{8,9},{9,8},{10,11... | collective-permute-start | bytes 49160 | tf_op jit(solution)/shard_map/ppermute | solution.py:479
  19.8 3.9 %collective-permute-start.2 = (bf16[8,1024]{1,0:T(8,128)(2,1)}, bf16[8,1024]{1,0:T(8,128)(2,1)S(1)}, u32[]{:S(2)}, u32[]{:S(2)}) collective-permute-start(bf16[8,1024]{1,0:T(8,128)(2,1)} %get-tuple-element.54), channel_id=1, source_target_pairs={{0,2},{1,3},{2,0},{3,1},{4,6},{5,7},{6,4},{7,5},{8,10},{9,11},{10,... | collective-permute-start | bytes 49160 | tf_op jit(solution)/shard_map/ppermute | solution.py:479
  21.3 3.5 %collective-permute-start.3 = (bf16[8,1024]{1,0:T(8,128)(2,1)}, bf16[8,1024]{1,0:T(8,128)(2,1)S(1)}, u32[]{:S(2)}, u32[]{:S(2)}) collective-permute-start(bf16[8,1024]{1,0:T(8,128)(2,1)} %get-tuple-element.55), channel_id=1, source_target_pairs={{0,3},{1,2},{2,1},{3,0},{4,7},{5,6},{6,5},{7,4},{8,11},{9,10},{10,... | collective-permute-start | bytes 49160 | tf_op jit(solution)/shard_map/ppermute | solution.py:479
  21.3 3.5 %copy-start.9 = (bf16[8,1024]{1,0:T(8,128)(2,1)}, bf16[8,1024]{1,0:T(8,128)(2,1)S(1)}, u32[]{:S(2)}) copy-start(bf16[8,1024]{1,0:T(8,128)(2,1)S(1)} %collective-permute-done.1.refs_1_) | copy-start | bytes 49156
  23.7 1.1 %copy-start.10 = (bf16[8,1024]{1,0:T(8,128)(2,1)}, bf16[8,1024]{1,0:T(8,128)(2,1)S(1)}, u32[]{:S(2)}) copy-start(bf16[8,1024]{1,0:T(8,128)(2,1)S(1)} %collective-permute-done.2.refs_2_) | copy-start | bytes 49156
  24.8 0.6 copy-start.11
  31.2 6.2 %copy-start.4 = (bf16[64,256]{1,0:T(8,128)(2,1)S(1)}, bf16[64,256]{1,0:T(8,128)(2,1)}, u32[]{:S(2)}) copy-start(bf16[64,256]{1,0:T(8,128)(2,1)} %source_spectra.1.refs_0_) | copy-start | bytes 98308
  31.3 15.1 %copy-start = (bf16[256,512]{1,0:T(8,128)(2,1)S(1)}, bf16[256,512]{1,0:T(8,128)(2,1)}, u32[]{:S(2)}) copy-start(bf16[256,512]{1,0:T(8,128)(2,1)} %constant.4.clone.rows_ref.table_ref.refs_4_) | copy-start | bytes 786436
  31.3 15.1 %copy-start.2 = (bf16[2,512,256]{2,1,0:T(8,128)(2,1)S(1)}, bf16[2,512,256]{2,1,0:T(8,128)(2,1)}, u32[]{:S(2)}) copy-start(bf16[2,512,256]{2,1,0:T(8,128)(2,1)} %get-tuple-element.60.keep_ref) | copy-start | bytes 1572868
  31.3 15.1 %collective-permute-start.7 = (bf16[2,512,256]{2,1,0:T(8,128)(2,1)}, bf16[2,512,256]{2,1,0:T(8,128)(2,1)S(1)}, u32[]{:S(2)}, u32[]{:S(2)}) collective-permute-start(bf16[2,512,256]{2,1,0:T(8,128)(2,1)} %get-tuple-element.61), channel_id=1, source_target_pairs={{0,2},{1,3},{2,0},{3,1},{4,6},{5,7},{6,4},{7,5},{8,10},{9,11},{10,... | collective-permute-start | bytes 1572872 | tf_op jit(solution)/shard_map/ppermute | solution.py:479
  36.5 34.4 %copy-start.1 = (bf16[2,512,256]{2,1,0:T(8,128)(2,1)S(1)}, bf16[2,512,256]{2,1,0:T(8,128)(2,1)}, u32[]{:S(2)}) copy-start(bf16[2,512,256]{2,1,0:T(8,128)(2,1)} %get-tuple-element.75.keep_ref) | copy-start | bytes 1572868
  36.5 27.6 %collective-permute-start.14 = (bf16[2,512,256]{2,1,0:T(8,128)(2,1)}, bf16[2,512,256]{2,1,0:T(8,128)(2,1)S(1)}, u32[]{:S(2)}, u32[]{:S(2)}) collective-permute-start(bf16[2,512,256]{2,1,0:T(8,128)(2,1)} %get-tuple-element.76), channel_id=1, source_target_pairs={{0,2},{1,3},{2,0},{3,1},{4,6},{5,7},{6,4},{7,5},{8,10},{9,11},{10,... | collective-permute-start | bytes 1572872 | tf_op jit(solution)/shard_map/ppermute | solution.py:479
  37.4 12.2 %collective-permute-start.6 = (bf16[64,256]{1,0:T(8,128)(2,1)S(1)}, bf16[64,256]{1,0:T(8,128)(2,1)S(1)}, u32[]{:S(2)}, u32[]{:S(2)}) collective-permute-start(bf16[64,256]{1,0:T(8,128)(2,1)S(1)} %copy-done.4), channel_id=1, source_target_pairs={{0,12},{1,13},{2,14},{3,15},{4,8},{5,9},{6,10},{7,11},{8,4},{9,5},... | collective-permute-start | bytes 98312 | tf_op jit(solution)/shard_map/ppermute | solution.py:479
  41.3 20.1 %collective-permute-start.5 = (bf16[64,256]{1,0:T(8,128)(2,1)S(1)}, bf16[64,256]{1,0:T(8,128)(2,1)S(1)}, u32[]{:S(2)}, u32[]{:S(2)}) collective-permute-start(bf16[64,256]{1,0:T(8,128)(2,1)S(1)} %copy-done.4), channel_id=1, source_target_pairs={{0,8},{1,9},{2,10},{3,11},{4,12},{5,13},{6,14},{7,15},{8,0},{9,1},... | collective-permute-start | bytes 98312 | tf_op jit(solution)/shard_map/ppermute | solution.py:479
  41.3 20.1 %collective-permute-start.4 = (bf16[64,256]{1,0:T(8,128)(2,1)S(1)}, bf16[64,256]{1,0:T(8,128)(2,1)S(1)}, u32[]{:S(2)}, u32[]{:S(2)}) collective-permute-start(bf16[64,256]{1,0:T(8,128)(2,1)S(1)} %copy-done.4), channel_id=1, source_target_pairs={{0,4},{1,5},{2,6},{3,7},{4,0},{5,1},{6,2},{7,3},{8,12},{9,13},{10,... | collective-permute-start | bytes 98312 | tf_op jit(solution)/shard_map/ppermute | solution.py:479
  46.7 0.7 copy-start.6
  47.5 0.7 copy-start.8
  61.3 10.0 %copy-start.7 = (bf16[3,256,256]{2,1,0:T(8,128)(2,1)S(1)}, bf16[3,256,256]{2,1,0:T(8,128)(2,1)}, u32[]{:S(2)}) copy-start(bf16[3,256,256]{2,1,0:T(8,128)(2,1)} %copy-done.6) | copy-start | bytes 1179652
  61.3 27.2 %collective-permute-start.16 = (bf16[3,256,256]{2,1,0:T(8,128)(2,1)}, bf16[3,256,256]{2,1,0:T(8,128)(2,1)S(1)}, u32[]{:S(2)}, u32[]{:S(2)}) collective-permute-start(bf16[3,256,256]{2,1,0:T(8,128)(2,1)} %copy-done.8), channel_id=1, source_target_pairs={{0,8},{1,9},{2,10},{3,11},{4,12},{5,13},{6,14},{7,15},{8,0},{9,1},... | collective-permute-start | bytes 1179656 | tf_op jit(solution)/shard_map/ppermute | solution.py:479
  62.2 5.8 %collective-permute-start.10 = (bf16[16,8,512]{2,1,0:T(8,128)(2,1)S(1)}, bf16[16,8,512]{2,1,0:T(8,128)(2,1)S(1)}, u32[]{:S(2)}, u32[]{:S(2)}) collective-permute-start(bf16[16,8,512]{2,1,0:T(8,128)(2,1)S(1)} %whiten.1.refs_0_), channel_id=1, source_target_pairs={{0,3},{1,2},{2,1},{3,0},{4,7},{5,6},{6,5},{7,4},{8,11},{9,10},{10,... | collective-permute-start | bytes 393224 | tf_op jit(solution)/shard_map/ppermute | solution.py:479
  62.2 8.7 %collective-permute-start.9 = (bf16[16,8,512]{2,1,0:T(8,128)(2,1)S(1)}, bf16[16,8,512]{2,1,0:T(8,128)(2,1)S(1)}, u32[]{:S(2)}, u32[]{:S(2)}) collective-permute-start(bf16[16,8,512]{2,1,0:T(8,128)(2,1)S(1)} %whiten.1.refs_0_), channel_id=1, source_target_pairs={{0,2},{1,3},{2,0},{3,1},{4,6},{5,7},{6,4},{7,5},{8,10},{9,11},{10,... | collective-permute-start | bytes 393224 | tf_op jit(solution)/shard_map/ppermute | solution.py:479
  63.8 7.5 %collective-permute-start.8 = (bf16[16,8,512]{2,1,0:T(8,128)(2,1)S(1)}, bf16[16,8,512]{2,1,0:T(8,128)(2,1)S(1)}, u32[]{:S(2)}, u32[]{:S(2)}) collective-permute-start(bf16[16,8,512]{2,1,0:T(8,128)(2,1)S(1)} %whiten.1.refs_0_), channel_id=1, source_target_pairs={{0,1},{1,0},{2,3},{3,2},{4,5},{5,4},{6,7},{7,6},{8,9},{9,8},{10,11... | collective-permute-start | bytes 393224 | tf_op jit(solution)/shard_map/ppermute | solution.py:479
  64.1 35.4 %collective-permute-start.11 = (bf16[4,256,256]{2,1,0:T(8,128)(2,1)S(1)}, bf16[4,256,256]{2,1,0:T(8,128)(2,1)S(1)}, u32[]{:S(2)}, u32[]{:S(2)}) collective-permute-start(bf16[4,256,256]{2,1,0:T(8,128)(2,1)S(1)} %get-tuple-element.72), channel_id=1, source_target_pairs={{0,1},{1,0},{2,3},{3,2},{4,5},{5,4},{6,7},{7,6},{8,9},{9,8},{10,11... | collective-permute-start | bytes 1572872 | tf_op jit(solution)/shard_map/ppermute | solution.py:479
  67.9 31.6 %collective-permute-start.12 = (bf16[4,256,256]{2,1,0:T(8,128)(2,1)S(1)}, bf16[4,256,256]{2,1,0:T(8,128)(2,1)S(1)}, u32[]{:S(2)}, u32[]{:S(2)}) collective-permute-start(bf16[4,256,256]{2,1,0:T(8,128)(2,1)S(1)} %get-tuple-element.73), channel_id=1, source_target_pairs={{0,2},{1,3},{2,0},{3,1},{4,6},{5,7},{6,4},{7,5},{8,10},{9,11},{10,... | collective-permute-start | bytes 1572872 | tf_op jit(solution)/shard_map/ppermute | solution.py:479
  70.9 28.6 %collective-permute-start.13 = (bf16[4,256,256]{2,1,0:T(8,128)(2,1)S(1)}, bf16[4,256,256]{2,1,0:T(8,128)(2,1)S(1)}, u32[]{:S(2)}, u32[]{:S(2)}) collective-permute-start(bf16[4,256,256]{2,1,0:T(8,128)(2,1)S(1)} %get-tuple-element.74), channel_id=1, source_target_pairs={{0,3},{1,2},{2,1},{3,0},{4,7},{5,6},{6,5},{7,4},{8,11},{9,10},{10,... | collective-permute-start | bytes 1572872 | tf_op jit(solution)/shard_map/ppermute | solution.py:479
  71.3 19.9 %collective-permute-start.17 = (bf16[3,256,256]{2,1,0:T(8,128)(2,1)S(1)}, bf16[3,256,256]{2,1,0:T(8,128)(2,1)S(1)}, u32[]{:S(2)}, u32[]{:S(2)}) collective-permute-start(bf16[3,256,256]{2,1,0:T(8,128)(2,1)S(1)} %copy-done.7), channel_id=1, source_target_pairs={{0,12},{1,13},{2,14},{3,15},{4,8},{5,9},{6,10},{7,11},{8,4},{9,5},... | collective-permute-start | bytes 1179656 | tf_op jit(solution)/shard_map/ppermute | solution.py:479
  88.5 11.0 %copy-start.3 = (bf16[256,256]{1,0:T(8,128)(2,1)S(1)}, bf16[256,256]{1,0:T(8,128)(2,1)}, u32[]{:S(2)}) copy-start(bf16[256,256]{1,0:T(8,128)(2,1)} %constant.5.clone.refs_8_) | copy-start | bytes 393220
  88.5 11.0 %copy-start.5 = (s32[256]{0:T(256)S(1)}, s32[256]{0:T(256)}, u32[]{:S(2)}) copy-start(s32[256]{0:T(256)} %alive_ref.1) | copy-start | bytes 3076
  88.5 10.9 %collective-permute-start.15 = (bf16[3,256,256]{2,1,0:T(8,128)(2,1)S(1)}, bf16[3,256,256]{2,1,0:T(8,128)(2,1)S(1)}, u32[]{:S(2)}, u32[]{:S(2)}) collective-permute-start(bf16[3,256,256]{2,1,0:T(8,128)(2,1)S(1)} %get-tuple-element.78), channel_id=1, source_target_pairs={{0,4},{1,5},{2,6},{3,7},{4,0},{5,1},{6,2},{7,3},{8,12},{9,13},{10,... | collective-permute-start | bytes 1179656 | tf_op jit(solution)/shard_map/ppermute | solution.py:479

commit v7 on v5

--- a/solution.py
+++ b/solution.py
@@ -76,14 +76,17 @@
     return window(data_ref, row, column * width, STEP, width)
 
 
-def prepare_kernel(data_ref, table_ref, whole_ref, block_ref, out_ref, in_sems, out_sems):
+def prepare_kernel(data_ref, rows_ref, whole_ref, block_ref, out_ref, table_ref, in_sems, out_sems, sem):
     _, place = position()
     planes, width = out_ref.shape[0] // 2, out_ref.shape[3]
     copies = []
+    table = pltpu.make_async_copy(rows_ref, table_ref, sem)
+    table.start()
     for plane in range(planes):
         source = window(data_ref, place * STEP, plane * TEAM * width, SEGMENT_LENGTH, TEAM * width)
         copies.append(pltpu.make_async_copy(source, block_ref.at[plane], in_sems.at[plane]))
         copies[plane].start()
+    table.wait()
     for plane in range(planes):
         copies[plane].wait()
         for core in range(2):
@@ -102,12 +105,14 @@
     planes = count // TEAM
     return pl.pallas_call(
         prepare_kernel,
-        in_specs=[pl.BlockSpec(memory_space=pl.ANY), pl.BlockSpec(memory_space=pltpu.VMEM)],
+        in_specs=[pl.BlockSpec(memory_space=pl.ANY)] * 2,
         scratch_shapes=[
             pltpu.VMEM((planes, SEGMENT_LENGTH, TEAM * width), jnp.bfloat16),
             pltpu.VMEM((planes * 2, 2, BINS, width), jnp.bfloat16),
+            pltpu.VMEM((BINS, SEGMENT_LENGTH), jnp.bfloat16),
             pltpu.SemaphoreType.DMA((planes,)),
             pltpu.SemaphoreType.DMA((planes,)),
+            pltpu.SemaphoreType.DMA,
         ],
         out_specs=pl.BlockSpec(memory_space=pl.ANY),
         out_shape=jax.ShapeDtypeStruct((planes * 2, 2, BINS, width), jnp.bfloat16),
@@ -360,8 +365,7 @@
 
 def left_kernel(*refs):
     src_refs, left_ref = refs[:-1], refs[-1]
-    src = [ref[i, 0].astype(jnp.float32) for ref in src_refs for i in range(ref.shape[0])]
-    src = jnp.concatenate(src, axis=0)
+    src = jnp.concatenate([ref[0].astype(jnp.float32) for ref in src_refs], axis=0)
     lane = lax.broadcasted_iota(jnp.int32, (SOURCES, DEPTH), 1)
     turned = jnp.where(lane % (2 * SUB) < SUB, -pltpu.roll(src, DEPTH - SUB, 1), pltpu.roll(src, SUB, 1))
     row = lax.broadcasted_iota(jnp.int32, (1, 2 * SUB, DEPTH), 1)
@@ -375,7 +379,7 @@
     return pl.pallas_call(
         left_kernel,
         grid=(TILES,),
-        in_specs=[pl.BlockSpec((part.shape[0], 1, SHARE, DEPTH), lambda i: (0, i, 0, 0)) for part in src],
+        in_specs=[pl.BlockSpec((1, SHARE, DEPTH), lambda i: (i, 0, 0))] * TEAM,
         out_specs=pl.BlockSpec((1, SOURCES * 2 * SUB, DEPTH), lambda i: (i, 0, 0)),
         out_shape=jax.ShapeDtypeStruct((TILES, SOURCES * 2 * SUB, DEPTH), jnp.bfloat16),
         compiler_params=pltpu.CompilerParams(vmem_limit_bytes=16 << 20),
@@ -395,7 +399,7 @@
     src = jnp.transpose(src.reshape(SOURCES, SEGMENT_TALLY, TILES, 2 * SUB), (2, 0, 1, 3))
     src = src.reshape(TILES, SOURCES, SEGMENT_TALLY * 2 * SUB)
     src = jnp.pad(src, ((0, 0), (0, 0), (0, DEPTH - SEGMENT_TALLY * 2 * SUB)))
-    return [src[None, :, k * SHARE : (k + 1) * SHARE] for k in range(TEAM)]
+    return [src[:, k * SHARE : (k + 1) * SHARE] for k in range(TEAM)]
 
 
 BATCH = 8
@@ -495,12 +499,11 @@
         got_near = swap(give_near, 2)
         arrived, whole, far, got_near = lax.optimization_barrier((arrived, whole, far, got_near))
         other = regroup(whole)
-        src = whiten([spectra] + arrived)[None]
+        src = whiten([spectra] + arrived)
         keep_near, src, other = lax.optimization_barrier((keep_near, src, other))
-        src = jnp.concatenate([src, swap(src, 1)])
         near = straddle(keep_near, got_near, table)
         other = swap(other, 2)
-        src = [src, swap(src, 2)]
+        src = [src] + [swap(src, k) for k in team]
         split = [near[0], swap(near[1], TEAM), swap(far[0], 2 * TEAM), swap(far[1], 3 * TEAM)]
     else:
         me = lax.axis_index("chan")

time: 106 us -> 105 us (level)
  the two profiles are of different devices: /device:TPU:9 before, /device:TPU:0 now
where the time goes in v7:
time: 105 us
  waiting for transfers between devices  48.9 us (47%)
  Pallas kernels  32 us (30%)
  starting transfers between devices  21.5 us (20%)
  local copies, waits for them, and re-layouts  2.14 us (2%)
    ppermute x16, waiting for transfers between devices, body(): lax.ppermute(x, 'chan', [(i, i ^ k) for i in range(count)])  48.9 us
    ppermute x16, starting transfers between devices, body(): lax.ppermute(x, 'chan', [(i, i ^ k) for i in range(count)])  15.2 us
    pallas_call x2, Pallas kernels, halves(): pl.pallas_call(functools.partial(halves_kernel, planes), in_specs=[pl.Blo...  7.97 us
    all_to_all x1, starting transfers between devices, body(): lax.all_to_all(whole, 'chan', 0, 0, tiled=True, axis_index_groups=across)  6.33 us
    pallas_call x1, Pallas kernels, pick(): pl.pallas_call(functools.partial(pick_kernel, width), grid=(count // TEAM...  6.1 us
    pallas_call x1, Pallas kernels, correlate(): pl.pallas_call(functools.partial(correlate_kernel, relative), out_specs=p...  5.41 us
    pallas_call x1, Pallas kernels, prepare(): pl.pallas_call(prepare_kernel, in_specs=[pl.BlockSpec(memory_space=pl.ANY...  4 us
    pallas_call x1, Pallas kernels, lend(): pl.pallas_call(lend_kernel, in_specs=[pl.BlockSpec(memory_space=pl.ANY)],...  2.78 us
  transfers between devices with their start and end apart: 17, of which 8 were waited for; matrix products, arithmetic and copies ran while one was open for 0% of the time, Pallas kernels for 21%

profile of v7, /device:TPU:0, one launch (start us, length us, event | category | flops | bytes accessed | tf_op | source)
XLA Modules:
  0.0 104.8 jit_solution(2120578605919287027)
XLA Ops:
  0.0 4.0 %prepare.1 = bf16[8,2,256,256]{3,2,1,0:T(8,128)(2,1)} custom-call(bf16[896,4096]{1,0:T(8,128)(2,1)} %data_ref.5, bf16[256,512]{1,0:T(8,128)(2,1)} %constant.4.clone.rows_ref.table_ref.refs_4_), custom_call_target="tpu_custom_call" | custom-call | tf_op jit(solution)/shard_map/prepare/pallas_call | solution.py:106
  4.0 6.3 %all-to-all-start = ((bf16[8,2,256,256]{3,2,1,0:T(8,128)(2,1)}), bf16[8,2,256,256]{3,2,1,0:T(8,128)(2,1)S(1)}, u32[]{:S(2)}, u32[]{:S(2)}) async-start(bf16[8,2,256,256]{3,2,1,0:T(8,128)(2,1)} %prepare.1), calls=%async_computation | async-start | bytes 4194304 | tf_op jit(solution)/shard_map/all_to_all | solution.py:489
  10.3 2.8 %lend.1 = bf16[8,384,256]{2,1,0:T(8,128)(2,1)} custom-call(bf16[896,4096]{1,0:T(8,128)(2,1)} %data_ref.5), custom_call_target="tpu_custom_call" | custom-call | tf_op jit(solution)/shard_map/lend/pallas_call | solution.py:156
  13.1 0.6 collective-permute-start
  13.7 6.1 %pick.1 = (bf16[8,1024]{1,0:T(8,128)(2,1)}, bf16[8,1024]{1,0:T(8,128)(2,1)}, bf16[8,1024]{1,0:T(8,128)(2,1)}, bf16[8,1024]{1,0:T(8,128)(2,1)}) custom-call(s32[2,16]{1,0:T(2,128)} %sources_ref.1, s32[256]{0:T(256)} %alive_ref.1, bf16[896,4096]{1,0:T(8,128)(2,1)} %data_ref.5), custom_call_target="tpu_custom_call" | custom-call | tf_op jit(solution)/shard_map/pick/pallas_call | solution.py:278
  19.8 1.6 %collective-permute-start.2 = (bf16[8,1024]{1,0:T(8,128)(2,1)}, bf16[8,1024]{1,0:T(8,128)(2,1)S(1)}, u32[]{:S(2)}, u32[]{:S(2)}) collective-permute-start(bf16[8,1024]{1,0:T(8,128)(2,1)} %get-tuple-element.50), channel_id=1, source_target_pairs={{0,2},{1,3},{2,0},{3,1},{4,6},{5,7},{6,4},{7,5},{8,10},{9,11},{10,... | collective-permute-start | bytes 49160 | tf_op jit(solution)/shard_map/ppermute | solution.py:481
  21.7 2.1 %collective-permute-done.2.refs_2_ = bf16[8,1024]{1,0:T(8,128)(2,1)S(1)} collective-permute-done((bf16[8,1024]{1,0:T(8,128)(2,1)}, bf16[8,1024]{1,0:T(8,128)(2,1)S(1)}, u32[]{:S(2)}, u32[]{:S(2)}) %collective-permute-start.2) | collective-permute-done | bytes 16416 | tf_op jit(solution)/shard_map/ppermute | solution.py:481
  23.8 0.9 collective-permute-done.3.refs_3_
  24.8 0.6 copy-done.12
  25.4 1.8 %source_spectra.1.refs_0_ = bf16[64,256]{1,0:T(8,128)(2,1)} custom-call(bf16[8,1024]{1,0:T(8,128)(2,1)} %get-tuple-element.48.refs_0_, bf16[8,1024]{1,0:T(8,128)(2,1)} %copy-done.10, bf16[8,1024]{1,0:T(8,128)(2,1)} %copy-done.11, bf16[8,1024]{1,0:T(8,128)(2,1)} %copy-done.12, bf16[256,512]{1,0:T(8,128)(2,1)} %constant.4.clone.rows_ref.table_ref.refs_4_), custom_call_target="tpu_custom_call" | custom-call | tf_op jit(solution)/shard_map/source_spectra/pallas_call | solution.py:315
  27.2 4.0 %halves.2 = (bf16[2,512,256]{2,1,0:T(8,128)(2,1)}, bf16[2,512,256]{2,1,0:T(8,128)(2,1)}) custom-call(bf16[896,4096]{1,0:T(8,128)(2,1)} %data_ref.5, bf16[8,384,256]{2,1,0:T(8,128)(2,1)} %collective-permute-done.lent_ref, bf16[256,512]{1,0:T(8,128)(2,1)} %constant.4.clone.rows_ref.table_ref.refs_4_), custom_call_target="tpu_custom_call" | custom-call | tf_op jit(solution)/shard_map/halves/pallas_call | solution.py:197
  31.2 1.3 %collective-permute-start.7 = (bf16[2,512,256]{2,1,0:T(8,128)(2,1)}, bf16[2,512,256]{2,1,0:T(8,128)(2,1)S(1)}, u32[]{:S(2)}, u32[]{:S(2)}) collective-permute-start(bf16[2,512,256]{2,1,0:T(8,128)(2,1)} %get-tuple-element.57), channel_id=1, source_target_pairs={{0,2},{1,3},{2,0},{3,1},{4,6},{5,7},{6,4},{7,5},{8,10},{9,11},{10,... | collective-permute-start | bytes 1572872 | tf_op jit(solution)/shard_map/ppermute | solution.py:481
  32.6 4.0 %halves.3 = (bf16[2,512,256]{2,1,0:T(8,128)(2,1)}, bf16[2,512,256]{2,1,0:T(8,128)(2,1)}) custom-call(bf16[896,4096]{1,0:T(8,128)(2,1)} %data_ref.5, bf16[8,384,256]{2,1,0:T(8,128)(2,1)} %collective-permute-done.lent_ref, bf16[256,512]{1,0:T(8,128)(2,1)} %constant.4.clone.rows_ref.table_ref.refs_4_), custom_call_target="tpu_custom_call" | custom-call | tf_op jit(solution)/shard_map/halves/pallas_call | solution.py:197
  36.5 0.8 collective-permute-start.8
  37.4 3.9 %collective-permute-start.6 = (bf16[64,256]{1,0:T(8,128)(2,1)S(1)}, bf16[64,256]{1,0:T(8,128)(2,1)S(1)}, u32[]{:S(2)}, u32[]{:S(2)}) collective-permute-start(bf16[64,256]{1,0:T(8,128)(2,1)S(1)} %copy-done.4), channel_id=1, source_target_pairs={{0,12},{1,13},{2,14},{3,15},{4,8},{5,9},{6,10},{7,11},{8,4},{9,5},... | collective-permute-start | bytes 98312 | tf_op jit(solution)/shard_map/ppermute | solution.py:481
  41.3 0.6 collective-permute-start.4
  41.9 4.4 %collective-permute-done.7.got_ref = bf16[2,512,256]{2,1,0:T(8,128)(2,1)S(1)} collective-permute-done((bf16[2,512,256]{2,1,0:T(8,128)(2,1)}, bf16[2,512,256]{2,1,0:T(8,128)(2,1)S(1)}, u32[]{:S(2)}, u32[]{:S(2)}) %collective-permute-start.7) | collective-permute-done | bytes 524320 | tf_op jit(solution)/shard_map/ppermute | solution.py:481
  46.2 0.4 straddle.2
  46.6 0.7 copy-done.6
  47.4 0.8 copy-done.8
  48.1 2.2 %collective-permute-done.6.refs_3_ = bf16[64,256]{1,0:T(8,128)(2,1)S(1)} collective-permute-done((bf16[64,256]{1,0:T(8,128)(2,1)S(1)}, bf16[64,256]{1,0:T(8,128)(2,1)S(1)}, u32[]{:S(2)}, u32[]{:S(2)}) %collective-permute-start.6) | collective-permute-done | bytes 32800 | tf_op jit(solution)/shard_map/ppermute | solution.py:481
  50.3 11.9 %collective-permute-done.5.refs_2_ = bf16[64,256]{1,0:T(8,128)(2,1)S(1)} collective-permute-done((bf16[64,256]{1,0:T(8,128)(2,1)S(1)}, bf16[64,256]{1,0:T(8,128)(2,1)S(1)}, u32[]{:S(2)}, u32[]{:S(2)}) %collective-permute-start.5) | collective-permute-done | bytes 32800 | tf_op jit(solution)/shard_map/ppermute | solution.py:481
  62.3 0.4 whiten.1.refs_0_
  62.8 1.6 %collective-permute-start.12 = (bf16[8,256,256]{2,1,0:T(8,128)(2,1)S(1)}, bf16[8,256,256]{2,1,0:T(8,128)(2,1)S(1)}, u32[]{:S(2)}, u32[]{:S(2)}) collective-permute-start(bf16[8,256,256]{2,1,0:T(8,128)(2,1)S(1)} %regroup.1), channel_id=1, source_target_pairs={{0,2},{1,3},{2,0},{3,1},{4,6},{5,7},{6,4},{7,5},{8,10},{9,11},{10,... | collective-permute-start | bytes 3145736 | tf_op jit(solution)/shard_map/ppermute | solution.py:481
  64.4 2.6 %collective-permute-start.15 = (bf16[3,256,256]{2,1,0:T(8,128)(2,1)S(1)}, bf16[3,256,256]{2,1,0:T(8,128)(2,1)S(1)}, u32[]{:S(2)}, u32[]{:S(2)}) collective-permute-start(bf16[3,256,256]{2,1,0:T(8,128)(2,1)S(1)} %copy-done.7), channel_id=1, source_target_pairs={{0,12},{1,13},{2,14},{3,15},{4,8},{5,9},{6,10},{7,11},{8,4},{9,5},... | collective-permute-start | bytes 1179656 | tf_op jit(solution)/shard_map/ppermute | solution.py:481
  67.4 1.0 collective-permute-start.13
  68.3 20.7 %collective-permute-done.11.refs_3_ = bf16[16,8,512]{2,1,0:T(8,128)(2,1)S(1)} collective-permute-done((bf16[16,8,512]{2,1,0:T(8,128)(2,1)S(1)}, bf16[16,8,512]{2,1,0:T(8,128)(2,1)S(1)}, u32[]{:S(2)}, u32[]{:S(2)}) %collective-permute-start.11) | collective-permute-done | bytes 131104 | tf_op jit(solution)/shard_map/ppermute | solution.py:481
  89.1 0.8 collective-permute-start.10
  89.9 5.5 %collective-permute-done.10.refs_2_ = bf16[16,8,512]{2,1,0:T(8,128)(2,1)S(1)} collective-permute-done((bf16[16,8,512]{2,1,0:T(8,128)(2,1)S(1)}, bf16[16,8,512]{2,1,0:T(8,128)(2,1)S(1)}, u32[]{:S(2)}, u32[]{:S(2)}) %collective-permute-start.10) | collective-permute-done | bytes 131104 | tf_op jit(solution)/shard_map/ppermute | solution.py:481
  95.6 1.1 %collective-permute-done.9.refs_1_ = bf16[16,8,512]{2,1,0:T(8,128)(2,1)S(1)} collective-permute-done((bf16[16,8,512]{2,1,0:T(8,128)(2,1)S(1)}, bf16[16,8,512]{2,1,0:T(8,128)(2,1)S(1)}, u32[]{:S(2)}, u32[]{:S(2)}) %collective-permute-start.9) | collective-permute-done | bytes 131104 | tf_op jit(solution)/shard_map/ppermute | solution.py:481
  96.7 2.7 %left.1.left_ref = bf16[16,512,512]{2,1,0:T(8,128)(2,1)S(1)} custom-call(bf16[16,8,512]{2,1,0:T(8,128)(2,1)S(1)} %whiten.1.refs_0_, bf16[16,8,512]{2,1,0:T(8,128)(2,1)S(1)} %collective-permute-done.9.refs_1_, bf16[16,8,512]{2,1,0:T(8,128)(2,1)S(1)} %collective-permute-done.10.refs_2_, bf16[16,8,512]{2,1,0:T(8,128)(2,1)S(1)} %collective-permute-done.11.refs_3_), custom_call_target="tpu_custom_call" | custom-call | bytes 1048576 | tf_op jit(solution)/shard_map/left/pallas_call | solution.py:379
  99.4 5.4 %correlate.1 = bf16[32,256,256]{2,1,0:T(8,128)(2,1)} custom-call(bf16[16,512,512]{2,1,0:T(8,128)(2,1)S(1)} %left.1.left_ref, bf16[8,2,256,256]{3,2,1,0:T(8,128)(2,1)S(1)} %all-to-all-done.whole_ref, bf16[8,256,256]{2,1,0:T(8,128)(2,1)S(1)} %collective-permute-done.12.other_ref, bf16[3,256,256]{2,1,0:T(8,128)(2,1)S(1)} %get-tuple-element.69.refs_0_, ...), custom_call_target="tpu_custom_call" | custom-call | tf_op jit(solution)/shard_map/correlate/pallas_call | solution.py:460
  (40 shorter events, 1.1 us)
Async XLA Ops:
  4.0 58.2 %all-to-all-start = ((bf16[8,2,256,256]{3,2,1,0:T(8,128)(2,1)}), bf16[8,2,256,256]{3,2,1,0:T(8,128)(2,1)S(1)}, u32[]{:S(2)}, u32[]{:S(2)}) async-start(bf16[8,2,256,256]{3,2,1,0:T(8,128)(2,1)} %prepare.1), calls=%async_computation | async-start | bytes 4194304 | tf_op jit(solution)/shard_map/all_to_all | solution.py:489
  13.1 14.1 %collective-permute-start = (bf16[8,384,256]{2,1,0:T(8,128)(2,1)}, bf16[8,384,256]{2,1,0:T(8,128)(2,1)}, u32[]{:S(2)}, u32[]{:S(2)}) collective-permute-start(bf16[8,384,256]{2,1,0:T(8,128)(2,1)} %lend.1), channel_id=1, source_target_pairs={{0,1},{1,0},{2,3},{3,2},{4,5},{5,4},{6,7},{7,6},{8,9},{9,8},{10,11... | collective-permute-start | bytes 4718600 | tf_op jit(solution)/shard_map/ppermute | solution.py:481
  19.8 1.9 %collective-permute-start.1 = (bf16[8,1024]{1,0:T(8,128)(2,1)}, bf16[8,1024]{1,0:T(8,128)(2,1)S(1)}, u32[]{:S(2)}, u32[]{:S(2)}) collective-permute-start(bf16[8,1024]{1,0:T(8,128)(2,1)} %get-tuple-element.49), channel_id=1, source_target_pairs={{0,1},{1,0},{2,3},{3,2},{4,5},{5,4},{6,7},{7,6},{8,9},{9,8},{10,11... | collective-permute-start | bytes 49160 | tf_op jit(solution)/shard_map/ppermute | solution.py:481
  19.8 4.0 %collective-permute-start.2 = (bf16[8,1024]{1,0:T(8,128)(2,1)}, bf16[8,1024]{1,0:T(8,128)(2,1)S(1)}, u32[]{:S(2)}, u32[]{:S(2)}) collective-permute-start(bf16[8,1024]{1,0:T(8,128)(2,1)} %get-tuple-element.50), channel_id=1, source_target_pairs={{0,2},{1,3},{2,0},{3,1},{4,6},{5,7},{6,4},{7,5},{8,10},{9,11},{10,... | collective-permute-start | bytes 49160 | tf_op jit(solution)/shard_map/ppermute | solution.py:481
  21.4 3.4 %collective-permute-start.3 = (bf16[8,1024]{1,0:T(8,128)(2,1)}, bf16[8,1024]{1,0:T(8,128)(2,1)S(1)}, u32[]{:S(2)}, u32[]{:S(2)}) collective-permute-start(bf16[8,1024]{1,0:T(8,128)(2,1)} %get-tuple-element.51), channel_id=1, source_target_pairs={{0,3},{1,2},{2,1},{3,0},{4,7},{5,6},{6,5},{7,4},{8,11},{9,10},{10,... | collective-permute-start | bytes 49160 | tf_op jit(solution)/shard_map/ppermute | solution.py:481
  21.7 3.1 %copy-start.10 = (bf16[8,1024]{1,0:T(8,128)(2,1)}, bf16[8,1024]{1,0:T(8,128)(2,1)S(1)}, u32[]{:S(2)}) copy-start(bf16[8,1024]{1,0:T(8,128)(2,1)S(1)} %collective-permute-done.1.refs_1_) | copy-start | bytes 49156
  23.8 1.0 copy-start.11
  24.8 0.6 copy-start.12
  31.2 6.2 %copy-start.4 = (bf16[64,256]{1,0:T(8,128)(2,1)S(1)}, bf16[64,256]{1,0:T(8,128)(2,1)}, u32[]{:S(2)}) copy-start(bf16[64,256]{1,0:T(8,128)(2,1)} %source_spectra.1.refs_0_) | copy-start | bytes 98308
  31.2 15.0 %copy-start = (bf16[256,512]{1,0:T(8,128)(2,1)S(1)}, bf16[256,512]{1,0:T(8,128)(2,1)}, u32[]{:S(2)}) copy-start(bf16[256,512]{1,0:T(8,128)(2,1)} %constant.4.clone.rows_ref.table_ref.refs_4_) | copy-start | bytes 786436
  31.2 15.0 %copy-start.2 = (bf16[2,512,256]{2,1,0:T(8,128)(2,1)S(1)}, bf16[2,512,256]{2,1,0:T(8,128)(2,1)}, u32[]{:S(2)}) copy-start(bf16[2,512,256]{2,1,0:T(8,128)(2,1)} %get-tuple-element.56.keep_ref) | copy-start | bytes 1572868
  31.2 15.0 %collective-permute-start.7 = (bf16[2,512,256]{2,1,0:T(8,128)(2,1)}, bf16[2,512,256]{2,1,0:T(8,128)(2,1)S(1)}, u32[]{:S(2)}, u32[]{:S(2)}) collective-permute-start(bf16[2,512,256]{2,1,0:T(8,128)(2,1)} %get-tuple-element.57), channel_id=1, source_target_pairs={{0,2},{1,3},{2,0},{3,1},{4,6},{5,7},{6,4},{7,5},{8,10},{9,11},{10,... | collective-permute-start | bytes 1572872 | tf_op jit(solution)/shard_map/ppermute | solution.py:481
  36.5 25.7 %collective-permute-start.8 = (bf16[2,512,256]{2,1,0:T(8,128)(2,1)}, bf16[2,512,256]{2,1,0:T(8,128)(2,1)S(1)}, u32[]{:S(2)}, u32[]{:S(2)}) collective-permute-start(bf16[2,512,256]{2,1,0:T(8,128)(2,1)} %get-tuple-element.60), channel_id=1, source_target_pairs={{0,2},{1,3},{2,0},{3,1},{4,6},{5,7},{6,4},{7,5},{8,10},{9,11},{10,... | collective-permute-start | bytes 1572872 | tf_op jit(solution)/shard_map/ppermute | solution.py:481
  37.4 13.0 %collective-permute-start.6 = (bf16[64,256]{1,0:T(8,128)(2,1)S(1)}, bf16[64,256]{1,0:T(8,128)(2,1)S(1)}, u32[]{:S(2)}, u32[]{:S(2)}) collective-permute-start(bf16[64,256]{1,0:T(8,128)(2,1)S(1)} %copy-done.4), channel_id=1, source_target_pairs={{0,12},{1,13},{2,14},{3,15},{4,8},{5,9},{6,10},{7,11},{8,4},{9,5},... | collective-permute-start | bytes 98312 | tf_op jit(solution)/shard_map/ppermute | solution.py:481
  41.3 20.9 %collective-permute-start.5 = (bf16[64,256]{1,0:T(8,128)(2,1)S(1)}, bf16[64,256]{1,0:T(8,128)(2,1)S(1)}, u32[]{:S(2)}, u32[]{:S(2)}) collective-permute-start(bf16[64,256]{1,0:T(8,128)(2,1)S(1)} %copy-done.4), channel_id=1, source_target_pairs={{0,8},{1,9},{2,10},{3,11},{4,12},{5,13},{6,14},{7,15},{8,0},{9,1},... | collective-permute-start | bytes 98312 | tf_op jit(solution)/shard_map/ppermute | solution.py:481
  41.3 20.9 %collective-permute-start.4 = (bf16[64,256]{1,0:T(8,128)(2,1)S(1)}, bf16[64,256]{1,0:T(8,128)(2,1)S(1)}, u32[]{:S(2)}, u32[]{:S(2)}) collective-permute-start(bf16[64,256]{1,0:T(8,128)(2,1)S(1)} %copy-done.4), channel_id=1, source_target_pairs={{0,4},{1,5},{2,6},{3,7},{4,0},{5,1},{6,2},{7,3},{8,12},{9,13},{10,... | collective-permute-start | bytes 98312 | tf_op jit(solution)/shard_map/ppermute | solution.py:481
  46.2 20.7 %copy-start.1 = (bf16[2,512,256]{2,1,0:T(8,128)(2,1)S(1)}, bf16[2,512,256]{2,1,0:T(8,128)(2,1)}, u32[]{:S(2)}) copy-start(bf16[2,512,256]{2,1,0:T(8,128)(2,1)} %get-tuple-element.67.keep_ref) | copy-start | bytes 1572868
  46.6 0.7 copy-start.6
  47.4 0.8 copy-start.8
  62.2 2.1 %copy-start.9 = (bf16[3,256,256]{2,1,0:T(8,128)(2,1)S(1)}, bf16[3,256,256]{2,1,0:T(8,128)(2,1)}, u32[]{:S(2)}) copy-start(bf16[3,256,256]{2,1,0:T(8,128)(2,1)} %copy-done.8) | copy-start | bytes 1179652
  62.2 2.1 %copy-start.7 = (bf16[3,256,256]{2,1,0:T(8,128)(2,1)S(1)}, bf16[3,256,256]{2,1,0:T(8,128)(2,1)}, u32[]{:S(2)}) copy-start(bf16[3,256,256]{2,1,0:T(8,128)(2,1)} %copy-done.6) | copy-start | bytes 1179652
  62.8 36.6 %collective-permute-start.12 = (bf16[8,256,256]{2,1,0:T(8,128)(2,1)S(1)}, bf16[8,256,256]{2,1,0:T(8,128)(2,1)S(1)}, u32[]{:S(2)}, u32[]{:S(2)}) collective-permute-start(bf16[8,256,256]{2,1,0:T(8,128)(2,1)S(1)} %regroup.1), channel_id=1, source_target_pairs={{0,2},{1,3},{2,0},{3,1},{4,6},{5,7},{6,4},{7,5},{8,10},{9,11},{10,... | collective-permute-start | bytes 3145736 | tf_op jit(solution)/shard_map/ppermute | solution.py:481
  64.3 35.0 %collective-permute-start.14 = (bf16[3,256,256]{2,1,0:T(8,128)(2,1)S(1)}, bf16[3,256,256]{2,1,0:T(8,128)(2,1)S(1)}, u32[]{:S(2)}, u32[]{:S(2)}) collective-permute-start(bf16[3,256,256]{2,1,0:T(8,128)(2,1)S(1)} %copy-done.9), channel_id=1, source_target_pairs={{0,8},{1,9},{2,10},{3,11},{4,12},{5,13},{6,14},{7,15},{8,0},{9,1},... | collective-permute-start | bytes 1179656 | tf_op jit(solution)/shard_map/ppermute | solution.py:481
  64.3 24.7 %collective-permute-start.11 = (bf16[16,8,512]{2,1,0:T(8,128)(2,1)S(1)}, bf16[16,8,512]{2,1,0:T(8,128)(2,1)S(1)}, u32[]{:S(2)}, u32[]{:S(2)}) collective-permute-start(bf16[16,8,512]{2,1,0:T(8,128)(2,1)S(1)} %whiten.1.refs_0_), channel_id=1, source_target_pairs={{0,3},{1,2},{2,1},{3,0},{4,7},{5,6},{6,5},{7,4},{8,11},{9,10},{10,... | collective-permute-start | bytes 393224 | tf_op jit(solution)/shard_map/ppermute | solution.py:481
  64.4 35.0 %collective-permute-start.15 = (bf16[3,256,256]{2,1,0:T(8,128)(2,1)S(1)}, bf16[3,256,256]{2,1,0:T(8,128)(2,1)S(1)}, u32[]{:S(2)}, u32[]{:S(2)}) collective-permute-start(bf16[3,256,256]{2,1,0:T(8,128)(2,1)S(1)} %copy-done.7), channel_id=1, source_target_pairs={{0,12},{1,13},{2,14},{3,15},{4,8},{5,9},{6,10},{7,11},{8,4},{9,5},... | collective-permute-start | bytes 1179656 | tf_op jit(solution)/shard_map/ppermute | solution.py:481
  67.3 32.1 %copy-start.3 = (bf16[256,256]{1,0:T(8,128)(2,1)S(1)}, bf16[256,256]{1,0:T(8,128)(2,1)}, u32[]{:S(2)}) copy-start(bf16[256,256]{1,0:T(8,128)(2,1)} %constant.5.clone.refs_5_) | copy-start | bytes 393220
  67.3 32.1 %copy-start.5 = (s32[256]{0:T(256)S(1)}, s32[256]{0:T(256)}, u32[]{:S(2)}) copy-start(s32[256]{0:T(256)} %alive_ref.1) | copy-start | bytes 3076
  67.4 32.0 %collective-permute-start.13 = (bf16[3,256,256]{2,1,0:T(8,128)(2,1)S(1)}, bf16[3,256,256]{2,1,0:T(8,128)(2,1)S(1)}, u32[]{:S(2)}, u32[]{:S(2)}) collective-permute-start(bf16[3,256,256]{2,1,0:T(8,128)(2,1)S(1)} %get-tuple-element.70), channel_id=1, source_target_pairs={{0,4},{1,5},{2,6},{3,7},{4,0},{5,1},{6,2},{7,3},{8,12},{9,13},{10,... | collective-permute-start | bytes 1179656 | tf_op jit(solution)/shard_map/ppermute | solution.py:481
  89.1 6.3 %collective-permute-start.10 = (bf16[16,8,512]{2,1,0:T(8,128)(2,1)S(1)}, bf16[16,8,512]{2,1,0:T(8,128)(2,1)S(1)}, u32[]{:S(2)}, u32[]{:S(2)}) collective-permute-start(bf16[16,8,512]{2,1,0:T(8,128)(2,1)S(1)} %whiten.1.refs_0_), channel_id=1, source_target_pairs={{0,2},{1,3},{2,0},{3,1},{4,6},{5,7},{6,4},{7,5},{8,10},{9,11},{10,... | collective-permute-start | bytes 393224 | tf_op jit(solution)/shard_map/ppermute | solution.py:481
  95.3 1.3 %collective-permute-start.9 = (bf16[16,8,512]{2,1,0:T(8,128)(2,1)S(1)}, bf16[16,8,512]{2,1,0:T(8,128)(2,1)S(1)}, u32[]{:S(2)}, u32[]{:S(2)}) collective-permute-start(bf16[16,8,512]{2,1,0:T(8,128)(2,1)S(1)} %whiten.1.refs_0_), channel_id=1, source_target_pairs={{0,1},{1,0},{2,3},{3,2},{4,5},{5,4},{6,7},{7,6},{8,9},{9,8},{10,11... | collective-permute-start | bytes 393224 | tf_op jit(solution)/shard_map/ppermute | solution.py:481

commit v8 on v6

--- a/solution.py
+++ b/solution.py
@@ -497,7 +497,7 @@
         arrived, whole, far = lax.optimization_barrier((arrived, whole, far))
         others = regroup(whole)
         src = whiten([spectra] + arrived)
-        keep_near, src, others = lax.optimization_barrier((keep_near, src, others))
+        keep_near, others = lax.optimization_barrier((keep_near, others))
         others = [swap(others[k - 1], k) for k in team]
         near = straddle(keep_near, swap(give_near, 2), table)
         split = [near[0], swap(near[1], TEAM), swap(far[0], 2 * TEAM), swap(far[1], 3 * TEAM)]

time: 105 us -> 105 us (level)
  no operation moved by 1% of the time
where the time goes in v8:
time: 105 us
  waiting for transfers between devices  49.1 us (47%)
  Pallas kernels  32 us (30%)
  starting transfers between devices  21.5 us (20%)
  local copies, waits for them, and re-layouts  2.12 us (2%)
    ppermute x18, waiting for transfers between devices, body(): lax.ppermute(x, 'chan', [(i, i ^ k) for i in range(count)])  49.1 us
    ppermute x18, starting transfers between devices, body(): lax.ppermute(x, 'chan', [(i, i ^ k) for i in range(count)])  15.2 us
    pallas_call x2, Pallas kernels, halves(): pl.pallas_call(functools.partial(halves_kernel, planes), in_specs=[pl.Blo...  7.95 us
    all_to_all x1, starting transfers between devices, body(): lax.all_to_all(whole, 'chan', 0, 0, tiled=True, axis_index_groups=across)  6.32 us
    pallas_call x1, Pallas kernels, pick(): pl.pallas_call(functools.partial(pick_kernel, width), grid=(count // TEAM...  6.12 us
    pallas_call x1, Pallas kernels, correlate(): pl.pallas_call(functools.partial(correlate_kernel, relative), out_specs=p...  5.39 us
    pallas_call x1, Pallas kernels, prepare(): pl.pallas_call(prepare_kernel, in_specs=[pl.BlockSpec(memory_space=pl.ANY...  3.99 us
    pallas_call x1, Pallas kernels, lend(): pl.pallas_call(lend_kernel, in_specs=[pl.BlockSpec(memory_space=pl.ANY)],...  2.78 us
  transfers between devices with their start and end apart: 19, of which 9 were waited for; matrix products, arithmetic and copies ran while one was open for 0% of the time, Pallas kernels for 22%

profile of v8, /device:TPU:0, one launch (start us, length us, event | category | flops | bytes accessed | tf_op | source)
XLA Modules:
  0.0 104.9 jit_solution(14510758142804448562)
XLA Ops:
  0.0 4.0 %prepare.1 = bf16[4,4,256,256]{3,2,1,0:T(8,128)(2,1)} custom-call(bf16[896,4096]{1,0:T(8,128)(2,1)} %data_ref.5, bf16[256,512]{1,0:T(8,128)(2,1)} %constant.4.clone.rows_ref.table_ref.refs_4_), custom_call_target="tpu_custom_call" | custom-call | tf_op jit(solution)/shard_map/prepare/pallas_call | solution.py:104
  4.0 6.3 %all-to-all-start = ((bf16[4,4,256,256]{3,2,1,0:T(8,128)(2,1)}), bf16[4,4,256,256]{3,2,1,0:T(8,128)(2,1)S(1)}, u32[]{:S(2)}, u32[]{:S(2)}) async-start(bf16[4,4,256,256]{3,2,1,0:T(8,128)(2,1)} %prepare.1), calls=%async_computation | async-start | bytes 4194304 | tf_op jit(solution)/shard_map/all_to_all | solution.py:487
  10.3 2.8 %lend.1 = bf16[8,384,256]{2,1,0:T(8,128)(2,1)} custom-call(bf16[896,4096]{1,0:T(8,128)(2,1)} %data_ref.5), custom_call_target="tpu_custom_call" | custom-call | tf_op jit(solution)/shard_map/lend/pallas_call | solution.py:155
  13.2 6.1 %pick.1 = (bf16[8,1024]{1,0:T(8,128)(2,1)}, bf16[8,1024]{1,0:T(8,128)(2,1)}, bf16[8,1024]{1,0:T(8,128)(2,1)}, bf16[8,1024]{1,0:T(8,128)(2,1)}) custom-call(s32[2,16]{1,0:T(2,128)} %sources_ref.1, s32[256]{0:T(256)} %alive_ref.1, bf16[896,4096]{1,0:T(8,128)(2,1)} %data_ref.5), custom_call_target="tpu_custom_call" | custom-call | tf_op jit(solution)/shard_map/pick/pallas_call | solution.py:277
  19.3 0.5 collective-permute-start.1
  19.8 1.5 %collective-permute-start.2 = (bf16[8,1024]{1,0:T(8,128)(2,1)}, bf16[8,1024]{1,0:T(8,128)(2,1)S(1)}, u32[]{:S(2)}, u32[]{:S(2)}) collective-permute-start(bf16[8,1024]{1,0:T(8,128)(2,1)} %get-tuple-element.53), channel_id=1, source_target_pairs={{0,2},{1,3},{2,0},{3,1},{4,6},{5,7},{6,4},{7,5},{8,10},{9,11},{10,... | collective-permute-start | bytes 49160 | tf_op jit(solution)/shard_map/ppermute | solution.py:479
  21.3 2.4 %collective-permute-done.2.refs_2_ = bf16[8,1024]{1,0:T(8,128)(2,1)S(1)} collective-permute-done((bf16[8,1024]{1,0:T(8,128)(2,1)}, bf16[8,1024]{1,0:T(8,128)(2,1)S(1)}, u32[]{:S(2)}, u32[]{:S(2)}) %collective-permute-start.2) | collective-permute-done | bytes 16416 | tf_op jit(solution)/shard_map/ppermute | solution.py:479
  23.8 1.1 %collective-permute-done.3.refs_3_ = bf16[8,1024]{1,0:T(8,128)(2,1)S(1)} collective-permute-done((bf16[8,1024]{1,0:T(8,128)(2,1)}, bf16[8,1024]{1,0:T(8,128)(2,1)S(1)}, u32[]{:S(2)}, u32[]{:S(2)}) %collective-permute-start.3) | collective-permute-done | bytes 16416 | tf_op jit(solution)/shard_map/ppermute | solution.py:479
  24.8 0.6 copy-done.11
  25.4 1.8 %source_spectra.1.refs_0_ = bf16[64,256]{1,0:T(8,128)(2,1)} custom-call(bf16[8,1024]{1,0:T(8,128)(2,1)} %get-tuple-element.51.refs_0_, bf16[8,1024]{1,0:T(8,128)(2,1)} %copy-done.9, bf16[8,1024]{1,0:T(8,128)(2,1)} %copy-done.10, bf16[8,1024]{1,0:T(8,128)(2,1)} %copy-done.11, bf16[256,512]{1,0:T(8,128)(2,1)} %constant.4.clone.rows_ref.table_ref.refs_4_), custom_call_target="tpu_custom_call" | custom-call | tf_op jit(solution)/shard_map/source_spectra/pallas_call | solution.py:314
  27.3 4.0 %halves.2 = (bf16[2,512,256]{2,1,0:T(8,128)(2,1)}, bf16[2,512,256]{2,1,0:T(8,128)(2,1)}) custom-call(bf16[896,4096]{1,0:T(8,128)(2,1)} %data_ref.5, bf16[8,384,256]{2,1,0:T(8,128)(2,1)} %collective-permute-done.lent_ref, bf16[256,512]{1,0:T(8,128)(2,1)} %constant.4.clone.rows_ref.table_ref.refs_4_), custom_call_target="tpu_custom_call" | custom-call | tf_op jit(solution)/shard_map/halves/pallas_call | solution.py:196
  31.3 1.2 %collective-permute-start.7 = (bf16[2,512,256]{2,1,0:T(8,128)(2,1)}, bf16[2,512,256]{2,1,0:T(8,128)(2,1)S(1)}, u32[]{:S(2)}, u32[]{:S(2)}) collective-permute-start(bf16[2,512,256]{2,1,0:T(8,128)(2,1)} %get-tuple-element.58), channel_id=1, source_target_pairs={{0,2},{1,3},{2,0},{3,1},{4,6},{5,7},{6,4},{7,5},{8,10},{9,11},{10,... | collective-permute-start | bytes 1572872 | tf_op jit(solution)/shard_map/ppermute | solution.py:479
  32.5 4.0 %halves.3 = (bf16[2,512,256]{2,1,0:T(8,128)(2,1)}, bf16[2,512,256]{2,1,0:T(8,128)(2,1)}) custom-call(bf16[896,4096]{1,0:T(8,128)(2,1)} %data_ref.5, bf16[8,384,256]{2,1,0:T(8,128)(2,1)} %collective-permute-done.lent_ref, bf16[256,512]{1,0:T(8,128)(2,1)} %constant.4.clone.rows_ref.table_ref.refs_4_), custom_call_target="tpu_custom_call" | custom-call | tf_op jit(solution)/shard_map/halves/pallas_call | solution.py:196
  36.5 1.0 collective-permute-start.14
  37.4 3.8 %collective-permute-start.6 = (bf16[64,256]{1,0:T(8,128)(2,1)S(1)}, bf16[64,256]{1,0:T(8,128)(2,1)S(1)}, u32[]{:S(2)}, u32[]{:S(2)}) collective-permute-start(bf16[64,256]{1,0:T(8,128)(2,1)S(1)} %copy-done.4), channel_id=1, source_target_pairs={{0,12},{1,13},{2,14},{3,15},{4,8},{5,9},{6,10},{7,11},{8,4},{9,5},... | collective-permute-start | bytes 98312 | tf_op jit(solution)/shard_map/ppermute | solution.py:479
  41.3 0.6 collective-permute-start.4
  41.8 4.5 %collective-permute-done.7.got_ref = bf16[2,512,256]{2,1,0:T(8,128)(2,1)S(1)} collective-permute-done((bf16[2,512,256]{2,1,0:T(8,128)(2,1)}, bf16[2,512,256]{2,1,0:T(8,128)(2,1)S(1)}, u32[]{:S(2)}, u32[]{:S(2)}) %collective-permute-start.7) | collective-permute-done | bytes 524320 | tf_op jit(solution)/shard_map/ppermute | solution.py:479
  46.7 0.7 copy-done.6
  47.5 0.7 copy-done.8
  48.2 1.4 %collective-permute-done.6.refs_3_ = bf16[64,256]{1,0:T(8,128)(2,1)S(1)} collective-permute-done((bf16[64,256]{1,0:T(8,128)(2,1)S(1)}, bf16[64,256]{1,0:T(8,128)(2,1)S(1)}, u32[]{:S(2)}, u32[]{:S(2)}) %collective-permute-start.6) | collective-permute-done | bytes 32800 | tf_op jit(solution)/shard_map/ppermute | solution.py:479
  49.7 11.7 %collective-permute-done.5.refs_2_ = bf16[64,256]{1,0:T(8,128)(2,1)S(1)} collective-permute-done((bf16[64,256]{1,0:T(8,128)(2,1)S(1)}, bf16[64,256]{1,0:T(8,128)(2,1)S(1)}, u32[]{:S(2)}, u32[]{:S(2)}) %collective-permute-start.5) | collective-permute-done | bytes 32800 | tf_op jit(solution)/shard_map/ppermute | solution.py:479
  61.6 0.4 whiten.1.refs_0_
  62.1 1.6 %collective-permute-start.9 = (bf16[16,8,512]{2,1,0:T(8,128)(2,1)S(1)}, bf16[16,8,512]{2,1,0:T(8,128)(2,1)S(1)}, u32[]{:S(2)}, u32[]{:S(2)}) collective-permute-start(bf16[16,8,512]{2,1,0:T(8,128)(2,1)S(1)} %whiten.1.refs_0_), channel_id=1, source_target_pairs={{0,2},{1,3},{2,0},{3,1},{4,6},{5,7},{6,4},{7,5},{8,10},{9,11},{10,... | collective-permute-start | bytes 393224 | tf_op jit(solution)/shard_map/ppermute | solution.py:479
  64.4 3.4 %collective-permute-done.10.refs_3_ = bf16[16,8,512]{2,1,0:T(8,128)(2,1)S(1)} collective-permute-done((bf16[16,8,512]{2,1,0:T(8,128)(2,1)S(1)}, bf16[16,8,512]{2,1,0:T(8,128)(2,1)S(1)}, u32[]{:S(2)}, u32[]{:S(2)}) %collective-permute-start.10) | collective-permute-done | bytes 131104 | tf_op jit(solution)/shard_map/ppermute | solution.py:479
  67.8 1.6 %collective-permute-start.12 = (bf16[4,256,256]{2,1,0:T(8,128)(2,1)S(1)}, bf16[4,256,256]{2,1,0:T(8,128)(2,1)S(1)}, u32[]{:S(2)}, u32[]{:S(2)}) collective-permute-start(bf16[4,256,256]{2,1,0:T(8,128)(2,1)S(1)} %get-tuple-element.71), channel_id=1, source_target_pairs={{0,2},{1,3},{2,0},{3,1},{4,6},{5,7},{6,4},{7,5},{8,10},{9,11},{10,... | collective-permute-start | bytes 1572872 | tf_op jit(solution)/shard_map/ppermute | solution.py:479
  69.4 1.4 %collective-permute-done.9.refs_2_ = bf16[16,8,512]{2,1,0:T(8,128)(2,1)S(1)} collective-permute-done((bf16[16,8,512]{2,1,0:T(8,128)(2,1)S(1)}, bf16[16,8,512]{2,1,0:T(8,128)(2,1)S(1)}, u32[]{:S(2)}, u32[]{:S(2)}) %collective-permute-start.9) | collective-permute-done | bytes 131104 | tf_op jit(solution)/shard_map/ppermute | solution.py:479
  70.8 0.4 straddle.3
  71.2 2.4 %collective-permute-start.17 = (bf16[3,256,256]{2,1,0:T(8,128)(2,1)S(1)}, bf16[3,256,256]{2,1,0:T(8,128)(2,1)S(1)}, u32[]{:S(2)}, u32[]{:S(2)}) collective-permute-start(bf16[3,256,256]{2,1,0:T(8,128)(2,1)S(1)} %copy-done.7), channel_id=1, source_target_pairs={{0,12},{1,13},{2,14},{3,15},{4,8},{5,9},{6,10},{7,11},{8,4},{9,5},... | collective-permute-start | bytes 1179656 | tf_op jit(solution)/shard_map/ppermute | solution.py:479
  73.6 14.9 %collective-permute-done.16.refs_5_ = bf16[3,256,256]{2,1,0:T(8,128)(2,1)S(1)} collective-permute-done((bf16[3,256,256]{2,1,0:T(8,128)(2,1)}, bf16[3,256,256]{2,1,0:T(8,128)(2,1)S(1)}, u32[]{:S(2)}, u32[]{:S(2)}) %collective-permute-start.16) | collective-permute-done | bytes 393248 | tf_op jit(solution)/shard_map/ppermute | solution.py:479
  88.6 2.7 %left.1.left_ref = bf16[16,512,512]{2,1,0:T(8,128)(2,1)S(1)} custom-call(bf16[16,8,512]{2,1,0:T(8,128)(2,1)S(1)} %whiten.1.refs_0_, bf16[16,8,512]{2,1,0:T(8,128)(2,1)S(1)} %collective-permute-done.8.refs_1_, bf16[16,8,512]{2,1,0:T(8,128)(2,1)S(1)} %collective-permute-done.9.refs_2_, bf16[16,8,512]{2,1,0:T(8,128)(2,1)S(1)} %collective-permute-done.10.refs_3_), custom_call_target="tpu_custom_call" | custom-call | bytes 1048576 | tf_op jit(solution)/shard_map/left/pallas_call | solution.py:378
  91.2 8.3 %collective-permute-done.15.refs_4_ = bf16[3,256,256]{2,1,0:T(8,128)(2,1)S(1)} collective-permute-done((bf16[3,256,256]{2,1,0:T(8,128)(2,1)S(1)}, bf16[3,256,256]{2,1,0:T(8,128)(2,1)S(1)}, u32[]{:S(2)}, u32[]{:S(2)}) %collective-permute-start.15) | collective-permute-done | bytes 393248 | tf_op jit(solution)/shard_map/ppermute | solution.py:479
  99.5 5.4 %correlate.1 = bf16[32,256,256]{2,1,0:T(8,128)(2,1)} custom-call(bf16[16,512,512]{2,1,0:T(8,128)(2,1)S(1)} %left.1.left_ref, bf16[4,4,256,256]{3,2,1,0:T(8,128)(2,1)S(1)} %all-to-all-done.whole_ref, bf16[4,256,256]{2,1,0:T(8,128)(2,1)S(1)} %collective-permute-done.11.refs_0_, bf16[4,256,256]{2,1,0:T(8,128)(2,1)S(1)} %collective-permute-done.12.refs_1_, ...), custom_call_target="tpu_custom_call" | custom-call | tf_op jit(solution)/shard_map/correlate/pallas_call | solution.py:458
  (42 shorter events, 1.6 us)
Async XLA Ops:
  4.0 57.3 %all-to-all-start = ((bf16[4,4,256,256]{3,2,1,0:T(8,128)(2,1)}), bf16[4,4,256,256]{3,2,1,0:T(8,128)(2,1)S(1)}, u32[]{:S(2)}, u32[]{:S(2)}) async-start(bf16[4,4,256,256]{3,2,1,0:T(8,128)(2,1)} %prepare.1), calls=%async_computation | async-start | bytes 4194304 | tf_op jit(solution)/shard_map/all_to_all | solution.py:487
  13.1 14.2 %collective-permute-start = (bf16[8,384,256]{2,1,0:T(8,128)(2,1)}, bf16[8,384,256]{2,1,0:T(8,128)(2,1)}, u32[]{:S(2)}, u32[]{:S(2)}) collective-permute-start(bf16[8,384,256]{2,1,0:T(8,128)(2,1)} %lend.1), channel_id=1, source_target_pairs={{0,1},{1,0},{2,3},{3,2},{4,5},{5,4},{6,7},{7,6},{8,9},{9,8},{10,11... | collective-permute-start | bytes 4718600 | tf_op jit(solution)/shard_map/ppermute | solution.py:479
  19.3 2.0 %collective-permute-start.1 = (bf16[8,1024]{1,0:T(8,128)(2,1)}, bf16[8,1024]{1,0:T(8,128)(2,1)S(1)}, u32[]{:S(2)}, u32[]{:S(2)}) collective-permute-start(bf16[8,1024]{1,0:T(8,128)(2,1)} %get-tuple-element.52), channel_id=1, source_target_pairs={{0,1},{1,0},{2,3},{3,2},{4,5},{5,4},{6,7},{7,6},{8,9},{9,8},{10,11... | collective-permute-start | bytes 49160 | tf_op jit(solution)/shard_map/ppermute | solution.py:479
  19.8 3.9 %collective-permute-start.2 = (bf16[8,1024]{1,0:T(8,128)(2,1)}, bf16[8,1024]{1,0:T(8,128)(2,1)S(1)}, u32[]{:S(2)}, u32[]{:S(2)}) collective-permute-start(bf16[8,1024]{1,0:T(8,128)(2,1)} %get-tuple-element.53), channel_id=1, source_target_pairs={{0,2},{1,3},{2,0},{3,1},{4,6},{5,7},{6,4},{7,5},{8,10},{9,11},{10,... | collective-permute-start | bytes 49160 | tf_op jit(solution)/shard_map/ppermute | solution.py:479
  21.3 3.5 %collective-permute-start.3 = (bf16[8,1024]{1,0:T(8,128)(2,1)}, bf16[8,1024]{1,0:T(8,128)(2,1)S(1)}, u32[]{:S(2)}, u32[]{:S(2)}) collective-permute-start(bf16[8,1024]{1,0:T(8,128)(2,1)} %get-tuple-element.54), channel_id=1, source_target_pairs={{0,3},{1,2},{2,1},{3,0},{4,7},{5,6},{6,5},{7,4},{8,11},{9,10},{10,... | collective-permute-start | bytes 49160 | tf_op jit(solution)/shard_map/ppermute | solution.py:479
  21.3 3.5 %copy-start.9 = (bf16[8,1024]{1,0:T(8,128)(2,1)}, bf16[8,1024]{1,0:T(8,128)(2,1)S(1)}, u32[]{:S(2)}) copy-start(bf16[8,1024]{1,0:T(8,128)(2,1)S(1)} %collective-permute-done.1.refs_1_) | copy-start | bytes 49156
  23.7 1.1 %copy-start.10 = (bf16[8,1024]{1,0:T(8,128)(2,1)}, bf16[8,1024]{1,0:T(8,128)(2,1)S(1)}, u32[]{:S(2)}) copy-start(bf16[8,1024]{1,0:T(8,128)(2,1)S(1)} %collective-permute-done.2.refs_2_) | copy-start | bytes 49156
  24.8 0.6 copy-start.11
  31.2 6.2 %copy-start.4 = (bf16[64,256]{1,0:T(8,128)(2,1)S(1)}, bf16[64,256]{1,0:T(8,128)(2,1)}, u32[]{:S(2)}) copy-start(bf16[64,256]{1,0:T(8,128)(2,1)} %source_spectra.1.refs_0_) | copy-start | bytes 98308
  31.3 15.1 %copy-start = (bf16[256,512]{1,0:T(8,128)(2,1)S(1)}, bf16[256,512]{1,0:T(8,128)(2,1)}, u32[]{:S(2)}) copy-start(bf16[256,512]{1,0:T(8,128)(2,1)} %constant.4.clone.rows_ref.table_ref.refs_4_) | copy-start | bytes 786436
  31.3 15.1 %copy-start.2 = (bf16[2,512,256]{2,1,0:T(8,128)(2,1)S(1)}, bf16[2,512,256]{2,1,0:T(8,128)(2,1)}, u32[]{:S(2)}) copy-start(bf16[2,512,256]{2,1,0:T(8,128)(2,1)} %get-tuple-element.57.keep_ref) | copy-start | bytes 1572868
  31.3 15.1 %collective-permute-start.7 = (bf16[2,512,256]{2,1,0:T(8,128)(2,1)}, bf16[2,512,256]{2,1,0:T(8,128)(2,1)S(1)}, u32[]{:S(2)}, u32[]{:S(2)}) collective-permute-start(bf16[2,512,256]{2,1,0:T(8,128)(2,1)} %get-tuple-element.58), channel_id=1, source_target_pairs={{0,2},{1,3},{2,0},{3,1},{4,6},{5,7},{6,4},{7,5},{8,10},{9,11},{10,... | collective-permute-start | bytes 1572872 | tf_op jit(solution)/shard_map/ppermute | solution.py:479
  36.5 34.3 %copy-start.1 = (bf16[2,512,256]{2,1,0:T(8,128)(2,1)S(1)}, bf16[2,512,256]{2,1,0:T(8,128)(2,1)}, u32[]{:S(2)}) copy-start(bf16[2,512,256]{2,1,0:T(8,128)(2,1)} %get-tuple-element.73.keep_ref) | copy-start | bytes 1572868
  36.5 27.6 %collective-permute-start.14 = (bf16[2,512,256]{2,1,0:T(8,128)(2,1)}, bf16[2,512,256]{2,1,0:T(8,128)(2,1)S(1)}, u32[]{:S(2)}, u32[]{:S(2)}) collective-permute-start(bf16[2,512,256]{2,1,0:T(8,128)(2,1)} %get-tuple-element.74), channel_id=1, source_target_pairs={{0,2},{1,3},{2,0},{3,1},{4,6},{5,7},{6,4},{7,5},{8,10},{9,11},{10,... | collective-permute-start | bytes 1572872 | tf_op jit(solution)/shard_map/ppermute | solution.py:479
  37.4 12.2 %collective-permute-start.6 = (bf16[64,256]{1,0:T(8,128)(2,1)S(1)}, bf16[64,256]{1,0:T(8,128)(2,1)S(1)}, u32[]{:S(2)}, u32[]{:S(2)}) collective-permute-start(bf16[64,256]{1,0:T(8,128)(2,1)S(1)} %copy-done.4), channel_id=1, source_target_pairs={{0,12},{1,13},{2,14},{3,15},{4,8},{5,9},{6,10},{7,11},{8,4},{9,5},... | collective-permute-start | bytes 98312 | tf_op jit(solution)/shard_map/ppermute | solution.py:479
  41.3 20.1 %collective-permute-start.5 = (bf16[64,256]{1,0:T(8,128)(2,1)S(1)}, bf16[64,256]{1,0:T(8,128)(2,1)S(1)}, u32[]{:S(2)}, u32[]{:S(2)}) collective-permute-start(bf16[64,256]{1,0:T(8,128)(2,1)S(1)} %copy-done.4), channel_id=1, source_target_pairs={{0,8},{1,9},{2,10},{3,11},{4,12},{5,13},{6,14},{7,15},{8,0},{9,1},... | collective-permute-start | bytes 98312 | tf_op jit(solution)/shard_map/ppermute | solution.py:479
  41.3 20.1 %collective-permute-start.4 = (bf16[64,256]{1,0:T(8,128)(2,1)S(1)}, bf16[64,256]{1,0:T(8,128)(2,1)S(1)}, u32[]{:S(2)}, u32[]{:S(2)}) collective-permute-start(bf16[64,256]{1,0:T(8,128)(2,1)S(1)} %copy-done.4), channel_id=1, source_target_pairs={{0,4},{1,5},{2,6},{3,7},{4,0},{5,1},{6,2},{7,3},{8,12},{9,13},{10,... | collective-permute-start | bytes 98312 | tf_op jit(solution)/shard_map/ppermute | solution.py:479
  46.7 0.7 copy-start.6
  47.5 0.7 copy-start.8
  61.3 9.9 %copy-start.7 = (bf16[3,256,256]{2,1,0:T(8,128)(2,1)S(1)}, bf16[3,256,256]{2,1,0:T(8,128)(2,1)}, u32[]{:S(2)}) copy-start(bf16[3,256,256]{2,1,0:T(8,128)(2,1)} %copy-done.6) | copy-start | bytes 1179652
  61.3 27.2 %collective-permute-start.16 = (bf16[3,256,256]{2,1,0:T(8,128)(2,1)}, bf16[3,256,256]{2,1,0:T(8,128)(2,1)S(1)}, u32[]{:S(2)}, u32[]{:S(2)}) collective-permute-start(bf16[3,256,256]{2,1,0:T(8,128)(2,1)} %copy-done.8), channel_id=1, source_target_pairs={{0,8},{1,9},{2,10},{3,11},{4,12},{5,13},{6,14},{7,15},{8,0},{9,1},... | collective-permute-start | bytes 1179656 | tf_op jit(solution)/shard_map/ppermute | solution.py:479
  62.0 5.8 %collective-permute-start.10 = (bf16[16,8,512]{2,1,0:T(8,128)(2,1)S(1)}, bf16[16,8,512]{2,1,0:T(8,128)(2,1)S(1)}, u32[]{:S(2)}, u32[]{:S(2)}) collective-permute-start(bf16[16,8,512]{2,1,0:T(8,128)(2,1)S(1)} %whiten.1.refs_0_), channel_id=1, source_target_pairs={{0,3},{1,2},{2,1},{3,0},{4,7},{5,6},{6,5},{7,4},{8,11},{9,10},{10,... | collective-permute-start | bytes 393224 | tf_op jit(solution)/shard_map/ppermute | solution.py:479
  62.1 8.7 %collective-permute-start.9 = (bf16[16,8,512]{2,1,0:T(8,128)(2,1)S(1)}, bf16[16,8,512]{2,1,0:T(8,128)(2,1)S(1)}, u32[]{:S(2)}, u32[]{:S(2)}) collective-permute-start(bf16[16,8,512]{2,1,0:T(8,128)(2,1)S(1)} %whiten.1.refs_0_), channel_id=1, source_target_pairs={{0,2},{1,3},{2,0},{3,1},{4,6},{5,7},{6,4},{7,5},{8,10},{9,11},{10,... | collective-permute-start | bytes 393224 | tf_op jit(solution)/shard_map/ppermute | solution.py:479
  63.7 7.5 %collective-permute-start.8 = (bf16[16,8,512]{2,1,0:T(8,128)(2,1)S(1)}, bf16[16,8,512]{2,1,0:T(8,128)(2,1)S(1)}, u32[]{:S(2)}, u32[]{:S(2)}) collective-permute-start(bf16[16,8,512]{2,1,0:T(8,128)(2,1)S(1)} %whiten.1.refs_0_), channel_id=1, source_target_pairs={{0,1},{1,0},{2,3},{3,2},{4,5},{5,4},{6,7},{7,6},{8,9},{9,8},{10,11... | collective-permute-start | bytes 393224 | tf_op jit(solution)/shard_map/ppermute | solution.py:479
  64.1 35.4 %collective-permute-start.11 = (bf16[4,256,256]{2,1,0:T(8,128)(2,1)S(1)}, bf16[4,256,256]{2,1,0:T(8,128)(2,1)S(1)}, u32[]{:S(2)}, u32[]{:S(2)}) collective-permute-start(bf16[4,256,256]{2,1,0:T(8,128)(2,1)S(1)} %get-tuple-element.70), channel_id=1, source_target_pairs={{0,1},{1,0},{2,3},{3,2},{4,5},{5,4},{6,7},{7,6},{8,9},{9,8},{10,11... | collective-permute-start | bytes 1572872 | tf_op jit(solution)/shard_map/ppermute | solution.py:479
  67.8 31.7 %collective-permute-start.12 = (bf16[4,256,256]{2,1,0:T(8,128)(2,1)S(1)}, bf16[4,256,256]{2,1,0:T(8,128)(2,1)S(1)}, u32[]{:S(2)}, u32[]{:S(2)}) collective-permute-start(bf16[4,256,256]{2,1,0:T(8,128)(2,1)S(1)} %get-tuple-element.71), channel_id=1, source_target_pairs={{0,2},{1,3},{2,0},{3,1},{4,6},{5,7},{6,4},{7,5},{8,10},{9,11},{10,... | collective-permute-start | bytes 1572872 | tf_op jit(solution)/shard_map/ppermute | solution.py:479
  70.8 28.7 %collective-permute-start.13 = (bf16[4,256,256]{2,1,0:T(8,128)(2,1)S(1)}, bf16[4,256,256]{2,1,0:T(8,128)(2,1)S(1)}, u32[]{:S(2)}, u32[]{:S(2)}) collective-permute-start(bf16[4,256,256]{2,1,0:T(8,128)(2,1)S(1)} %get-tuple-element.72), channel_id=1, source_target_pairs={{0,3},{1,2},{2,1},{3,0},{4,7},{5,6},{6,5},{7,4},{8,11},{9,10},{10,... | collective-permute-start | bytes 1572872 | tf_op jit(solution)/shard_map/ppermute | solution.py:479
  71.2 20.0 %collective-permute-start.17 = (bf16[3,256,256]{2,1,0:T(8,128)(2,1)S(1)}, bf16[3,256,256]{2,1,0:T(8,128)(2,1)S(1)}, u32[]{:S(2)}, u32[]{:S(2)}) collective-permute-start(bf16[3,256,256]{2,1,0:T(8,128)(2,1)S(1)} %copy-done.7), channel_id=1, source_target_pairs={{0,12},{1,13},{2,14},{3,15},{4,8},{5,9},{6,10},{7,11},{8,4},{9,5},... | collective-permute-start | bytes 1179656 | tf_op jit(solution)/shard_map/ppermute | solution.py:479
  88.5 11.0 %copy-start.3 = (bf16[256,256]{1,0:T(8,128)(2,1)S(1)}, bf16[256,256]{1,0:T(8,128)(2,1)}, u32[]{:S(2)}) copy-start(bf16[256,256]{1,0:T(8,128)(2,1)} %constant.5.clone.refs_8_) | copy-start | bytes 393220
  88.5 11.0 %copy-start.5 = (s32[256]{0:T(256)S(1)}, s32[256]{0:T(256)}, u32[]{:S(2)}) copy-start(s32[256]{0:T(256)} %alive_ref.1) | copy-start | bytes 3076
  88.5 10.9 %collective-permute-start.15 = (bf16[3,256,256]{2,1,0:T(8,128)(2,1)S(1)}, bf16[3,256,256]{2,1,0:T(8,128)(2,1)S(1)}, u32[]{:S(2)}, u32[]{:S(2)}) collective-permute-start(bf16[3,256,256]{2,1,0:T(8,128)(2,1)S(1)} %get-tuple-element.76), channel_id=1, source_target_pairs={{0,4},{1,5},{2,6},{3,7},{4,0},{5,1},{6,2},{7,3},{8,12},{9,13},{10,... | collective-permute-start | bytes 1179656 | tf_op jit(solution)/shard_map/ppermute | solution.py:479

commit v9 on v6

--- a/solution.py
+++ b/solution.py
@@ -426,7 +426,8 @@
                 at = pl.multiple_of((plane ^ mine) * span + (2 * j + 1) * rows, rows)
                 right_ref[index, pl.ds(at, rows), :] = split_refs[plane][j, tile, :]
         right = right_ref[index]
-        power = jnp.square(right.astype(jnp.float32)).reshape(DEPTH // rows, rows, width)
+        held = right[: DEPTH - pad].astype(jnp.float32)
+        power = jnp.square(held).reshape(SEGMENT_TALLY, rows, width)
         power = jnp.sum(power, axis=0)
         level = (power[:SUB] + power[SUB:]) / SEGMENT_TALLY
         factor = alive / jnp.sqrt(level + 0.01)

time: 105 us -> 105 us (level)
  no operation moved by 1% of the time
where the time goes in v9:
time: 105 us
  waiting for transfers between devices  49.2 us (47%)
  Pallas kernels  32 us (30%)
  starting transfers between devices  21.4 us (20%)
  local copies, waits for them, and re-layouts  2.12 us (2%)
    ppermute x18, waiting for transfers between devices, body(): lax.ppermute(x, 'chan', [(i, i ^ k) for i in range(count)])  49.2 us
    ppermute x18, starting transfers between devices, body(): lax.ppermute(x, 'chan', [(i, i ^ k) for i in range(count)])  15.1 us
    pallas_call x2, Pallas kernels, halves(): pl.pallas_call(functools.partial(halves_kernel, planes), in_specs=[pl.Blo...  7.95 us
    all_to_all x1, starting transfers between devices, body(): lax.all_to_all(whole, 'chan', 0, 0, tiled=True, axis_index_groups=across)  6.32 us
    pallas_call x1, Pallas kernels, pick(): pl.pallas_call(functools.partial(pick_kernel, width), grid=(count // TEAM...  6.12 us
    pallas_call x1, Pallas kernels, correlate(): pl.pallas_call(functools.partial(correlate_kernel, relative), out_specs=p...  5.37 us
    pallas_call x1, Pallas kernels, prepare(): pl.pallas_call(prepare_kernel, in_specs=[pl.BlockSpec(memory_space=pl.ANY...  3.99 us
    pallas_call x1, Pallas kernels, lend(): pl.pallas_call(lend_kernel, in_specs=[pl.BlockSpec(memory_space=pl.ANY)],...  2.78 us
  transfers between devices with their start and end apart: 19, of which 9 were waited for; matrix products, arithmetic and copies ran while one was open for 0% of the time, Pallas kernels for 22%

profile of v9, /device:TPU:0, one launch (start us, length us, event | category | flops | bytes accessed | tf_op | source)
XLA Modules:
  0.0 104.9 jit_solution(3779304145131355400)
XLA Ops:
  0.0 4.0 %prepare.1 = bf16[4,4,256,256]{3,2,1,0:T(8,128)(2,1)} custom-call(bf16[896,4096]{1,0:T(8,128)(2,1)} %data_ref.5, bf16[256,512]{1,0:T(8,128)(2,1)} %constant.4.clone.rows_ref.table_ref.refs_4_), custom_call_target="tpu_custom_call" | custom-call | tf_op jit(solution)/shard_map/prepare/pallas_call | solution.py:104
  4.0 6.3 %all-to-all-start = ((bf16[4,4,256,256]{3,2,1,0:T(8,128)(2,1)}), bf16[4,4,256,256]{3,2,1,0:T(8,128)(2,1)S(1)}, u32[]{:S(2)}, u32[]{:S(2)}) async-start(bf16[4,4,256,256]{3,2,1,0:T(8,128)(2,1)} %prepare.1), calls=%async_computation | async-start | bytes 4194304 | tf_op jit(solution)/shard_map/all_to_all | solution.py:488
  10.3 2.8 %lend.1 = bf16[8,384,256]{2,1,0:T(8,128)(2,1)} custom-call(bf16[896,4096]{1,0:T(8,128)(2,1)} %data_ref.5), custom_call_target="tpu_custom_call" | custom-call | tf_op jit(solution)/shard_map/lend/pallas_call | solution.py:155
  13.2 6.1 %pick.1 = (bf16[8,1024]{1,0:T(8,128)(2,1)}, bf16[8,1024]{1,0:T(8,128)(2,1)}, bf16[8,1024]{1,0:T(8,128)(2,1)}, bf16[8,1024]{1,0:T(8,128)(2,1)}) custom-call(s32[2,16]{1,0:T(2,128)} %sources_ref.1, s32[256]{0:T(256)} %alive_ref.1, bf16[896,4096]{1,0:T(8,128)(2,1)} %data_ref.5), custom_call_target="tpu_custom_call" | custom-call | tf_op jit(solution)/shard_map/pick/pallas_call | solution.py:277
  19.3 0.5 collective-permute-start.1
  19.8 1.5 %collective-permute-start.2 = (bf16[8,1024]{1,0:T(8,128)(2,1)}, bf16[8,1024]{1,0:T(8,128)(2,1)S(1)}, u32[]{:S(2)}, u32[]{:S(2)}) collective-permute-start(bf16[8,1024]{1,0:T(8,128)(2,1)} %get-tuple-element.54), channel_id=1, source_target_pairs={{0,2},{1,3},{2,0},{3,1},{4,6},{5,7},{6,4},{7,5},{8,10},{9,11},{10,... | collective-permute-start | bytes 49160 | tf_op jit(solution)/shard_map/ppermute | solution.py:480
  21.3 2.4 %collective-permute-done.2.refs_2_ = bf16[8,1024]{1,0:T(8,128)(2,1)S(1)} collective-permute-done((bf16[8,1024]{1,0:T(8,128)(2,1)}, bf16[8,1024]{1,0:T(8,128)(2,1)S(1)}, u32[]{:S(2)}, u32[]{:S(2)}) %collective-permute-start.2) | collective-permute-done | bytes 16416 | tf_op jit(solution)/shard_map/ppermute | solution.py:480
  23.8 1.1 %collective-permute-done.3.refs_3_ = bf16[8,1024]{1,0:T(8,128)(2,1)S(1)} collective-permute-done((bf16[8,1024]{1,0:T(8,128)(2,1)}, bf16[8,1024]{1,0:T(8,128)(2,1)S(1)}, u32[]{:S(2)}, u32[]{:S(2)}) %collective-permute-start.3) | collective-permute-done | bytes 16416 | tf_op jit(solution)/shard_map/ppermute | solution.py:480
  24.8 0.6 copy-done.11
  25.4 1.8 %source_spectra.1.refs_0_ = bf16[64,256]{1,0:T(8,128)(2,1)} custom-call(bf16[8,1024]{1,0:T(8,128)(2,1)} %get-tuple-element.52.refs_0_, bf16[8,1024]{1,0:T(8,128)(2,1)} %copy-done.9, bf16[8,1024]{1,0:T(8,128)(2,1)} %copy-done.10, bf16[8,1024]{1,0:T(8,128)(2,1)} %copy-done.11, bf16[256,512]{1,0:T(8,128)(2,1)} %constant.4.clone.rows_ref.table_ref.refs_4_), custom_call_target="tpu_custom_call" | custom-call | tf_op jit(solution)/shard_map/source_spectra/pallas_call | solution.py:314
  27.3 4.0 %halves.2 = (bf16[2,512,256]{2,1,0:T(8,128)(2,1)}, bf16[2,512,256]{2,1,0:T(8,128)(2,1)}) custom-call(bf16[896,4096]{1,0:T(8,128)(2,1)} %data_ref.5, bf16[8,384,256]{2,1,0:T(8,128)(2,1)} %collective-permute-done.lent_ref, bf16[256,512]{1,0:T(8,128)(2,1)} %constant.4.clone.rows_ref.table_ref.refs_4_), custom_call_target="tpu_custom_call" | custom-call | tf_op jit(solution)/shard_map/halves/pallas_call | solution.py:196
  31.3 1.2 %collective-permute-start.7 = (bf16[2,512,256]{2,1,0:T(8,128)(2,1)}, bf16[2,512,256]{2,1,0:T(8,128)(2,1)S(1)}, u32[]{:S(2)}, u32[]{:S(2)}) collective-permute-start(bf16[2,512,256]{2,1,0:T(8,128)(2,1)} %get-tuple-element.61), channel_id=1, source_target_pairs={{0,2},{1,3},{2,0},{3,1},{4,6},{5,7},{6,4},{7,5},{8,10},{9,11},{10,... | collective-permute-start | bytes 1572872 | tf_op jit(solution)/shard_map/ppermute | solution.py:480
  32.5 4.0 %halves.3 = (bf16[2,512,256]{2,1,0:T(8,128)(2,1)}, bf16[2,512,256]{2,1,0:T(8,128)(2,1)}) custom-call(bf16[896,4096]{1,0:T(8,128)(2,1)} %data_ref.5, bf16[8,384,256]{2,1,0:T(8,128)(2,1)} %collective-permute-done.lent_ref, bf16[256,512]{1,0:T(8,128)(2,1)} %constant.4.clone.rows_ref.table_ref.refs_4_), custom_call_target="tpu_custom_call" | custom-call | tf_op jit(solution)/shard_map/halves/pallas_call | solution.py:196
  36.5 1.0 collective-permute-start.14
  37.4 3.8 %collective-permute-start.6 = (bf16[64,256]{1,0:T(8,128)(2,1)S(1)}, bf16[64,256]{1,0:T(8,128)(2,1)S(1)}, u32[]{:S(2)}, u32[]{:S(2)}) collective-permute-start(bf16[64,256]{1,0:T(8,128)(2,1)S(1)} %copy-done.4), channel_id=1, source_target_pairs={{0,12},{1,13},{2,14},{3,15},{4,8},{5,9},{6,10},{7,11},{8,4},{9,5},... | collective-permute-start | bytes 98312 | tf_op jit(solution)/shard_map/ppermute | solution.py:480
  41.3 0.6 collective-permute-start.4
  41.8 4.5 %collective-permute-done.7.got_ref = bf16[2,512,256]{2,1,0:T(8,128)(2,1)S(1)} collective-permute-done((bf16[2,512,256]{2,1,0:T(8,128)(2,1)}, bf16[2,512,256]{2,1,0:T(8,128)(2,1)S(1)}, u32[]{:S(2)}, u32[]{:S(2)}) %collective-permute-start.7) | collective-permute-done | bytes 524320 | tf_op jit(solution)/shard_map/ppermute | solution.py:480
  46.3 0.4 straddle.2
  46.7 0.7 copy-done.6
  47.5 0.7 copy-done.8
  48.2 1.4 %collective-permute-done.6.refs_3_ = bf16[64,256]{1,0:T(8,128)(2,1)S(1)} collective-permute-done((bf16[64,256]{1,0:T(8,128)(2,1)S(1)}, bf16[64,256]{1,0:T(8,128)(2,1)S(1)}, u32[]{:S(2)}, u32[]{:S(2)}) %collective-permute-start.6) | collective-permute-done | bytes 32800 | tf_op jit(solution)/shard_map/ppermute | solution.py:480
  49.7 11.7 %collective-permute-done.5.refs_2_ = bf16[64,256]{1,0:T(8,128)(2,1)S(1)} collective-permute-done((bf16[64,256]{1,0:T(8,128)(2,1)S(1)}, bf16[64,256]{1,0:T(8,128)(2,1)S(1)}, u32[]{:S(2)}, u32[]{:S(2)}) %collective-permute-start.5) | collective-permute-done | bytes 32800 | tf_op jit(solution)/shard_map/ppermute | solution.py:480
  61.7 0.4 whiten.1.refs_0_
  62.2 1.6 %collective-permute-start.9 = (bf16[16,8,512]{2,1,0:T(8,128)(2,1)S(1)}, bf16[16,8,512]{2,1,0:T(8,128)(2,1)S(1)}, u32[]{:S(2)}, u32[]{:S(2)}) collective-permute-start(bf16[16,8,512]{2,1,0:T(8,128)(2,1)S(1)} %whiten.1.refs_0_), channel_id=1, source_target_pairs={{0,2},{1,3},{2,0},{3,1},{4,6},{5,7},{6,4},{7,5},{8,10},{9,11},{10,... | collective-permute-start | bytes 393224 | tf_op jit(solution)/shard_map/ppermute | solution.py:480
  64.3 3.6 %collective-permute-done.10.refs_3_ = bf16[16,8,512]{2,1,0:T(8,128)(2,1)S(1)} collective-permute-done((bf16[16,8,512]{2,1,0:T(8,128)(2,1)S(1)}, bf16[16,8,512]{2,1,0:T(8,128)(2,1)S(1)}, u32[]{:S(2)}, u32[]{:S(2)}) %collective-permute-start.10) | collective-permute-done | bytes 131104 | tf_op jit(solution)/shard_map/ppermute | solution.py:480
  67.9 1.6 %collective-permute-start.12 = (bf16[4,256,256]{2,1,0:T(8,128)(2,1)S(1)}, bf16[4,256,256]{2,1,0:T(8,128)(2,1)S(1)}, u32[]{:S(2)}, u32[]{:S(2)}) collective-permute-start(bf16[4,256,256]{2,1,0:T(8,128)(2,1)S(1)} %get-tuple-element.73), channel_id=1, source_target_pairs={{0,2},{1,3},{2,0},{3,1},{4,6},{5,7},{6,4},{7,5},{8,10},{9,11},{10,... | collective-permute-start | bytes 1572872 | tf_op jit(solution)/shard_map/ppermute | solution.py:480
  69.5 1.4 %collective-permute-done.9.refs_2_ = bf16[16,8,512]{2,1,0:T(8,128)(2,1)S(1)} collective-permute-done((bf16[16,8,512]{2,1,0:T(8,128)(2,1)S(1)}, bf16[16,8,512]{2,1,0:T(8,128)(2,1)S(1)}, u32[]{:S(2)}, u32[]{:S(2)}) %collective-permute-start.9) | collective-permute-done | bytes 131104 | tf_op jit(solution)/shard_map/ppermute | solution.py:480
  71.3 2.4 %collective-permute-start.17 = (bf16[3,256,256]{2,1,0:T(8,128)(2,1)S(1)}, bf16[3,256,256]{2,1,0:T(8,128)(2,1)S(1)}, u32[]{:S(2)}, u32[]{:S(2)}) collective-permute-start(bf16[3,256,256]{2,1,0:T(8,128)(2,1)S(1)} %copy-done.7), channel_id=1, source_target_pairs={{0,12},{1,13},{2,14},{3,15},{4,8},{5,9},{6,10},{7,11},{8,4},{9,5},... | collective-permute-start | bytes 1179656 | tf_op jit(solution)/shard_map/ppermute | solution.py:480
  73.7 14.8 %collective-permute-done.16.refs_5_ = bf16[3,256,256]{2,1,0:T(8,128)(2,1)S(1)} collective-permute-done((bf16[3,256,256]{2,1,0:T(8,128)(2,1)}, bf16[3,256,256]{2,1,0:T(8,128)(2,1)S(1)}, u32[]{:S(2)}, u32[]{:S(2)}) %collective-permute-start.16) | collective-permute-done | bytes 393248 | tf_op jit(solution)/shard_map/ppermute | solution.py:480
  88.6 2.7 %left.1.left_ref = bf16[16,512,512]{2,1,0:T(8,128)(2,1)S(1)} custom-call(bf16[16,8,512]{2,1,0:T(8,128)(2,1)S(1)} %whiten.1.refs_0_, bf16[16,8,512]{2,1,0:T(8,128)(2,1)S(1)} %collective-permute-done.8.refs_1_, bf16[16,8,512]{2,1,0:T(8,128)(2,1)S(1)} %collective-permute-done.9.refs_2_, bf16[16,8,512]{2,1,0:T(8,128)(2,1)S(1)} %collective-permute-done.10.refs_3_), custom_call_target="tpu_custom_call" | custom-call | bytes 1048576 | tf_op jit(solution)/shard_map/left/pallas_call | solution.py:378
  91.2 8.3 %collective-permute-done.15.refs_4_ = bf16[3,256,256]{2,1,0:T(8,128)(2,1)S(1)} collective-permute-done((bf16[3,256,256]{2,1,0:T(8,128)(2,1)S(1)}, bf16[3,256,256]{2,1,0:T(8,128)(2,1)S(1)}, u32[]{:S(2)}, u32[]{:S(2)}) %collective-permute-start.15) | collective-permute-done | bytes 393248 | tf_op jit(solution)/shard_map/ppermute | solution.py:480
  99.5 5.4 %correlate.1 = bf16[32,256,256]{2,1,0:T(8,128)(2,1)} custom-call(bf16[16,512,512]{2,1,0:T(8,128)(2,1)S(1)} %left.1.left_ref, bf16[4,4,256,256]{3,2,1,0:T(8,128)(2,1)S(1)} %all-to-all-done.whole_ref, bf16[4,256,256]{2,1,0:T(8,128)(2,1)S(1)} %collective-permute-done.11.refs_0_, bf16[4,256,256]{2,1,0:T(8,128)(2,1)S(1)} %collective-permute-done.12.refs_1_, ...), custom_call_target="tpu_custom_call" | custom-call | tf_op jit(solution)/shard_map/correlate/pallas_call | solution.py:459
  (42 shorter events, 1.5 us)
Async XLA Ops:
  4.0 57.3 %all-to-all-start = ((bf16[4,4,256,256]{3,2,1,0:T(8,128)(2,1)}), bf16[4,4,256,256]{3,2,1,0:T(8,128)(2,1)S(1)}, u32[]{:S(2)}, u32[]{:S(2)}) async-start(bf16[4,4,256,256]{3,2,1,0:T(8,128)(2,1)} %prepare.1), calls=%async_computation | async-start | bytes 4194304 | tf_op jit(solution)/shard_map/all_to_all | solution.py:488
  13.1 14.2 %collective-permute-start = (bf16[8,384,256]{2,1,0:T(8,128)(2,1)}, bf16[8,384,256]{2,1,0:T(8,128)(2,1)}, u32[]{:S(2)}, u32[]{:S(2)}) collective-permute-start(bf16[8,384,256]{2,1,0:T(8,128)(2,1)} %lend.1), channel_id=1, source_target_pairs={{0,1},{1,0},{2,3},{3,2},{4,5},{5,4},{6,7},{7,6},{8,9},{9,8},{10,11... | collective-permute-start | bytes 4718600 | tf_op jit(solution)/shard_map/ppermute | solution.py:480
  19.3 2.0 %collective-permute-start.1 = (bf16[8,1024]{1,0:T(8,128)(2,1)}, bf16[8,1024]{1,0:T(8,128)(2,1)S(1)}, u32[]{:S(2)}, u32[]{:S(2)}) collective-permute-start(bf16[8,1024]{1,0:T(8,128)(2,1)} %get-tuple-element.53), channel_id=1, source_target_pairs={{0,1},{1,0},{2,3},{3,2},{4,5},{5,4},{6,7},{7,6},{8,9},{9,8},{10,11... | collective-permute-start | bytes 49160 | tf_op jit(solution)/shard_map/ppermute | solution.py:480
  19.8 3.9 %collective-permute-start.2 = (bf16[8,1024]{1,0:T(8,128)(2,1)}, bf16[8,1024]{1,0:T(8,128)(2,1)S(1)}, u32[]{:S(2)}, u32[]{:S(2)}) collective-permute-start(bf16[8,1024]{1,0:T(8,128)(2,1)} %get-tuple-element.54), channel_id=1, source_target_pairs={{0,2},{1,3},{2,0},{3,1},{4,6},{5,7},{6,4},{7,5},{8,10},{9,11},{10,... | collective-permute-start | bytes 49160 | tf_op jit(solution)/shard_map/ppermute | solution.py:480
  21.3 3.5 %collective-permute-start.3 = (bf16[8,1024]{1,0:T(8,128)(2,1)}, bf16[8,1024]{1,0:T(8,128)(2,1)S(1)}, u32[]{:S(2)}, u32[]{:S(2)}) collective-permute-start(bf16[8,1024]{1,0:T(8,128)(2,1)} %get-tuple-element.55), channel_id=1, source_target_pairs={{0,3},{1,2},{2,1},{3,0},{4,7},{5,6},{6,5},{7,4},{8,11},{9,10},{10,... | collective-permute-start | bytes 49160 | tf_op jit(solution)/shard_map/ppermute | solution.py:480
  21.3 3.5 %copy-start.9 = (bf16[8,1024]{1,0:T(8,128)(2,1)}, bf16[8,1024]{1,0:T(8,128)(2,1)S(1)}, u32[]{:S(2)}) copy-start(bf16[8,1024]{1,0:T(8,128)(2,1)S(1)} %collective-permute-done.1.refs_1_) | copy-start | bytes 49156
  23.7 1.1 %copy-start.10 = (bf16[8,1024]{1,0:T(8,128)(2,1)}, bf16[8,1024]{1,0:T(8,128)(2,1)S(1)}, u32[]{:S(2)}) copy-start(bf16[8,1024]{1,0:T(8,128)(2,1)S(1)} %collective-permute-done.2.refs_2_) | copy-start | bytes 49156
  24.8 0.6 copy-start.11
  31.2 6.2 %copy-start.4 = (bf16[64,256]{1,0:T(8,128)(2,1)S(1)}, bf16[64,256]{1,0:T(8,128)(2,1)}, u32[]{:S(2)}) copy-start(bf16[64,256]{1,0:T(8,128)(2,1)} %source_spectra.1.refs_0_) | copy-start | bytes 98308
  31.3 15.1 %copy-start = (bf16[256,512]{1,0:T(8,128)(2,1)S(1)}, bf16[256,512]{1,0:T(8,128)(2,1)}, u32[]{:S(2)}) copy-start(bf16[256,512]{1,0:T(8,128)(2,1)} %constant.4.clone.rows_ref.table_ref.refs_4_) | copy-start | bytes 786436
  31.3 15.1 %copy-start.2 = (bf16[2,512,256]{2,1,0:T(8,128)(2,1)S(1)}, bf16[2,512,256]{2,1,0:T(8,128)(2,1)}, u32[]{:S(2)}) copy-start(bf16[2,512,256]{2,1,0:T(8,128)(2,1)} %get-tuple-element.60.keep_ref) | copy-start | bytes 1572868
  31.3 15.1 %collective-permute-start.7 = (bf16[2,512,256]{2,1,0:T(8,128)(2,1)}, bf16[2,512,256]{2,1,0:T(8,128)(2,1)S(1)}, u32[]{:S(2)}, u32[]{:S(2)}) collective-permute-start(bf16[2,512,256]{2,1,0:T(8,128)(2,1)} %get-tuple-element.61), channel_id=1, source_target_pairs={{0,2},{1,3},{2,0},{3,1},{4,6},{5,7},{6,4},{7,5},{8,10},{9,11},{10,... | collective-permute-start | bytes 1572872 | tf_op jit(solution)/shard_map/ppermute | solution.py:480
  36.5 34.4 %copy-start.1 = (bf16[2,512,256]{2,1,0:T(8,128)(2,1)S(1)}, bf16[2,512,256]{2,1,0:T(8,128)(2,1)}, u32[]{:S(2)}) copy-start(bf16[2,512,256]{2,1,0:T(8,128)(2,1)} %get-tuple-element.75.keep_ref) | copy-start | bytes 1572868
  36.5 27.6 %collective-permute-start.14 = (bf16[2,512,256]{2,1,0:T(8,128)(2,1)}, bf16[2,512,256]{2,1,0:T(8,128)(2,1)S(1)}, u32[]{:S(2)}, u32[]{:S(2)}) collective-permute-start(bf16[2,512,256]{2,1,0:T(8,128)(2,1)} %get-tuple-element.76), channel_id=1, source_target_pairs={{0,2},{1,3},{2,0},{3,1},{4,6},{5,7},{6,4},{7,5},{8,10},{9,11},{10,... | collective-permute-start | bytes 1572872 | tf_op jit(solution)/shard_map/ppermute | solution.py:480
  37.4 12.2 %collective-permute-start.6 = (bf16[64,256]{1,0:T(8,128)(2,1)S(1)}, bf16[64,256]{1,0:T(8,128)(2,1)S(1)}, u32[]{:S(2)}, u32[]{:S(2)}) collective-permute-start(bf16[64,256]{1,0:T(8,128)(2,1)S(1)} %copy-done.4), channel_id=1, source_target_pairs={{0,12},{1,13},{2,14},{3,15},{4,8},{5,9},{6,10},{7,11},{8,4},{9,5},... | collective-permute-start | bytes 98312 | tf_op jit(solution)/shard_map/ppermute | solution.py:480
  41.3 20.1 %collective-permute-start.5 = (bf16[64,256]{1,0:T(8,128)(2,1)S(1)}, bf16[64,256]{1,0:T(8,128)(2,1)S(1)}, u32[]{:S(2)}, u32[]{:S(2)}) collective-permute-start(bf16[64,256]{1,0:T(8,128)(2,1)S(1)} %copy-done.4), channel_id=1, source_target_pairs={{0,8},{1,9},{2,10},{3,11},{4,12},{5,13},{6,14},{7,15},{8,0},{9,1},... | collective-permute-start | bytes 98312 | tf_op jit(solution)/shard_map/ppermute | solution.py:480
  41.3 20.1 %collective-permute-start.4 = (bf16[64,256]{1,0:T(8,128)(2,1)S(1)}, bf16[64,256]{1,0:T(8,128)(2,1)S(1)}, u32[]{:S(2)}, u32[]{:S(2)}) collective-permute-start(bf16[64,256]{1,0:T(8,128)(2,1)S(1)} %copy-done.4), channel_id=1, source_target_pairs={{0,4},{1,5},{2,6},{3,7},{4,0},{5,1},{6,2},{7,3},{8,12},{9,13},{10,... | collective-permute-start | bytes 98312 | tf_op jit(solution)/shard_map/ppermute | solution.py:480
  46.7 0.7 copy-start.6
  47.5 0.7 copy-start.8
  61.3 10.0 %copy-start.7 = (bf16[3,256,256]{2,1,0:T(8,128)(2,1)S(1)}, bf16[3,256,256]{2,1,0:T(8,128)(2,1)}, u32[]{:S(2)}) copy-start(bf16[3,256,256]{2,1,0:T(8,128)(2,1)} %copy-done.6) | copy-start | bytes 1179652
  61.3 27.2 %collective-permute-start.16 = (bf16[3,256,256]{2,1,0:T(8,128)(2,1)}, bf16[3,256,256]{2,1,0:T(8,128)(2,1)S(1)}, u32[]{:S(2)}, u32[]{:S(2)}) collective-permute-start(bf16[3,256,256]{2,1,0:T(8,128)(2,1)} %copy-done.8), channel_id=1, source_target_pairs={{0,8},{1,9},{2,10},{3,11},{4,12},{5,13},{6,14},{7,15},{8,0},{9,1},... | collective-permute-start | bytes 1179656 | tf_op jit(solution)/shard_map/ppermute | solution.py:480
  62.2 5.8 %collective-permute-start.10 = (bf16[16,8,512]{2,1,0:T(8,128)(2,1)S(1)}, bf16[16,8,512]{2,1,0:T(8,128)(2,1)S(1)}, u32[]{:S(2)}, u32[]{:S(2)}) collective-permute-start(bf16[16,8,512]{2,1,0:T(8,128)(2,1)S(1)} %whiten.1.refs_0_), channel_id=1, source_target_pairs={{0,3},{1,2},{2,1},{3,0},{4,7},{5,6},{6,5},{7,4},{8,11},{9,10},{10,... | collective-permute-start | bytes 393224 | tf_op jit(solution)/shard_map/ppermute | solution.py:480
  62.2 8.7 %collective-permute-start.9 = (bf16[16,8,512]{2,1,0:T(8,128)(2,1)S(1)}, bf16[16,8,512]{2,1,0:T(8,128)(2,1)S(1)}, u32[]{:S(2)}, u32[]{:S(2)}) collective-permute-start(bf16[16,8,512]{2,1,0:T(8,128)(2,1)S(1)} %whiten.1.refs_0_), channel_id=1, source_target_pairs={{0,2},{1,3},{2,0},{3,1},{4,6},{5,7},{6,4},{7,5},{8,10},{9,11},{10,... | collective-permute-start | bytes 393224 | tf_op jit(solution)/shard_map/ppermute | solution.py:480
  63.8 7.5 %collective-permute-start.8 = (bf16[16,8,512]{2,1,0:T(8,128)(2,1)S(1)}, bf16[16,8,512]{2,1,0:T(8,128)(2,1)S(1)}, u32[]{:S(2)}, u32[]{:S(2)}) collective-permute-start(bf16[16,8,512]{2,1,0:T(8,128)(2,1)S(1)} %whiten.1.refs_0_), channel_id=1, source_target_pairs={{0,1},{1,0},{2,3},{3,2},{4,5},{5,4},{6,7},{7,6},{8,9},{9,8},{10,11... | collective-permute-start | bytes 393224 | tf_op jit(solution)/shard_map/ppermute | solution.py:480
  64.1 35.4 %collective-permute-start.11 = (bf16[4,256,256]{2,1,0:T(8,128)(2,1)S(1)}, bf16[4,256,256]{2,1,0:T(8,128)(2,1)S(1)}, u32[]{:S(2)}, u32[]{:S(2)}) collective-permute-start(bf16[4,256,256]{2,1,0:T(8,128)(2,1)S(1)} %get-tuple-element.72), channel_id=1, source_target_pairs={{0,1},{1,0},{2,3},{3,2},{4,5},{5,4},{6,7},{7,6},{8,9},{9,8},{10,11... | collective-permute-start | bytes 1572872 | tf_op jit(solution)/shard_map/ppermute | solution.py:480
  67.9 31.6 %collective-permute-start.12 = (bf16[4,256,256]{2,1,0:T(8,128)(2,1)S(1)}, bf16[4,256,256]{2,1,0:T(8,128)(2,1)S(1)}, u32[]{:S(2)}, u32[]{:S(2)}) collective-permute-start(bf16[4,256,256]{2,1,0:T(8,128)(2,1)S(1)} %get-tuple-element.73), channel_id=1, source_target_pairs={{0,2},{1,3},{2,0},{3,1},{4,6},{5,7},{6,4},{7,5},{8,10},{9,11},{10,... | collective-permute-start | bytes 1572872 | tf_op jit(solution)/shard_map/ppermute | solution.py:480
  70.9 28.6 %collective-permute-start.13 = (bf16[4,256,256]{2,1,0:T(8,128)(2,1)S(1)}, bf16[4,256,256]{2,1,0:T(8,128)(2,1)S(1)}, u32[]{:S(2)}, u32[]{:S(2)}) collective-permute-start(bf16[4,256,256]{2,1,0:T(8,128)(2,1)S(1)} %get-tuple-element.74), channel_id=1, source_target_pairs={{0,3},{1,2},{2,1},{3,0},{4,7},{5,6},{6,5},{7,4},{8,11},{9,10},{10,... | collective-permute-start | bytes 1572872 | tf_op jit(solution)/shard_map/ppermute | solution.py:480
  71.3 19.9 %collective-permute-start.17 = (bf16[3,256,256]{2,1,0:T(8,128)(2,1)S(1)}, bf16[3,256,256]{2,1,0:T(8,128)(2,1)S(1)}, u32[]{:S(2)}, u32[]{:S(2)}) collective-permute-start(bf16[3,256,256]{2,1,0:T(8,128)(2,1)S(1)} %copy-done.7), channel_id=1, source_target_pairs={{0,12},{1,13},{2,14},{3,15},{4,8},{5,9},{6,10},{7,11},{8,4},{9,5},... | collective-permute-start | bytes 1179656 | tf_op jit(solution)/shard_map/ppermute | solution.py:480
  88.5 11.0 %copy-start.3 = (bf16[256,256]{1,0:T(8,128)(2,1)S(1)}, bf16[256,256]{1,0:T(8,128)(2,1)}, u32[]{:S(2)}) copy-start(bf16[256,256]{1,0:T(8,128)(2,1)} %constant.5.clone.refs_8_) | copy-start | bytes 393220
  88.5 11.0 %copy-start.5 = (s32[256]{0:T(256)S(1)}, s32[256]{0:T(256)}, u32[]{:S(2)}) copy-start(s32[256]{0:T(256)} %alive_ref.1) | copy-start | bytes 3076
  88.5 10.9 %collective-permute-start.15 = (bf16[3,256,256]{2,1,0:T(8,128)(2,1)S(1)}, bf16[3,256,256]{2,1,0:T(8,128)(2,1)S(1)}, u32[]{:S(2)}, u32[]{:S(2)}) collective-permute-start(bf16[3,256,256]{2,1,0:T(8,128)(2,1)S(1)} %get-tuple-element.78), channel_id=1, source_target_pairs={{0,4},{1,5},{2,6},{3,7},{4,0},{5,1},{6,2},{7,3},{8,12},{9,13},{10,... | collective-permute-start | bytes 1179656 | tf_op jit(solution)/shard_map/ppermute | solution.py:480
